TPU v7x, 128 devices: a whole 4x4x4 slice. The times are simulated.
128 devices in a mesh: ctx: 16 (over y_hi, z, core), head: 8 (over y_lo, x).
Axes of the slice: x: 4, y: 4 (y_hi: 2, y_lo: 2; y = y_hi * 2 + y_lo), z: 4, core: 2. Of those that a mesh axis runs over, the one named last changes fastest.
Arguments:
- queries: bfloat16 [16384, 4096], P('ctx', 'head'), may hold values from -24 to 24
- key_states: bfloat16 [16384, 4096], P('ctx', 'head'), may hold values from -24 to 24
- value_states: bfloat16 [16384, 4096], P('ctx', 'head'), may hold values from -6 to 6
- out_grad: bfloat16 [16384, 4096], P('ctx', 'head'), may hold values from -6 to 6
- selected: int32 [256, 16], P('ctx'), may hold values from -1 to 255, as said below
Outputs:
- query_grad: bfloat16 [16384, 4096], P(('ctx', 'head'))
- key_grad: bfloat16 [16384, 4096], P(('ctx', 'head'))
- value_grad: bfloat16 [16384, 4096], P(('ctx', 'head'))
Inputs may be any that keep to these rules, and one draw needn't show every extreme that they name: `selected`: row i holds 16 distinct entries, each a block index or -1; block i itself is always among them and every other block named comes before i. In the aligned groups of 16 rows, the blocks named that lie in another group's range number at most 1 for each other group, exactly 1 for every earlier group, and none for a later group.
All inputs are finite; a program needn't handle non-finite values.
Results may differ from a plain program's by a relative error of at most 0.011.
Values may be sent and summed in bfloat16 or wider, within the bound.
No kernel may reach another device: no remote copies, remote signals or barrier semaphores. Data moves between devices by JAX's collectives and lax.ppermute only.
A program may use at most 192 MiB of HBM per device.

v0:
```python
import jax
import jax.numpy as jnp
from jax import lax
from jax.sharding import PartitionSpec as P

HDIM = 128
HEAD_DEV = 4
BLOCK = 64
TOPK = 16
CAP = 1
GROUP = 8


def pack_slots(member, ranking, per_dev):
    slots = jnp.arange(CAP, dtype=jnp.int32)
    locals_idx = jnp.arange(per_dev, dtype=jnp.int32)
    picks = member[:, None, :] & (ranking[:, None, :] == slots[None, :, None])
    return jnp.sum(jnp.where(picks, locals_idx[None, None, :], 0), axis=2)


def group_grads(query_blk, key_blk, value_blk, grad_blk, select_blk, own_ids):
    count = query_blk.shape[0]
    scale = 1.0 / HDIM**0.5
    width = HEAD_DEV * HDIM
    query_h = query_blk.reshape(count, BLOCK, HEAD_DEV, HDIM)
    key_h = key_blk.reshape(count, TOPK * BLOCK, HEAD_DEV, HDIM)
    value_h = value_blk.reshape(count, TOPK * BLOCK, HEAD_DEV, HDIM)
    grad_h = grad_blk.reshape(count, BLOCK, HEAD_DEV, HDIM)
    key_idx = jnp.arange(TOPK * BLOCK, dtype=jnp.int32)
    slot_of = key_idx // BLOCK
    key_pos = key_idx % BLOCK
    query_pos = jnp.arange(BLOCK, dtype=jnp.int32)
    block_of = select_blk[:, slot_of]
    allowed = (block_of >= 0)[:, None, :] & (
        (block_of != own_ids[:, None])[:, None, :]
        | (key_pos[None, None, :] <= query_pos[None, :, None])
    )
    scores = (
        jnp.einsum("gqhd,gkhd->ghqk", query_h, key_h, preferred_element_type=jnp.float32) * scale
    )
    scores = jnp.where(allowed[:, None], scores, -1e30)
    highest = jnp.max(scores, axis=-1, keepdims=True)
    expo = jnp.exp(scores - highest)
    probs = expo / jnp.sum(expo, axis=-1, keepdims=True)
    probs_low = probs.astype(jnp.bfloat16)
    output = jnp.einsum("ghqk,gkhd->gqhd", probs_low, value_h, preferred_element_type=jnp.float32)
    delta = jnp.einsum("gqhd,gqhd->ghq", grad_h.astype(jnp.float32), output)
    dprobs = jnp.einsum("gqhd,gkhd->ghqk", grad_h, value_h, preferred_element_type=jnp.float32)
    dscores = probs * (dprobs - delta[..., None])
    dscores_low = dscores.astype(jnp.bfloat16)
    dquery = (
        jnp.einsum("ghqk,gkhd->gqhd", dscores_low, key_h, preferred_element_type=jnp.float32)
        * scale
    ).astype(jnp.bfloat16)
    dkey = (
        jnp.einsum("ghqk,gqhd->gkhd", dscores_low, query_h, preferred_element_type=jnp.float32)
        * scale
    )
    dvalue = jnp.einsum("ghqk,gqhd->gkhd", probs_low, grad_h, preferred_element_type=jnp.float32)
    return (
        dquery.reshape(count, BLOCK, width),
        dkey.reshape(count * TOPK, BLOCK, width),
        dvalue.reshape(count * TOPK, BLOCK, width),
    )


def per_device(queries, key_states, value_states, out_grad, selected):
    ranges = lax.axis_size("ctx")
    here = lax.axis_index("ctx")
    per_dev = selected.shape[0]
    width = queries.shape[1]
    range_ids = jnp.arange(ranges, dtype=jnp.int32)
    locals_idx = jnp.arange(per_dev, dtype=jnp.int32)
    usable = selected >= 0
    owner = jnp.where(usable, selected // per_dev, here)
    local_blk = jnp.where(usable, selected % per_dev, 0)
    hits = (owner[:, :, None, None] == range_ids[None, None, :, None]) & (
        local_blk[:, :, None, None] == locals_idx[None, None, None, :]
    )
    remote = usable & (owner != here)
    member = jnp.any(hits & remote[:, :, None, None], axis=(0, 1))
    ranking = jnp.cumsum(member.astype(jnp.int32), axis=1) - 1
    wanted_ids = pack_slots(member, ranking, per_dev)
    asks = lax.all_to_all(wanted_ids, "ctx", split_axis=0, concat_axis=0, tiled=True)
    key_blocks = key_states.reshape(per_dev, BLOCK, width)
    value_blocks = value_states.reshape(per_dev, BLOCK, width)
    sent_keys = key_blocks[asks]
    sent_values = value_blocks[asks]
    got_keys, got_values = (
        lax.all_to_all(sent_keys, "ctx", split_axis=0, concat_axis=0, tiled=True),
        lax.all_to_all(sent_values, "ctx", split_axis=0, concat_axis=0, tiled=True),
    )
    bank_keys = jnp.concatenate([key_blocks, got_keys.reshape(ranges * CAP, BLOCK, width)], axis=0)
    bank_values = jnp.concatenate(
        [value_blocks, got_values.reshape(ranges * CAP, BLOCK, width)], axis=0
    )
    rank_sel = jnp.sum(jnp.where(hits, ranking[None, None], 0), axis=(2, 3))
    bank_index = jnp.where(owner == here, local_blk, per_dev + owner * CAP + rank_sel)
    steps = per_dev // GROUP
    own_all = (here * per_dev + locals_idx).reshape(steps, GROUP)
    inputs = (
        queries.reshape(steps, GROUP, BLOCK, width),
        out_grad.reshape(steps, GROUP, BLOCK, width),
        bank_index.reshape(steps, GROUP, TOPK),
        selected.reshape(steps, GROUP, TOPK),
        own_all,
    )

    def advance(carry, item):
        grad_keys, grad_values = carry
        query_c, grad_c, index_c, select_c, own_c = item
        key_c = bank_keys[index_c].reshape(GROUP, TOPK * BLOCK, width)
        value_c = bank_values[index_c].reshape(GROUP, TOPK * BLOCK, width)
        dquery, dkey, dvalue = group_grads(query_c, key_c, value_c, grad_c, select_c, own_c)
        flat = index_c.reshape(-1)
        return ((grad_keys.at[flat].add(dkey), grad_values.at[flat].add(dvalue)), dquery)

    zeros = jnp.zeros((per_dev + ranges * CAP, BLOCK, width), jnp.float32)
    (grad_keys, grad_values), dquery = lax.scan(advance, (zeros, zeros), inputs)
    query_local = dquery.reshape(per_dev * BLOCK, width)
    back_keys, back_values = (
        lax.all_to_all(
            grad_keys[per_dev:].reshape(ranges, CAP, BLOCK, width),
            "ctx",
            split_axis=0,
            concat_axis=0,
            tiled=True,
        ),
        lax.all_to_all(
            grad_values[per_dev:].reshape(ranges, CAP, BLOCK, width),
            "ctx",
            split_axis=0,
            concat_axis=0,
            tiled=True,
        ),
    )
    flat_asks = asks.reshape(-1)
    key_total = grad_keys[:per_dev].at[flat_asks].add(back_keys.reshape(ranges * CAP, BLOCK, width))
    value_total = (
        grad_values[:per_dev].at[flat_asks].add(back_values.reshape(ranges * CAP, BLOCK, width))
    )
    key_local = key_total.reshape(per_dev * BLOCK, width).astype(jnp.bfloat16)
    value_local = value_total.reshape(per_dev * BLOCK, width).astype(jnp.bfloat16)
    query_out, key_out, value_out = (
        lax.all_to_all(query_local, "head", split_axis=0, concat_axis=1, tiled=True),
        lax.all_to_all(key_local, "head", split_axis=0, concat_axis=1, tiled=True),
        lax.all_to_all(value_local, "head", split_axis=0, concat_axis=1, tiled=True),
    )
    return (query_out, key_out, value_out)


def solution(mesh):
    return jax.shard_map(
        per_device,
        mesh=mesh,
        in_specs=(
            P("ctx", "head"),
            P("ctx", "head"),
            P("ctx", "head"),
            P("ctx", "head"),
            P("ctx", None),
        ),
        out_specs=(P(("ctx", "head"), None), P(("ctx", "head"), None), P(("ctx", "head"), None)),
        check_vma=False,
    )
```

profile of v0, /device:TPU:1, one launch (start us, length us, event | category | flops | bytes accessed | tf_op | source)
XLA Modules:
  0.0 780.0 jit_solution(9552881560634844395)
XLA Ops:
  3.8 16.2 %all_to_all.83 = s32[16,1,1]{2,1,0:T(1,128)S(1)} all-to-all(s32[16,1,1]{2,1,0:T(1,128)S(1)} %copy.83), channel_id=1, replica_groups=mesh['ctx'=16,'head'=8] {'ctx'}, dimensions={0} | all-to-all | bytes 128 | tf_op jit(solution)/shard_map/all_to_all | solution.py:84
  30.9 14.5 %all-to-all-done.1 = bf16[16,1,64,512]{3,2,1,0:T(8,128)(2,1)S(1)} async-done(((bf16[16,1,64,512]{3,2,1,0:T(8,128)(2,1)}), bf16[16,1,64,512]{3,2,1,0:T(8,128)(2,1)S(1)}, u32[]{:S(2)}, u32[]{:S(2)}) %all-to-all-start.1) | async-done | bytes 1048608 | tf_op jit(solution)/shard_map/all_to_all | solution.py:90
  75.8 567.7 %while.16 = (s32[]{:T(128)}, f32[32,64,512]{2,1,0:T(8,128)}, f32[32,64,512]{2,1,0:T(8,128)}, bf16[2,8,64,512]{3,2,1,0:T(8,128)(2,1)}, s32[2,8,16]{2,1,0:T(8,128)...) while((s32[]{:T(128)}, f32[32,64,512]{2,1,0:T(8,128)}, ...), condition=%wide.region_9.10_spmd, body=%wide.region_4.9_spmd.sunk | while | flops 3265628928 | bytes 477484352 | solution.py:119
  108.5 12.5 %reshape.486 = bf16[8,1024,4,128]{3,2,1,0:T(4,128)(2,1)} reshape(bf16[128,64,512]{2,1,0:T(8,128)(2,1)} %gather_fusion.1) | data formatting | bytes 16777216 | tf_op jit(solution)/shard_map/while/body/eval_jaxpr/reshape;while/body/eval_jaxpr/reshape | solution.py:26
  129.0 12.5 %reshape.484 = bf16[8,1024,4,128]{3,2,1,0:T(4,128)(2,1)} reshape(bf16[128,64,512]{2,1,0:T(8,128)(2,1)} %gather_fusion) | data formatting | bytes 16777216 | tf_op jit(solution)/shard_map/while/body/eval_jaxpr/reshape;while/body/eval_jaxpr/reshape | solution.py:27
  151.3 12.6 %fusion.92 = (f32[8,4,64]{2,1,0:T(4,128)S(1)}, f32[8,4,64,1024]{3,2,1,0:T(8,128)}) fusion(f32[8,4,64,1024]{3,2,1,0:T(8,128)} %fusion.90, pred[8,64,1024]{2,1,0:T(8,128)(4,1)S(1)} %copy-done.1), kind=kOutput, calls=%fused_computation.100.clone.1 | output fusion | flops 12583935 | bytes 17309696 | tf_op jit(solution)/shard_map/while/body/eval_jaxpr/sub | solution.py:43
  204.3 19.2 %copy.155 = f32[8,1024,4,128]{3,2,1,0:T(4,128)} copy(f32[8,1024,4,128]{1,3,2,0:T(8,128)} %convolution_bitcast_fusion.2) | data formatting | bytes 33554432 | tf_op jit(solution)/shard_map/while/body/eval_jaxpr/ghqk,gqhd->gkhd/transpose | solution.py:59
  223.5 19.9 %reshape.489 = f32[128,64,512]{2,1,0:T(8,128)} reshape(f32[8,1024,4,128]{3,2,1,0:T(4,128)} %copy.155) | data formatting | bytes 33554432 | tf_op jit(solution)/shard_map/while/body/eval_jaxpr/reshape | solution.py:63
  243.4 37.4 %scatter_fusion.1 = f32[32,64,512]{2,1,0:T(8,128)} fusion(f32[32,64,512]{2,1,0:T(8,128)} %get-tuple-element.293, s32[128]{0:T(128)S(1)} %fusion.89, f32[128,64,512]{2,1,0:T(8,128)} %reshape.489), kind=kCustom, calls=%fused_computation.6.clone.1 | custom fusion | flops 4194304 | bytes 50332160 | tf_op jit(solution)/shard_map/while/body/eval_jaxpr/scatter-add | solution.py:116
  291.1 19.2 %copy.154 = f32[8,1024,4,128]{3,2,1,0:T(4,128)} copy(f32[8,1024,4,128]{1,3,2,0:T(8,128)} %multiply_bitcast_fusion.2) | data formatting | bytes 33554432 | tf_op jit(solution)/shard_map/while/body/eval_jaxpr/mul | solution.py:56
  310.3 19.9 %reshape.488 = f32[128,64,512]{2,1,0:T(8,128)} reshape(f32[8,1024,4,128]{3,2,1,0:T(4,128)} %copy.154) | data formatting | bytes 33554432 | tf_op jit(solution)/shard_map/while/body/eval_jaxpr/reshape | solution.py:62
  330.2 37.2 %scatter_fusion = f32[32,64,512]{2,1,0:T(8,128)} fusion(f32[32,64,512]{2,1,0:T(8,128)} %get-tuple-element.292, s32[128]{0:T(128)S(1)} %fusion.89, f32[128,64,512]{2,1,0:T(8,128)} %reshape.488), kind=kCustom, calls=%fused_computation.5.clone.1 | custom fusion | flops 4194304 | bytes 50332160 | tf_op jit(solution)/shard_map/while/body/eval_jaxpr/scatter-add | solution.py:116
  383.1 12.5 %reshape.486 = bf16[8,1024,4,128]{3,2,1,0:T(4,128)(2,1)} reshape(bf16[128,64,512]{2,1,0:T(8,128)(2,1)} %gather_fusion.1) | data formatting | bytes 16777216 | tf_op jit(solution)/shard_map/while/body/eval_jaxpr/reshape;while/body/eval_jaxpr/reshape | solution.py:26
  403.8 12.5 %reshape.484 = bf16[8,1024,4,128]{3,2,1,0:T(4,128)(2,1)} reshape(bf16[128,64,512]{2,1,0:T(8,128)(2,1)} %gather_fusion) | data formatting | bytes 16777216 | tf_op jit(solution)/shard_map/while/body/eval_jaxpr/reshape;while/body/eval_jaxpr/reshape | solution.py:27
  426.1 12.6 %fusion.92 = (f32[8,4,64]{2,1,0:T(4,128)S(1)}, f32[8,4,64,1024]{3,2,1,0:T(8,128)}) fusion(f32[8,4,64,1024]{3,2,1,0:T(8,128)} %fusion.90, pred[8,64,1024]{2,1,0:T(8,128)(4,1)S(1)} %copy-done.1), kind=kOutput, calls=%fused_computation.100.clone.1 | output fusion | flops 12583935 | bytes 17309696 | tf_op jit(solution)/shard_map/while/body/eval_jaxpr/sub | solution.py:43
  444.1 12.1 %multiply_convert_fusion.2 = bf16[8,4,64,1024]{3,2,1,0:T(8,128)(2,1)} fusion(f32[8,4,64]{2,1,0:T(4,128)S(1)} %fusion.93, f32[8,4,64,1024]{3,2,1,0:T(8,128)} %get-tuple-element.277, f32[8,4,64]{2,1,0:T(4,128)S(1)} %get-tuple-element.278, bf16[8,1024,4,128]{3,2,1,0:T(4,128)(2,1)} %reshape.484, bf16[8,64,4,128]{3,2,1,0:T(4,128)(2,1)S(1)} %reshape.485), kind=kOutput, calls=%fused_computation.12.clone.1 | convolution fusion | flops 545259520 | bytes 21512192 | tf_op jit(solution)/shard_map/while/body/eval_jaxpr/gqhd,gkhd->ghqk/dot_general | solution.py:48
  479.1 19.2 %copy.155 = f32[8,1024,4,128]{3,2,1,0:T(4,128)} copy(f32[8,1024,4,128]{1,3,2,0:T(8,128)} %convolution_bitcast_fusion.2) | data formatting | bytes 33554432 | tf_op jit(solution)/shard_map/while/body/eval_jaxpr/ghqk,gqhd->gkhd/transpose | solution.py:59
  498.3 19.9 %reshape.489 = f32[128,64,512]{2,1,0:T(8,128)} reshape(f32[8,1024,4,128]{3,2,1,0:T(4,128)} %copy.155) | data formatting | bytes 33554432 | tf_op jit(solution)/shard_map/while/body/eval_jaxpr/reshape | solution.py:63
  518.2 38.1 %scatter_fusion.1 = f32[32,64,512]{2,1,0:T(8,128)} fusion(f32[32,64,512]{2,1,0:T(8,128)} %get-tuple-element.293, s32[128]{0:T(128)S(1)} %fusion.89, f32[128,64,512]{2,1,0:T(8,128)} %reshape.489), kind=kCustom, calls=%fused_computation.6.clone.1 | custom fusion | flops 4194304 | bytes 50332160 | tf_op jit(solution)/shard_map/while/body/eval_jaxpr/scatter-add | solution.py:116
  566.6 19.2 %copy.154 = f32[8,1024,4,128]{3,2,1,0:T(4,128)} copy(f32[8,1024,4,128]{1,3,2,0:T(8,128)} %multiply_bitcast_fusion.2) | data formatting | bytes 33554432 | tf_op jit(solution)/shard_map/while/body/eval_jaxpr/mul | solution.py:56
  585.8 19.9 %reshape.488 = f32[128,64,512]{2,1,0:T(8,128)} reshape(f32[8,1024,4,128]{3,2,1,0:T(4,128)} %copy.154) | data formatting | bytes 33554432 | tf_op jit(solution)/shard_map/while/body/eval_jaxpr/reshape | solution.py:62
  605.7 37.8 %scatter_fusion = f32[32,64,512]{2,1,0:T(8,128)} fusion(f32[32,64,512]{2,1,0:T(8,128)} %get-tuple-element.292, s32[128]{0:T(128)S(1)} %fusion.89, f32[128,64,512]{2,1,0:T(8,128)} %reshape.488), kind=kCustom, calls=%fused_computation.5.clone.1 | custom fusion | flops 4194304 | bytes 50332160 | tf_op jit(solution)/shard_map/while/body/eval_jaxpr/scatter-add | solution.py:116
  678.1 24.4 %all-to-all-done.4 = f32[16,1,64,512]{3,2,1,0:T(8,128)} async-done(((f32[16,1,64,512]{3,2,1,0:T(8,128)}), f32[16,1,64,512]{3,2,1,0:T(8,128)}, u32[]{:S(2)}, u32[]{:S(2)}) %all-to-all-start.4) | async-done | bytes 2097184 | tf_op jit(solution)/shard_map/all_to_all | solution.py:122
  717.6 20.6 %all-to-all-done.6 = f32[16,1,64,512]{3,2,1,0:T(8,128)} async-done(((f32[16,1,64,512]{3,2,1,0:T(8,128)}), f32[16,1,64,512]{3,2,1,0:T(8,128)}, u32[]{:S(2)}, u32[]{:S(2)}) %all-to-all-start.6) | async-done | bytes 2097184 | tf_op jit(solution)/shard_map/all_to_all | solution.py:129
  (133 shorter events, 291.4 us)
Async XLA Ops:
  0.6 55.1 %copy-start.4 = (s32[16,16]{1,0:T(8,128)S(1)}, s32[16,16]{1,0:T(8,128)}, u32[]{:S(2)}) copy-start(s32[16,16]{1,0:T(8,128)} %param.11) | copy-start | bytes 3076
  0.6 55.1 %copy-start.2 = (bf16[1024,512]{1,0:T(8,128)(2,1)S(1)}, bf16[1024,512]{1,0:T(8,128)(2,1)}, u32[]{:S(2)}) copy-start(bf16[1024,512]{1,0:T(8,128)(2,1)} %param.8) | copy-start | bytes 3145732
  24.0 21.4 %all-to-all-start.1 = ((bf16[16,1,64,512]{3,2,1,0:T(8,128)(2,1)}), bf16[16,1,64,512]{3,2,1,0:T(8,128)(2,1)S(1)}, u32[]{:S(2)}, u32[]{:S(2)}) async-start(bf16[16,1,64,512]{3,2,1,0:T(8,128)(2,1)} %bitcast.19), calls=%async_computation.1 | async-start | bytes 2097152 | tf_op jit(solution)/shard_map/all_to_all | solution.py:90
  45.4 10.4 %copy-start.3 = (bf16[16,1,64,512]{3,2,1,0:T(8,128)(2,1)}, bf16[16,1,64,512]{3,2,1,0:T(8,128)(2,1)S(1)}, u32[]{:S(2)}) copy-start(bf16[16,1,64,512]{3,2,1,0:T(8,128)(2,1)S(1)} %all-to-all-done.1) | copy-start | bytes 3145732
  45.4 22.4 %all-to-all-start.2 = ((bf16[16,1,64,512]{3,2,1,0:T(8,128)(2,1)}), bf16[16,1,64,512]{3,2,1,0:T(8,128)(2,1)}, u32[]{:S(2)}, u32[]{:S(2)}) async-start(bf16[16,1,64,512]{3,2,1,0:T(8,128)(2,1)} %bitcast.23), calls=%async_computation.2 | async-start | bytes 2097152 | tf_op jit(solution)/shard_map/all_to_all | solution.py:91
  141.5 9.8 %copy-start.1 = (pred[8,64,1024]{2,1,0:T(8,128)(4,1)S(1)}, pred[8,64,1024]{2,1,0:T(8,128)(4,1)}, u32[]{:S(2)}) copy-start(pred[8,64,1024]{2,1,0:T(8,128)(4,1)} %or_and_fusion.2) | copy-start | bytes 1572868 | tf_op jit(solution)/shard_map/while
  141.5 22.3 %slice-start = ((s8[8388608]{0:T(1024)(128)(4,1)}), s8[4194304]{0:T(1024)(128)(4,1)S(1)}, s32[]{:S(2)}) async-start(s8[8388608]{0:T(1024)(128)(4,1)} %bitcast.97), calls=%async_computation.8 | async-start | bytes 8388608 | tf_op jit(solution)/shard_map/while
  151.3 12.6 %slice-start.1 = ((s8[8388608]{0:T(1024)(128)(4,1)}), s8[4194304]{0:T(1024)(128)(4,1)S(1)}, s32[]{:S(2)}) async-start(s8[8388608]{0:T(1024)(128)(4,1)} %bitcast.97), calls=%async_computation.9 | async-start | bytes 8388608 | tf_op jit(solution)/shard_map/while
  151.3 12.6 %copy-start = (f32[8,4,64,128]{3,1,2,0:T(4,128)S(1)}, f32[8,4,64,128]{3,1,2,0:T(4,128)}, u32[]{:S(2)}) copy-start(f32[8,4,64,128]{3,1,2,0:T(4,128)} %bitcast_convert_fusion.2) | copy-start | bytes 3145732 | tf_op jit(solution)/shard_map/while
  416.3 9.8 %copy-start.1 = (pred[8,64,1024]{2,1,0:T(8,128)(4,1)S(1)}, pred[8,64,1024]{2,1,0:T(8,128)(4,1)}, u32[]{:S(2)}) copy-start(pred[8,64,1024]{2,1,0:T(8,128)(4,1)} %or_and_fusion.2) | copy-start | bytes 1572868 | tf_op jit(solution)/shard_map/while
  416.3 22.3 %slice-start = ((s8[8388608]{0:T(1024)(128)(4,1)}), s8[4194304]{0:T(1024)(128)(4,1)S(1)}, s32[]{:S(2)}) async-start(s8[8388608]{0:T(1024)(128)(4,1)} %bitcast.97), calls=%async_computation.8 | async-start | bytes 8388608 | tf_op jit(solution)/shard_map/while
  426.1 12.6 %slice-start.1 = ((s8[8388608]{0:T(1024)(128)(4,1)}), s8[4194304]{0:T(1024)(128)(4,1)S(1)}, s32[]{:S(2)}) async-start(s8[8388608]{0:T(1024)(128)(4,1)} %bitcast.97), calls=%async_computation.9 | async-start | bytes 8388608 | tf_op jit(solution)/shard_map/while
  426.1 12.6 %copy-start = (f32[8,4,64,128]{3,1,2,0:T(4,128)S(1)}, f32[8,4,64,128]{3,1,2,0:T(4,128)}, u32[]{:S(2)}) copy-start(f32[8,4,64,128]{3,1,2,0:T(4,128)} %bitcast_convert_fusion.2) | copy-start | bytes 3145732 | tf_op jit(solution)/shard_map/while
  643.5 20.0 %all-to-all-start.3 = ((bf16[8,128,512]{2,1,0:T(8,128)(2,1)}), bf16[8,128,512]{2,1,0:T(8,128)(2,1)S(1)}, u32[]{:S(2)}, u32[]{:S(2)}) async-start(bf16[8,128,512]{2,1,0:T(8,128)(2,1)} %bitcast.109), calls=%async_computation.3 | async-start | bytes 2097152 | tf_op jit(solution)/shard_map/all_to_all | solution.py:145
  663.5 46.2 %copy-start.5 = (s32[16]{0:T(128)S(1)}, s32[16]{0:T(128)}, u32[]{:S(2)}) copy-start(s32[16]{0:T(128)} %get-tuple-element.154) | copy-start | bytes 196
  663.5 39.0 %all-to-all-start.4 = ((f32[16,1,64,512]{3,2,1,0:T(8,128)}), f32[16,1,64,512]{3,2,1,0:T(8,128)}, u32[]{:S(2)}, u32[]{:S(2)}) async-start(f32[16,1,64,512]{3,2,1,0:T(8,128)} %get-tuple-element.188), calls=%async_computation.4 | async-start | bytes 4194304 | tf_op jit(solution)/shard_map/all_to_all | solution.py:122
  702.5 35.7 %all-to-all-start.6 = ((f32[16,1,64,512]{3,2,1,0:T(8,128)}), f32[16,1,64,512]{3,2,1,0:T(8,128)}, u32[]{:S(2)}, u32[]{:S(2)}) async-start(f32[16,1,64,512]{3,2,1,0:T(8,128)} %get-tuple-element.186), calls=%async_computation.6 | async-start | bytes 4194304 | tf_op jit(solution)/shard_map/all_to_all | solution.py:129
  738.2 20.1 %all-to-all-start.5 = ((bf16[8,128,512]{2,1,0:T(8,128)(2,1)}), bf16[8,128,512]{2,1,0:T(8,128)(2,1)}, u32[]{:S(2)}, u32[]{:S(2)}) async-start(bf16[8,128,512]{2,1,0:T(8,128)(2,1)} %bitcast.31), calls=%async_computation.5 | async-start | bytes 2097152 | tf_op jit(solution)/shard_map/all_to_all | solution.py:146
  758.3 19.3 %all-to-all-start.7 = ((bf16[8,128,512]{2,1,0:T(8,128)(2,1)}), bf16[8,128,512]{2,1,0:T(8,128)(2,1)S(1)}, u32[]{:S(2)}, u32[]{:S(2)}) async-start(bf16[8,128,512]{2,1,0:T(8,128)(2,1)} %bitcast.36), calls=%async_computation.7 | async-start | bytes 2097152 | tf_op jit(solution)/shard_map/all_to_all | solution.py:147
where the time goes:
time: 791 us; the launch traced here: 780 us
  local copies, waits for them, and re-layouts  286 us (36%)
  other arithmetic  207 us (26%)
  matrix products  111 us (14%)
  waiting for transfers between devices  103 us (13%)
  starting transfers between devices  38.7 us (5%)
  loops' own time  17.4 us (2%)
  blocking collectives  16.2 us (2%)
    scatter-add x2, other arithmetic, advance(): grad_values.at[flat].add(dvalue)  75.6 us
    scatter-add x2, other arithmetic, advance(): grad_keys.at[flat].add(dkey)  74.9 us
    reshape x2, local copies, waits for them, and re-layouts, group_grads(): dvalue.reshape(count * TOPK, BLOCK, width)  39.8 us
    reshape x2, local copies, waits for them, and re-layouts, group_grads(): dkey.reshape(count * TOPK, BLOCK, width)  39.8 us
    transpose x2, local copies, waits for them, and re-layouts, group_grads(): jnp.einsum('ghqk,gqhd->gkhd', probs_low, grad_h, preferred_element_type=j...  38.4 us
    mul x2, local copies, waits for them, and re-layouts, group_grads(): jnp.einsum('ghqk,gqhd->gkhd', dscores_low, query_h, preferred_element_typ...  38.4 us
    sub x2, other arithmetic, group_grads(): expo = jnp.exp(scores - highest)  25.1 us
    reshape x2, local copies, waits for them, and re-layouts, group_grads(): key_h = key_blk.reshape(count, TOPK * BLOCK, HEAD_DEV, HDIM)  25.1 us
  transfers between devices with their start and end apart: 7, of which 7 were waited for; matrix products, arithmetic and copies ran while one was open for 5% of the time, Pallas kernels for 0%

commit v1 on v0

v1 whole, which is shorter than its diff:
```python
import jax
import jax.numpy as jnp
from jax import lax
from jax.experimental import pallas as pl
from jax.experimental.pallas import tpu as pltpu
from jax.sharding import PartitionSpec as P

HDIM = 128
BLOCK = 64
CHUNK = 256
SCALE = 1.0 / HDIM**0.5
LOG2E = 1.4426950408889634
EXP_SCALE = SCALE * LOG2E
MASKED = -1e30
F32 = jnp.float32
BF16 = jnp.bfloat16


def mm(a, b, dims):
    return lax.dot_general(a, b, (dims, ((), ())), preferred_element_type=F32)


NN = ((1,), (0,))
NT = ((1,), (1,))


def add_bias(scores, bias):
    keys, width = scores.shape
    blocks = keys // BLOCK
    return (scores.reshape(blocks, BLOCK, width) + bias[:, None, :]).reshape(keys, width)


def causal(scores):
    key_pos = lax.broadcasted_iota(jnp.int32, scores.shape, 0)
    query_pos = lax.broadcasted_iota(jnp.int32, scores.shape, 1)
    return jnp.where(key_pos <= query_pos, scores, MASKED)


def local_scores(k_ref, q, bias_ref, chunk):
    first = chunk * CHUNK
    last = first + CHUNK
    cols = pl.ds(first, CHUNK)
    diag = mm(k_ref[pl.ds(first, CHUNK), :], q, NT)
    diag = causal(add_bias(diag, bias_ref[pl.ds(first // BLOCK, CHUNK // BLOCK), cols]))
    if chunk == 0:
        return diag
    past = mm(k_ref[pl.ds(0, first), :], q, NT)
    past = add_bias(past, bias_ref[pl.ds(0, first // BLOCK), cols])
    return jnp.concatenate([past, diag], axis=0)


def local_stats_kernel(q_ref, do_ref, k_ref, v_ref, bias_ref, stat_ref):
    for chunk in range(q_ref.shape[0] // CHUNK):
        rows = pl.ds(chunk * CHUNK, CHUNK)
        end = (chunk + 1) * CHUNK
        s = local_scores(k_ref, q_ref[rows, :], bias_ref, chunk)
        dp = mm(v_ref[pl.ds(0, end), :], do_ref[rows, :], NT)
        top = jnp.max(s, axis=0, keepdims=True) * EXP_SCALE
        e = jnp.exp2(s * EXP_SCALE - top)
        stat_ref[0, 0:1, rows] = top
        stat_ref[0, 1:2, rows] = jnp.sum(e, axis=0, keepdims=True)
        stat_ref[0, 2:3, rows] = jnp.sum(e * dp, axis=0, keepdims=True)


def remote_kernel(q_ref, do_ref, k_ref, v_ref, bias_ref, stat_ref, dq_ref, grad_ref, full_ref, dk_acc, dv_acc):
    slots = k_ref.shape[0]
    keys = slots * BLOCK
    k = k_ref[...].reshape(keys, HDIM)
    v = v_ref[...].reshape(keys, HDIM)
    k_t = k.T
    for chunk in range(q_ref.shape[0] // CHUNK):
        rows = pl.ds(chunk * CHUNK, CHUNK)
        q = q_ref[rows, :]
        do = do_ref[rows, :]
        s = add_bias(mm(k, q, NT), bias_ref[:, rows])
        dp = mm(v, do, NT)
        top_loc = stat_ref[0, 0:1, rows]
        top = jnp.maximum(jnp.max(s, axis=0, keepdims=True) * EXP_SCALE, top_loc)
        e = jnp.exp2(s * EXP_SCALE - top)
        keep = jnp.exp2(top_loc - top)
        total = stat_ref[0, 1:2, rows] * keep + jnp.sum(e, axis=0, keepdims=True)
        dot = stat_ref[0, 2:3, rows] * keep + jnp.sum(e * dp, axis=0, keepdims=True)
        inv = 1.0 / total
        delta = dot * inv
        full_ref[0, 0:1, rows] = top
        full_ref[0, 1:2, rows] = inv
        full_ref[0, 2:3, rows] = delta
        p = e * inv
        ds = (p * (dp - delta)).astype(BF16)
        p = p.astype(BF16)
        dq_ref[0, :, rows] = mm(k_t, ds, NN)
        dk = mm(ds, q, NN)
        dv = mm(p, do, NN)
        if chunk == 0:
            dk_acc[...] = dk
            dv_acc[...] = dv
        else:
            dk_acc[...] += dk
            dv_acc[...] += dv
    grad_ref[:, 0:BLOCK, :] = (dk_acc[...] * SCALE).astype(BF16).reshape(slots, BLOCK, HDIM)
    grad_ref[:, BLOCK:, :] = dv_acc[...].astype(BF16).reshape(slots, BLOCK, HDIM)


def local_grads_kernel(q_ref, do_ref, k_ref, v_ref, bias_ref, full_ref, dqr_ref, dq_ref, dk_ref, dv_ref):
    k_t = k_ref[...].T
    for chunk in range(q_ref.shape[0] // CHUNK):
        rows = pl.ds(chunk * CHUNK, CHUNK)
        end = (chunk + 1) * CHUNK
        q = q_ref[rows, :]
        do = do_ref[rows, :]
        s = local_scores(k_ref, q, bias_ref, chunk)
        dp = mm(v_ref[pl.ds(0, end), :], do, NT)
        top = full_ref[0, 0:1, rows]
        inv = full_ref[0, 1:2, rows]
        delta = full_ref[0, 2:3, rows]
        p = jnp.exp2(s * EXP_SCALE - top) * inv
        ds = (p * (dp - delta)).astype(BF16)
        p = p.astype(BF16)
        dq = (dqr_ref[0, :, rows] + mm(k_t[:, :end], ds, NN)) * SCALE
        dq_ref[rows, :] = dq.T.astype(BF16)
        dk = mm(ds, q, NN)
        dv = mm(p, do, NN)
        if chunk == 0:
            dk_ref[rows, :] = dk
            dv_ref[rows, :] = dv
        else:
            past = pl.ds(0, chunk * CHUNK)
            dk_ref[past, :] += dk[: chunk * CHUNK]
            dv_ref[past, :] += dv[: chunk * CHUNK]
            dk_ref[rows, :] = dk[chunk * CHUNK :]
            dv_ref[rows, :] = dv[chunk * CHUNK :]


def gather_kernel(asks_ref, k_ref, v_ref, out_ref, sem):
    copies = []
    for slot in range(out_ref.shape[0]):
        rows = pl.ds(asks_ref[slot] * BLOCK, BLOCK)
        for part, src in enumerate((k_ref, v_ref)):
            copy = pltpu.make_async_copy(
                src.at[rows, :], out_ref.at[slot, pl.ds(part * BLOCK, BLOCK), :], sem.at[slot, part]
            )
            copy.start()
            copies.append(copy)
    for copy in copies:
        copy.wait()


def finish_kernel(asks_ref, dk_ref, dv_ref, back_ref, out_ref, acc):
    slots = back_ref.shape[0]
    acc[0] = dk_ref[...] * SCALE
    acc[1] = dv_ref[...]

    def add(slot, _):
        rows = pl.ds(pl.multiple_of(asks_ref[slot] * BLOCK, BLOCK), BLOCK)
        acc[0, rows, :] += back_ref[slot, 0:BLOCK, :].astype(F32)
        acc[1, rows, :] += back_ref[slot, BLOCK:, :].astype(F32)
        return 0

    lax.fori_loop(0, slots, add, 0)
    parts, _, per_part, width = out_ref.shape
    for part in range(parts):
        for which in range(2):
            out_ref[part, which] = acc[which, pl.ds(part * per_part, per_part), :].astype(BF16)


def params(**kwargs):
    return pltpu.CompilerParams(vmem_limit_bytes=48 << 20, **kwargs)


def per_device(queries, key_states, value_states, out_grad, selected):
    ranges = lax.axis_size("ctx")
    members = lax.axis_size("head")
    here = lax.axis_index("ctx")
    per_dev = selected.shape[0]
    tokens, width = queries.shape
    heads = width // HDIM
    ids = jnp.arange(ranges, dtype=jnp.int32)
    usable = selected >= 0
    owner = jnp.where(usable, selected // per_dev, -1)
    local_blk = jnp.where(usable, selected % per_dev, 0)
    from_range = owner[None] == ids[:, None, None]
    wanted = jnp.max(jnp.where(from_range, local_blk[None], 0), axis=(1, 2))
    asks = lax.all_to_all(wanted, "ctx", split_axis=0, concat_axis=0, tiled=True)

    blocks = jnp.arange(per_dev, dtype=jnp.int32)
    has_local = jnp.any(selected[None] == (here * per_dev + blocks)[:, None, None], axis=2)
    has_remote = jnp.any(from_range, axis=2) & (ids != here)[:, None]
    bias = jnp.where(jnp.concatenate([has_local, has_remote], axis=0), 0.0, MASKED).astype(F32)
    bias = jnp.repeat(bias, BLOCK, axis=1)
    bias_local, bias_remote = bias[:per_dev], bias[per_dev:]

    head_cols = pl.BlockSpec((tokens, HDIM), lambda h: (0, h))
    whole = lambda a: pl.BlockSpec(a.shape, lambda h: (0,) * len(a.shape))
    per_head = lambda shape: pl.BlockSpec((1,) + shape, lambda h: (h, 0, 0))
    pairs = tokens * tokens * heads
    in_any = pl.BlockSpec(memory_space=pl.ANY)

    sent = pl.pallas_call(
        gather_kernel,
        grid_spec=pltpu.PrefetchScalarGridSpec(
            num_scalar_prefetch=1,
            grid=(),
            in_specs=[in_any, in_any],
            out_specs=in_any,
            scratch_shapes=[pltpu.SemaphoreType.DMA((ranges, 2))],
        ),
        out_shape=jax.ShapeDtypeStruct((ranges, 2 * BLOCK, width), BF16),
    )(asks, key_states, value_states)
    got = lax.all_to_all(sent, "ctx", split_axis=0, concat_axis=0, tiled=True)

    stats = pl.pallas_call(
        local_stats_kernel,
        grid=(heads,),
        in_specs=[head_cols, head_cols, head_cols, head_cols, whole(bias_local)],
        out_specs=per_head((8, tokens)),
        out_shape=jax.ShapeDtypeStruct((heads, 8, tokens), F32),
        compiler_params=params(),
        cost_estimate=pl.CostEstimate(
            flops=2 * 2 * pairs * HDIM, bytes_accessed=4 * tokens * width * 2, transcendentals=pairs
        ),
    )(queries, out_grad, key_states, value_states, bias_local)

    slot_cols = lambda part: pl.BlockSpec((ranges, BLOCK, HDIM), lambda h: (0, part, h))
    remote_keys = ranges * BLOCK
    dq_remote, grads, full = pl.pallas_call(
        remote_kernel,
        grid=(heads,),
        in_specs=[
            head_cols,
            head_cols,
            slot_cols(0),
            slot_cols(1),
            whole(bias_remote),
            per_head((8, tokens)),
        ],
        out_specs=[
            per_head((HDIM, tokens)),
            pl.BlockSpec((ranges, 2 * BLOCK, HDIM), lambda h: (0, 0, h)),
            per_head((8, tokens)),
        ],
        out_shape=[
            jax.ShapeDtypeStruct((heads, HDIM, tokens), F32),
            jax.ShapeDtypeStruct((ranges, 2 * BLOCK, width), BF16),
            jax.ShapeDtypeStruct((heads, 8, tokens), F32),
        ],
        scratch_shapes=[pltpu.VMEM((remote_keys, HDIM), F32), pltpu.VMEM((remote_keys, HDIM), F32)],
        compiler_params=params(),
        cost_estimate=pl.CostEstimate(
            flops=5 * 2 * pairs * HDIM, bytes_accessed=8 * tokens * width * 2, transcendentals=pairs
        ),
    )(queries, out_grad, got, got, bias_remote, stats)
    back = lax.all_to_all(grads, "ctx", split_axis=0, concat_axis=0, tiled=True)

    dq, dk, dv = pl.pallas_call(
        local_grads_kernel,
        grid=(heads,),
        in_specs=[
            head_cols,
            head_cols,
            head_cols,
            head_cols,
            whole(bias_local),
            per_head((8, tokens)),
            per_head((HDIM, tokens)),
        ],
        out_specs=[head_cols, head_cols, head_cols],
        out_shape=[
            jax.ShapeDtypeStruct((tokens, width), BF16),
            jax.ShapeDtypeStruct((tokens, width), F32),
            jax.ShapeDtypeStruct((tokens, width), F32),
        ],
        compiler_params=params(),
        cost_estimate=pl.CostEstimate(
            flops=5 * 2 * pairs * HDIM, bytes_accessed=10 * tokens * width * 2, transcendentals=pairs
        ),
    )(queries, out_grad, key_states, value_states, bias_local, full, dq_remote)

    per_part = tokens // members
    dq_out = lax.all_to_all(
        dq.reshape(members, per_part, width), "head", split_axis=0, concat_axis=0, tiled=True
    )
    vmem = pl.BlockSpec(memory_space=pltpu.VMEM)
    totals = pl.pallas_call(
        finish_kernel,
        in_specs=[pl.BlockSpec(memory_space=pltpu.SMEM), vmem, vmem, vmem],
        out_specs=vmem,
        out_shape=jax.ShapeDtypeStruct((members, 2, per_part, width), BF16),
        scratch_shapes=[pltpu.VMEM((2, tokens, width), F32)],
        compiler_params=params(),
        cost_estimate=pl.CostEstimate(
            flops=4 * tokens * width, bytes_accessed=8 * tokens * width * 2, transcendentals=0
        ),
    )(asks, dk, dv, back)
    kv_out = lax.all_to_all(totals, "head", split_axis=0, concat_axis=0, tiled=True)
    query_out = dq_out.transpose(1, 0, 2).reshape(per_part, members * width)
    kv_out = kv_out.transpose(1, 2, 0, 3).reshape(2, per_part, members * width)
    return (query_out, kv_out[0], kv_out[1])


def solution(mesh):
    return jax.shard_map(
        per_device,
        mesh=mesh,
        in_specs=(
            P("ctx", "head"),
            P("ctx", "head"),
            P("ctx", "head"),
            P("ctx", "head"),
            P("ctx", None),
        ),
        out_specs=(P(("ctx", "head"), None), P(("ctx", "head"), None), P(("ctx", "head"), None)),
        check_vma=False,
    )
```

time: 791 us -> 237 us (0.30); the launches traced: 780 us -> 235 us
  local copies, waits for them, and re-layouts: 286 us -> 12.6 us
  other arithmetic: 207 us -> 2.86 us
  matrix products: 111 us -> 0 us
  Pallas kernels: 0 us -> 109 us
  waiting for transfers between devices: 103 us -> 72.8 us
  starting transfers between devices: 38.7 us -> 20.6 us
  loops' own time: 17.4 us -> 0 us
    scatter-add x6 -> x0, other arithmetic: 159 us -> none  [the longest x2 75.6 us: advance(): grad_values.at[flat].add(dvalue)]
    reshape x16 -> x1, local copies, waits for them, and re-layouts: 142 us -> 1.08 us  [per_device(): query_out = dq_out.transpose(1, 0, 2).reshape(per_part, members * width)]
    dot_general x12 -> x0, matrix products: 111 us -> none  [the longest x2 24.1 us: group_grads(): jnp.einsum('gqhd,gkhd->ghqk', grad_h, value_h, preferred_element_type=jnp...]
    pallas_call x0 -> x5, Pallas kernels: none -> 109 us  [the longest x1 65.6 us: per_device(): pl.pallas_call(gather_kernel, grid_spec=pltpu.PrefetchScalarGridSpec(num_...]
    gather x8 -> x0, local copies, waits for them, and re-layouts: 40.1 us -> none  [the longest x2 16 us: advance(): value_c = bank_values[index_c].reshape(GROUP, TOPK * BLOCK, width)]
    mul x2 -> x0, local copies, waits for them, and re-layouts: 38.4 us -> none  [group_grads(): jnp.einsum('ghqk,gqhd->gkhd', dscores_low, query_h, preferred_element_typ...]
    transpose x2 -> x0, local copies, waits for them, and re-layouts: 38.4 us -> none  [group_grads(): jnp.einsum('ghqk,gqhd->gkhd', probs_low, grad_h, preferred_element_type=j...]
    all_to_all x7 -> x4, waiting for transfers between devices: 103 us -> 72.8 us  [the longest x1 25.9 us: per_device(): lax.all_to_all(totals, 'head', split_axis=0, concat_axis=0, tiled=True)]
  transfers between devices with their start and end apart: 7 -> 4, of which waited for: 7 -> 4; matrix products, arithmetic and copies ran while one was open for 5% -> 1% of each run, Pallas kernels for 0% -> 10%
where the time goes in v1:
time: 237 us; the launch traced here: 235 us
  Pallas kernels  109 us (46%)
  waiting for transfers between devices  72.8 us (31%)
  starting transfers between devices  20.6 us (9%)
  blocking collectives  16.2 us (7%)
  local copies, waits for them, and re-layouts  12.6 us (5%)
  other arithmetic  2.86 us (1%)
    pallas_call x1, Pallas kernels, per_device(): pl.pallas_call(gather_kernel, grid_spec=pltpu.PrefetchScalarGridSpec(num_...  65.6 us
    all_to_all x1, waiting for transfers between devices, per_device(): lax.all_to_all(totals, 'head', split_axis=0, concat_axis=0, tiled=True)  25.9 us
    pallas_call x1, Pallas kernels, per_device(): pl.pallas_call(remote_kernel, grid=(heads,), in_specs=[head_cols, head_co...  21 us
    all_to_all x1, waiting for transfers between devices, per_device(): got = lax.all_to_all(sent, 'ctx', split_axis=0, concat_axis=0, tiled=True)  19.8 us
    all_to_all x1, blocking collectives, per_device(): lax.all_to_all(wanted, 'ctx', split_axis=0, concat_axis=0, tiled=True)  16.2 us
    all_to_all x1, waiting for transfers between devices, per_device(): back = lax.all_to_all(grads, 'ctx', split_axis=0, concat_axis=0, tiled=True)  15.8 us
    pallas_call x1, Pallas kernels, per_device(): pl.pallas_call(local_grads_kernel, grid=(heads,), in_specs=[head_cols, he...  11.5 us
    all_to_all x1, waiting for transfers between devices, per_device(): lax.all_to_all(dq.reshape(members, per_part, width), 'head', split_axis=0...  11.3 us
  transfers between devices with their start and end apart: 4, of which 4 were waited for; matrix products, arithmetic and copies ran while one was open for 1% of the time, Pallas kernels for 10%

profile of v1, /device:TPU:1, one launch (start us, length us, event | category | flops | bytes accessed | tf_op | source)
XLA Modules:
  0.0 234.9 jit_solution(11704942044389667522)
XLA Ops:
  1.8 16.2 %all_to_all.31 = s32[16,1,1]{2,1,0:T(1,128)S(1)} all-to-all(s32[16,1,1]{2,1,0:T(1,128)S(1)} %copy.26), channel_id=1, replica_groups=mesh['ctx'=16,'head'=8] {'ctx'}, dimensions={0} | all-to-all | bytes 128 | tf_op jit(solution)/shard_map/all_to_all | solution.py:183
  18.1 0.9 reduce.asks_ref
  18.9 65.6 %shard_map.76 = bf16[16,128,512]{2,1,0:T(8,128)(2,1)} custom-call(s32[16]{0:T(128)} %reduce.asks_ref, bf16[1024,512]{1,0:T(8,128)(2,1)} %k_ref.5, bf16[1024,512]{1,0:T(8,128)(2,1)} %v_ref.5), custom_call_target="tpu_custom_call" | custom-call | tf_op jit(solution)/shard_map/pallas_call | solution.py:198
  84.6 5.1 %all-to-all-start.1 = ((bf16[16,128,512]{2,1,0:T(8,128)(2,1)}), bf16[16,128,512]{2,1,0:T(8,128)(2,1)}, u32[]{:S(2)}, u32[]{:S(2)}) async-start(bf16[16,128,512]{2,1,0:T(8,128)(2,1)} %shard_map.76), calls=%async_computation.1 | async-start | bytes 4194304 | tf_op jit(solution)/shard_map/all_to_all | solution.py:209
  91.0 1.2 copy-done.5
  92.2 6.3 %shard_map.77.stat_ref = f32[4,8,1024]{2,1,0:T(8,128)S(1)} custom-call(bf16[1024,512]{1,0:T(8,128)(2,1)S(1)} %copy-done.4, bf16[1024,512]{1,0:T(8,128)(2,1)S(1)} %copy-done.5, bf16[1024,512]{1,0:T(8,128)(2,1)S(1)} %copy-done.1, bf16[1024,512]{1,0:T(8,128)(2,1)S(1)} %copy-done.2, f32[16,1024]{1,0:T(8,128)S(1)} %slice.23.bias_ref), custom_call_target="tpu_custom_call" | custom-call | flops 2147483648 | bytes 4194304 | tf_op jit(solution)/shard_map/pallas_call | solution.py:211
  98.5 19.8 %all-to-all-done.1.k_ref.v_ref = bf16[16,128,512]{2,1,0:T(8,128)(2,1)} async-done(((bf16[16,128,512]{2,1,0:T(8,128)(2,1)}), bf16[16,128,512]{2,1,0:T(8,128)(2,1)}, u32[]{:S(2)}, u32[]{:S(2)}) %all-to-all-start.1) | async-done | bytes 2097184 | tf_op jit(solution)/shard_map/all_to_all | solution.py:209
  118.3 1.2 copy-done.6
  119.6 21.0 %shard_map.78 = (f32[4,128,1024]{2,1,0:T(8,128)S(1)}, bf16[16,128,512]{2,1,0:T(8,128)(2,1)}, f32[4,8,1024]{2,1,0:T(8,128)S(1)}) custom-call(bf16[1024,512]{1,0:T(8,128)(2,1)S(1)} %copy-done.4, bf16[1024,512]{1,0:T(8,128)(2,1)S(1)} %copy-done.6, bf16[16,128,512]{2,1,0:T(8,128)(2,1)} %all-to-all-done.1.k_ref.v_ref, ...), custom_call_target="tpu_custom_call" | custom-call | flops 5368709120 | bytes 8388608 | tf_op jit(solution)/shard_map/pallas_call | solution.py:225
  140.6 1.3 copy-done.8
  141.9 6.9 %all-to-all-start.3 = ((bf16[16,128,512]{2,1,0:T(8,128)(2,1)}), bf16[16,128,512]{2,1,0:T(8,128)(2,1)}, u32[]{:S(2)}, u32[]{:S(2)}) async-start(bf16[16,128,512]{2,1,0:T(8,128)(2,1)} %get-tuple-element.14), calls=%async_computation.3 | async-start | bytes 4194304 | tf_op jit(solution)/shard_map/all_to_all | solution.py:252
  148.9 1.2 copy-done.7
  150.1 11.5 %shard_map.79 = (bf16[1024,512]{1,0:T(8,128)(2,1)}, f32[1024,512]{1,0:T(8,128)}, f32[1024,512]{1,0:T(8,128)}) custom-call(bf16[1024,512]{1,0:T(8,128)(2,1)S(1)} %copy-done.4, bf16[1024,512]{1,0:T(8,128)(2,1)S(1)} %copy-done.7, bf16[1024,512]{1,0:T(8,128)(2,1)S(1)} %copy-done.1, bf16[1024,512]{1,0:T(8,128)(2,1)S(1)} %copy-done.2, ...), custom_call_target="tpu_custom_call" | custom-call | flops 5368709120 | bytes 10485760 | tf_op jit(solution)/shard_map/pallas_call | solution.py:254
  161.6 15.8 %all-to-all-done.3.back_ref = bf16[16,128,512]{2,1,0:T(8,128)(2,1)} async-done(((bf16[16,128,512]{2,1,0:T(8,128)(2,1)}), bf16[16,128,512]{2,1,0:T(8,128)(2,1)}, u32[]{:S(2)}, u32[]{:S(2)}) %all-to-all-start.3) | async-done | bytes 2097184 | tf_op jit(solution)/shard_map/all_to_all | solution.py:252
  177.4 4.9 %all-to-all-start.2 = ((bf16[8,128,512]{2,1,0:T(8,128)(2,1)}), bf16[8,128,512]{2,1,0:T(8,128)(2,1)S(1)}, u32[]{:S(2)}, u32[]{:S(2)}) async-start(bf16[8,128,512]{2,1,0:T(8,128)(2,1)} %bitcast.1), calls=%async_computation.2 | async-start | bytes 2097152 | tf_op jit(solution)/shard_map/all_to_all | solution.py:279
  182.4 4.5 %shard_map.80 = bf16[8,2,128,512]{3,2,1,0:T(8,128)(2,1)} custom-call(s32[16]{0:T(128)S(1)} %copy-done.3, f32[1024,512]{1,0:T(8,128)S(1)} %copy-done, f32[1024,512]{1,0:T(8,128)} %get-tuple-element.13.dv_ref, bf16[16,128,512]{2,1,0:T(8,128)(2,1)} %all-to-all-done.3.back_ref), custom_call_target="tpu_custom_call" | custom-call | flops 2097152 | bytes 8388608 | tf_op jit(solution)/shard_map/pallas_call | solution.py:283
  186.9 11.3 %all-to-all-done.2 = bf16[8,128,512]{2,1,0:T(8,128)(2,1)S(1)} async-done(((bf16[8,128,512]{2,1,0:T(8,128)(2,1)}), bf16[8,128,512]{2,1,0:T(8,128)(2,1)S(1)}, u32[]{:S(2)}, u32[]{:S(2)}) %all-to-all-start.2) | async-done | bytes 1048608 | tf_op jit(solution)/shard_map/all_to_all | solution.py:279
  198.2 3.6 %all-to-all-start.4 = ((bf16[8,2,128,512]{3,2,1,0:T(8,128)(2,1)}), bf16[8,2,128,512]{3,2,1,0:T(8,128)(2,1)S(1)}, u32[]{:S(2)}, u32[]{:S(2)}) async-start(bf16[8,2,128,512]{3,2,1,0:T(8,128)(2,1)} %shard_map.80), calls=%async_computation.4 | async-start | bytes 4194304 | tf_op jit(solution)/shard_map/all_to_all | solution.py:294
  201.8 1.1 copy.32
  202.9 25.9 %all-to-all-done.4 = bf16[8,2,128,512]{3,2,1,0:T(8,128)(2,1)S(1)} async-done(((bf16[8,2,128,512]{3,2,1,0:T(8,128)(2,1)}), bf16[8,2,128,512]{3,2,1,0:T(8,128)(2,1)S(1)}, u32[]{:S(2)}, u32[]{:S(2)}) %all-to-all-start.4) | async-done | bytes 2097184 | tf_op jit(solution)/shard_map/all_to_all | solution.py:294
  228.8 1.2 fusion.5
  230.0 1.6 copy.29
  231.6 1.3 copy.31
  233.5 1.3 copy.30
  (31 shorter events, 3.1 us)
Async XLA Ops:
  84.5 5.5 %copy-start.9 = (s32[16,16]{1,0:T(8,128)S(1)}, s32[16,16]{1,0:T(8,128)}, u32[]{:S(2)}) copy-start(s32[16,16]{1,0:T(8,128)} %param.9) | copy-start | bytes 3076
  84.5 6.4 %copy-start.1 = (bf16[1024,512]{1,0:T(8,128)(2,1)S(1)}, bf16[1024,512]{1,0:T(8,128)(2,1)}, u32[]{:S(2)}) copy-start(bf16[1024,512]{1,0:T(8,128)(2,1)} %k_ref.5) | copy-start | bytes 3145732
  84.6 6.4 %copy-start.2 = (bf16[1024,512]{1,0:T(8,128)(2,1)S(1)}, bf16[1024,512]{1,0:T(8,128)(2,1)}, u32[]{:S(2)}) copy-start(bf16[1024,512]{1,0:T(8,128)(2,1)} %v_ref.5) | copy-start | bytes 3145732
  84.6 6.4 %copy-start.4 = (bf16[1024,512]{1,0:T(8,128)(2,1)S(1)}, bf16[1024,512]{1,0:T(8,128)(2,1)}, u32[]{:S(2)}) copy-start(bf16[1024,512]{1,0:T(8,128)(2,1)} %q_ref.5) | copy-start | bytes 3145732
  84.6 33.8 %all-to-all-start.1 = ((bf16[16,128,512]{2,1,0:T(8,128)(2,1)}), bf16[16,128,512]{2,1,0:T(8,128)(2,1)}, u32[]{:S(2)}, u32[]{:S(2)}) async-start(bf16[16,128,512]{2,1,0:T(8,128)(2,1)} %shard_map.76), calls=%async_computation.1 | async-start | bytes 4194304 | tf_op jit(solution)/shard_map/all_to_all | solution.py:209
  91.0 1.2 copy-start.5
  118.3 1.2 copy-start.6
  140.6 1.3 copy-start.8
  141.9 35.5 %all-to-all-start.3 = ((bf16[16,128,512]{2,1,0:T(8,128)(2,1)}), bf16[16,128,512]{2,1,0:T(8,128)(2,1)}, u32[]{:S(2)}, u32[]{:S(2)}) async-start(bf16[16,128,512]{2,1,0:T(8,128)(2,1)} %get-tuple-element.14), calls=%async_computation.3 | async-start | bytes 4194304 | tf_op jit(solution)/shard_map/all_to_all | solution.py:252
  148.9 1.2 copy-start.7
  161.6 20.8 %copy-start = (f32[1024,512]{1,0:T(8,128)S(1)}, f32[1024,512]{1,0:T(8,128)}, u32[]{:S(2)}) copy-start(f32[1024,512]{1,0:T(8,128)} %get-tuple-element.12.dk_ref) | copy-start | bytes 6291460
  161.6 20.8 %copy-start.3 = (s32[16]{0:T(128)S(1)}, s32[16]{0:T(128)}, u32[]{:S(2)}) copy-start(s32[16]{0:T(128)} %reduce.asks_ref) | copy-start | bytes 196
  177.4 20.7 %all-to-all-start.2 = ((bf16[8,128,512]{2,1,0:T(8,128)(2,1)}), bf16[8,128,512]{2,1,0:T(8,128)(2,1)S(1)}, u32[]{:S(2)}, u32[]{:S(2)}) async-start(bf16[8,128,512]{2,1,0:T(8,128)(2,1)} %bitcast.1), calls=%async_computation.2 | async-start | bytes 2097152 | tf_op jit(solution)/shard_map/all_to_all | solution.py:279
  198.2 30.6 %all-to-all-start.4 = ((bf16[8,2,128,512]{3,2,1,0:T(8,128)(2,1)}), bf16[8,2,128,512]{3,2,1,0:T(8,128)(2,1)S(1)}, u32[]{:S(2)}, u32[]{:S(2)}) async-start(bf16[8,2,128,512]{3,2,1,0:T(8,128)(2,1)} %shard_map.80), calls=%async_computation.4 | async-start | bytes 4194304 | tf_op jit(solution)/shard_map/all_to_all | solution.py:294

commit v2 on v1

v2 whole, which is shorter than its diff:
```python
import jax
import jax.numpy as jnp
from jax import lax
from jax.experimental import pallas as pl
from jax.experimental.pallas import tpu as pltpu
from jax.sharding import PartitionSpec as P

HDIM = 128
BLOCK = 64
CHUNK = 256
SCALE = 1.0 / HDIM**0.5
LOG2E = 1.4426950408889634
EXP_SCALE = SCALE * LOG2E
MASKED = -1e30
F32 = jnp.float32
BF16 = jnp.bfloat16


def mm(a, b, dims):
    return lax.dot_general(a, b, (dims, ((), ())), preferred_element_type=F32)


NN = ((1,), (0,))
NT = ((1,), (1,))


def add_bias(scores, bias):
    keys, width = scores.shape
    blocks = keys // BLOCK
    return (scores.reshape(blocks, BLOCK, width) + bias[:, None, :]).reshape(keys, width)


def causal(scores):
    key_pos = lax.broadcasted_iota(jnp.int32, scores.shape, 0)
    query_pos = lax.broadcasted_iota(jnp.int32, scores.shape, 1)
    return jnp.where(key_pos <= query_pos, scores, MASKED)


def local_scores(k_ref, q, bias_ref, chunk):
    first = chunk * CHUNK
    last = first + CHUNK
    cols = pl.ds(first, CHUNK)
    diag = mm(k_ref[pl.ds(first, CHUNK), :], q, NT)
    diag = causal(add_bias(diag, bias_ref[pl.ds(first // BLOCK, CHUNK // BLOCK), cols]))
    if chunk == 0:
        return diag
    past = mm(k_ref[pl.ds(0, first), :], q, NT)
    past = add_bias(past, bias_ref[pl.ds(0, first // BLOCK), cols])
    return jnp.concatenate([past, diag], axis=0)


def local_stats_kernel(q_ref, do_ref, k_ref, v_ref, bias_ref, stat_ref):
    for chunk in range(q_ref.shape[0] // CHUNK):
        rows = pl.ds(chunk * CHUNK, CHUNK)
        end = (chunk + 1) * CHUNK
        s = local_scores(k_ref, q_ref[rows, :], bias_ref, chunk)
        dp = mm(v_ref[pl.ds(0, end), :], do_ref[rows, :], NT)
        top = jnp.max(s, axis=0, keepdims=True) * EXP_SCALE
        e = jnp.exp2(s * EXP_SCALE - top)
        stat_ref[0, 0:1, rows] = top
        stat_ref[0, 1:2, rows] = jnp.sum(e, axis=0, keepdims=True)
        stat_ref[0, 2:3, rows] = jnp.sum(e * dp, axis=0, keepdims=True)


def remote_kernel(q_ref, do_ref, k_ref, v_ref, bias_ref, stat_ref, dq_ref, grad_ref, full_ref):
    slots = k_ref.shape[0] - 1
    keys = slots * BLOCK
    k = k_ref[0:slots].reshape(keys, HDIM)
    v = v_ref[0:slots].reshape(keys, HDIM)
    q = q_ref[...]
    do = do_ref[...]
    s = add_bias(mm(k, q, NT), bias_ref[0:slots, :])
    dp = mm(v, do, NT)
    top_loc = stat_ref[0, 0:1, :]
    top = jnp.maximum(jnp.max(s, axis=0, keepdims=True) * EXP_SCALE, top_loc)
    e = jnp.exp2(s * EXP_SCALE - top)
    keep = jnp.exp2(top_loc - top)
    total = stat_ref[0, 1:2, :] * keep + jnp.sum(e, axis=0, keepdims=True)
    dot = stat_ref[0, 2:3, :] * keep + jnp.sum(e * dp, axis=0, keepdims=True)
    inv = 1.0 / total
    delta = dot * inv
    full_ref[0, 0:1, :] = top
    full_ref[0, 1:2, :] = inv
    full_ref[0, 2:3, :] = delta
    p = e * inv
    ds = (p * (dp - delta)).astype(BF16)
    dq_ref[0] = mm(k.T, ds, NN)
    dk = mm(ds, q, NN) * SCALE
    dv = mm(p.astype(BF16), do, NN)
    grad_ref[0:slots, 0:BLOCK, :] = dk.astype(BF16).reshape(slots, BLOCK, HDIM)
    grad_ref[0:slots, BLOCK:, :] = dv.astype(BF16).reshape(slots, BLOCK, HDIM)
    grad_ref[slots] = jnp.zeros(grad_ref.shape[1:], BF16)


def local_grads_kernel(q_ref, do_ref, k_ref, v_ref, bias_ref, full_ref, dqr_ref, dq_ref, dk_ref, dv_ref):
    k_t = k_ref[...].T
    for chunk in range(q_ref.shape[0] // CHUNK):
        rows = pl.ds(chunk * CHUNK, CHUNK)
        end = (chunk + 1) * CHUNK
        q = q_ref[rows, :]
        do = do_ref[rows, :]
        s = local_scores(k_ref, q, bias_ref, chunk)
        dp = mm(v_ref[pl.ds(0, end), :], do, NT)
        top = full_ref[0, 0:1, rows]
        inv = full_ref[0, 1:2, rows]
        delta = full_ref[0, 2:3, rows]
        p = jnp.exp2(s * EXP_SCALE - top) * inv
        ds = (p * (dp - delta)).astype(BF16)
        p = p.astype(BF16)
        dq = (dqr_ref[0, :, rows] + mm(k_t[:, :end], ds, NN)) * SCALE
        parts = CHUNK // dq_ref.shape[2]
        dq_ref[pl.ds(chunk * parts, parts), 0] = dq.T.astype(BF16).reshape(parts, -1, HDIM)
        dk = mm(ds, q, NN)
        dv = mm(p, do, NN)
        if chunk == 0:
            dk_ref[rows, :] = dk
            dv_ref[rows, :] = dv
        else:
            past = pl.ds(0, chunk * CHUNK)
            dk_ref[past, :] += dk[: chunk * CHUNK]
            dv_ref[past, :] += dv[: chunk * CHUNK]
            dk_ref[rows, :] = dk[chunk * CHUNK :]
            dv_ref[rows, :] = dv[chunk * CHUNK :]


def gather_kernel(asks_ref, k_ref, v_ref, out_ref):
    for slot in range(out_ref.shape[0]):
        rows = pl.ds(pl.multiple_of(asks_ref[slot, 0] * BLOCK, BLOCK), BLOCK)
        out_ref[slot, 0:BLOCK, :] = k_ref[rows, :]
        out_ref[slot, BLOCK:, :] = v_ref[rows, :]


def finish_kernel(asks_ref, dk_ref, dv_ref, back_ref, _, out_ref, acc):
    acc[0] = dk_ref[...] * SCALE
    acc[1] = dv_ref[...]
    for slot in range(1, back_ref.shape[0]):
        rows = pl.ds(pl.multiple_of(asks_ref[slot, 0] * BLOCK, BLOCK), BLOCK)
        acc[0, rows, :] += back_ref[slot, 0:BLOCK, :].astype(F32)
        acc[1, rows, :] += back_ref[slot, BLOCK:, :].astype(F32)
    parts, _, per_part, _ = out_ref.shape
    for which in range(2):
        out_ref[:, which] = acc[which].astype(BF16).reshape(parts, per_part, HDIM)


def unpack_kernel(got_ref, *refs):
    outs, sem = refs[:-1], refs[-1]
    parts, _, _, width = got_ref.shape
    copies = []
    for part in range(parts):
        for which, out in enumerate(outs):
            cols = pl.ds(part * width, width)
            copy = pltpu.make_async_copy(got_ref.at[part, which], out.at[:, cols], sem.at[part, which])
            copy.start()
            copies.append(copy)
    for copy in copies:
        copy.wait()


def params(mib):
    return pltpu.CompilerParams(vmem_limit_bytes=mib << 20)


def per_device(queries, key_states, value_states, out_grad, selected):
    ranges = lax.axis_size("ctx")
    members = lax.axis_size("head")
    here = lax.axis_index("ctx")
    per_dev = selected.shape[0]
    tokens, width = queries.shape
    heads = width // HDIM
    ids = jnp.arange(ranges, dtype=jnp.int32)
    usable = selected >= 0
    owner = jnp.where(usable, selected // per_dev, -1)
    local_blk = jnp.where(usable, selected % per_dev, 0)
    from_range = owner[None] == ids[:, None, None]
    wanted = jnp.max(jnp.where(from_range, local_blk[None], 0), axis=(1, 2))
    wanted = jnp.broadcast_to(wanted[:, None], (ranges, HDIM))
    asks = lax.all_to_all(wanted, "ctx", split_axis=0, concat_axis=0, tiled=True)

    blocks = jnp.arange(per_dev, dtype=jnp.int32)
    has_local = jnp.any(selected[None] == (here * per_dev + blocks)[:, None, None], axis=2)
    has_remote = jnp.any(from_range, axis=2) & (ids != here)[:, None]
    bias = jnp.where(jnp.concatenate([has_local, has_remote], axis=0), 0.0, MASKED).astype(F32)
    bias = jnp.repeat(bias, BLOCK, axis=1)
    bias_local, bias_remote = bias[:per_dev], bias[per_dev:]

    head_cols = pl.BlockSpec((tokens, HDIM), lambda h: (0, h))
    whole = lambda a: pl.BlockSpec(a.shape, lambda h: (0,) * len(a.shape))
    per_head = lambda shape: pl.BlockSpec((1,) + shape, lambda h: (h, 0, 0))
    pairs = tokens * tokens * heads

    vmem = pl.BlockSpec(memory_space=pltpu.VMEM)
    smem = pl.BlockSpec(memory_space=pltpu.SMEM)
    sent = pl.pallas_call(
        gather_kernel,
        in_specs=[smem, vmem, vmem],
        out_specs=vmem,
        out_shape=jax.ShapeDtypeStruct((ranges, 2 * BLOCK, width), BF16),
        compiler_params=params(60),
    )(asks, key_states, value_states)
    got = lax.all_to_all(sent, "ctx", split_axis=0, concat_axis=0, tiled=True)

    stats = pl.pallas_call(
        local_stats_kernel,
        grid=(heads,),
        in_specs=[head_cols, head_cols, head_cols, head_cols, whole(bias_local)],
        out_specs=per_head((8, tokens)),
        out_shape=jax.ShapeDtypeStruct((heads, 8, tokens), F32),
        compiler_params=params(60),
        cost_estimate=pl.CostEstimate(
            flops=2 * 2 * pairs * HDIM, bytes_accessed=4 * tokens * width * 2, transcendentals=pairs
        ),
    )(queries, out_grad, key_states, value_states, bias_local)

    slot_cols = lambda part: pl.BlockSpec((ranges, BLOCK, HDIM), lambda h: (0, part, h))
    dq_remote, grads, full = pl.pallas_call(
        remote_kernel,
        grid=(heads,),
        in_specs=[
            head_cols,
            head_cols,
            slot_cols(0),
            slot_cols(1),
            whole(bias_remote),
            per_head((8, tokens)),
        ],
        out_specs=[
            per_head((HDIM, tokens)),
            pl.BlockSpec((ranges, 2 * BLOCK, HDIM), lambda h: (0, 0, h)),
            per_head((8, tokens)),
        ],
        out_shape=[
            jax.ShapeDtypeStruct((heads, HDIM, tokens), F32),
            jax.ShapeDtypeStruct((ranges, 2 * BLOCK, width), BF16),
            jax.ShapeDtypeStruct((heads, 8, tokens), F32),
        ],
        compiler_params=params(60),
        cost_estimate=pl.CostEstimate(
            flops=5 * 2 * pairs * HDIM, bytes_accessed=8 * tokens * width * 2, transcendentals=pairs
        ),
    )(queries, out_grad, got, got, bias_remote, stats)
    back = lax.all_to_all(grads, "ctx", split_axis=0, concat_axis=0, tiled=True)

    per_part = tokens // members
    mine, dk, dv = pl.pallas_call(
        local_grads_kernel,
        grid=(heads,),
        in_specs=[
            head_cols,
            head_cols,
            head_cols,
            head_cols,
            whole(bias_local),
            per_head((8, tokens)),
            per_head((HDIM, tokens)),
        ],
        out_specs=[
            pl.BlockSpec((members, 1, per_part, HDIM), lambda h: (0, 2, 0, h)),
            head_cols,
            head_cols,
        ],
        out_shape=[
            jax.ShapeDtypeStruct((members, 3, per_part, width), BF16),
            jax.ShapeDtypeStruct((tokens, width), F32),
            jax.ShapeDtypeStruct((tokens, width), F32),
        ],
        compiler_params=params(60),
        cost_estimate=pl.CostEstimate(
            flops=5 * 2 * pairs * HDIM, bytes_accessed=10 * tokens * width * 2, transcendentals=pairs
        ),
    )(queries, out_grad, key_states, value_states, bias_local, full, dq_remote)

    mine = pl.pallas_call(
        finish_kernel,
        grid=(heads,),
        in_specs=[
            smem,
            head_cols,
            head_cols,
            pl.BlockSpec((ranges, 2 * BLOCK, HDIM), lambda h: (0, 0, h)),
            pl.BlockSpec(memory_space=pl.ANY),
        ],
        out_specs=pl.BlockSpec((members, 2, per_part, HDIM), lambda h: (0, 0, 0, h)),
        out_shape=jax.ShapeDtypeStruct(mine.shape, BF16),
        scratch_shapes=[pltpu.VMEM((2, tokens, HDIM), F32)],
        input_output_aliases={4: 0},
        compiler_params=params(60),
        cost_estimate=pl.CostEstimate(
            flops=4 * tokens * width, bytes_accessed=8 * tokens * width * 2, transcendentals=0
        ),
    )(asks, dk, dv, back, mine)
    theirs = lax.all_to_all(mine, "head", split_axis=0, concat_axis=0, tiled=True)
    key_out, value_out, query_out = pl.pallas_call(
        unpack_kernel,
        in_specs=[vmem],
        out_specs=[pl.BlockSpec(memory_space=pl.ANY)] * 3,
        out_shape=[jax.ShapeDtypeStruct((per_part, members * width), BF16)] * 3,
        scratch_shapes=[pltpu.SemaphoreType.DMA((members, 3))],
        compiler_params=params(16),
    )(theirs)
    return (query_out, key_out, value_out)


def solution(mesh):
    return jax.shard_map(
        per_device,
        mesh=mesh,
        in_specs=(
            P("ctx", "head"),
            P("ctx", "head"),
            P("ctx", "head"),
            P("ctx", "head"),
            P("ctx", None),
        ),
        out_specs=(P(("ctx", "head"), None), P(("ctx", "head"), None), P(("ctx", "head"), None)),
        check_vma=False,
    )
```

time: 237 us -> 160 us (0.68)
  Pallas kernels: 109 us -> 46 us
  blocking collectives: 16.2 us -> 58.3 us
  waiting for transfers between devices: 72.8 us -> 35.2 us
  starting transfers between devices: 20.6 us -> 11.1 us
  local copies, waits for them, and re-layouts: 12.6 us -> 4.42 us
    pallas_call x2 -> x3, Pallas kernels: 70.1 us -> 9.9 us  [the longest x1 5.03 us: per_device(): pl.pallas_call(finish_kernel, grid=(heads,), in_specs=[smem, head_cols, h...]
    all_to_all x0 -> x1, blocking collectives: none -> 41.9 us  [per_device(): lax.all_to_all(mine, 'head', split_axis=0, concat_axis=0, tiled=True)]
    all_to_all x2 -> x0, waiting for transfers between devices: 37.2 us -> none  [the longest x1 25.9 us: per_device(): lax.all_to_all(totals, 'head', split_axis=0, concat_axis=0, tiled=True)]
    all_to_all x2 -> x0, starting transfers between devices: 8.55 us -> none  [the longest x1 4.95 us: per_device(): lax.all_to_all(dq.reshape(members, per_part, width), 'head', split_axis=0...]
    unnamed x22 -> x6, local copies, waits for them, and re-layouts: 7.66 us -> 2.72 us
    pallas_call x1, Pallas kernels: 21 us -> 16.9 us  [per_device(): pl.pallas_call(remote_kernel, grid=(heads,), in_specs=[head_cols, head_co...]
    slice x3 -> x0, local copies, waits for them, and re-layouts: 3.42 us -> none  [per_device(): return (query_out, kv_out[0], kv_out[1])]
  transfers between devices with their start and end apart: 4 -> 2, of which waited for: 4 -> 2; matrix products, arithmetic and copies ran while one was open for 1% -> 2% of each run, Pallas kernels for 10% -> 12%
where the time goes in v2:
time: 160 us; the launch traced here: 158 us
  blocking collectives  58.3 us (36%)
  Pallas kernels  46 us (29%)
  waiting for transfers between devices  35.2 us (22%)
  starting transfers between devices  11.1 us (7%)
  local copies, waits for them, and re-layouts  4.42 us (3%)
  other arithmetic  1.97 us (1%)
    all_to_all x1, blocking collectives, per_device(): lax.all_to_all(mine, 'head', split_axis=0, concat_axis=0, tiled=True)  41.9 us
    all_to_all x1, waiting for transfers between devices, per_device(): got = lax.all_to_all(sent, 'ctx', split_axis=0, concat_axis=0, tiled=True)  18.7 us
    pallas_call x1, Pallas kernels, per_device(): pl.pallas_call(remote_kernel, grid=(heads,), in_specs=[head_cols, head_co...  16.9 us
    all_to_all x1, waiting for transfers between devices, per_device(): back = lax.all_to_all(grads, 'ctx', split_axis=0, concat_axis=0, tiled=True)  16.6 us
    all_to_all x1, blocking collectives, per_device(): lax.all_to_all(wanted, 'ctx', split_axis=0, concat_axis=0, tiled=True)  16.4 us
    pallas_call x1, Pallas kernels, per_device(): pl.pallas_call(local_grads_kernel, grid=(heads,), in_specs=[head_cols, he...  11.9 us
    pallas_call x1, Pallas kernels, per_device(): pl.pallas_call(local_stats_kernel, grid=(heads,), in_specs=[head_cols, he...  7.34 us
    all_to_all x1, starting transfers between devices, per_device(): back = lax.all_to_all(grads, 'ctx', split_axis=0, concat_axis=0, tiled=True)  6.93 us
  transfers between devices with their start and end apart: 2, of which 2 were waited for; matrix products, arithmetic and copies ran while one was open for 2% of the time, Pallas kernels for 12%

profile of v2, /device:TPU:1, one launch (start us, length us, event | category | flops | bytes accessed | tf_op | source)
XLA Modules:
  0.0 157.7 jit_solution(17687988723867652488)
XLA Ops:
  0.6 0.7 fusion.1
  1.3 0.4 select_reduce_fusion
  1.7 0.1 broadcast_in_dim.42
  1.8 16.4 %all_to_all.23 = s32[16,1,128]{2,1,0:T(1,128)} all-to-all(s32[16,1,128]{2,1,0:T(1,128)S(1)} %broadcast_in_dim.42), channel_id=1, replica_groups=mesh['ctx'=16,'head'=8] {'ctx'}, dimensions={0} | all-to-all | bytes 16384 | tf_op jit(solution)/shard_map/all_to_all | solution.py:177
  18.2 3.0 %shard_map.76 = bf16[16,128,512]{2,1,0:T(8,128)(2,1)} custom-call(s32[16,128]{1,0:T(8,128)} %bitcast.1, bf16[1024,512]{1,0:T(8,128)(2,1)} %k_ref.5, bf16[1024,512]{1,0:T(8,128)(2,1)} %v_ref.5), custom_call_target="tpu_custom_call" | custom-call | tf_op jit(solution)/shard_map/pallas_call | solution.py:193
  21.2 4.2 %all-to-all-start.1 = ((bf16[16,128,512]{2,1,0:T(8,128)(2,1)}), bf16[16,128,512]{2,1,0:T(8,128)(2,1)S(1)}, u32[]{:S(2)}, u32[]{:S(2)}) async-start(bf16[16,128,512]{2,1,0:T(8,128)(2,1)} %shard_map.76), calls=%async_computation.1 | async-start | bytes 4194304 | tf_op jit(solution)/shard_map/all_to_all | solution.py:200
  25.4 0.4 fusion
  25.7 0.4 compare_reduce_fusion
  26.1 0.1 broadcast_and_fusion
  26.2 0.1 broadcast_in_dim.46
  26.3 0.7 slice.17.bias_ref
  27.1 0.1 broadcast_in_dim.45
  27.2 0.7 slice.15.bias_ref
  27.9 7.3 %shard_map.77.stat_ref = f32[4,8,1024]{2,1,0:T(8,128)} custom-call(bf16[1024,512]{1,0:T(8,128)(2,1)} %q_ref.5, bf16[1024,512]{1,0:T(8,128)(2,1)} %do_ref.5, bf16[1024,512]{1,0:T(8,128)(2,1)} %k_ref.5, bf16[1024,512]{1,0:T(8,128)(2,1)} %v_ref.5, f32[16,1024]{1,0:T(8,128)} %slice.15.bias_ref), custom_call_target="tpu_custom_call" | custom-call | flops 2147483648 | bytes 4194304 | tf_op jit(solution)/shard_map/pallas_call | solution.py:202
  35.2 18.7 %all-to-all-done.1.k_ref.v_ref = bf16[16,128,512]{2,1,0:T(8,128)(2,1)S(1)} async-done(((bf16[16,128,512]{2,1,0:T(8,128)(2,1)}), bf16[16,128,512]{2,1,0:T(8,128)(2,1)S(1)}, u32[]{:S(2)}, u32[]{:S(2)}) %all-to-all-start.1) | async-done | bytes 2097184 | tf_op jit(solution)/shard_map/all_to_all | solution.py:200
  53.9 1.3 copy-done.1
  55.2 16.9 %shard_map.78 = (f32[4,128,1024]{2,1,0:T(8,128)}, bf16[16,128,512]{2,1,0:T(8,128)(2,1)}, f32[4,8,1024]{2,1,0:T(8,128)}) custom-call(bf16[1024,512]{1,0:T(8,128)(2,1)} %q_ref.5, bf16[1024,512]{1,0:T(8,128)(2,1)} %do_ref.5, bf16[16,128,512]{2,1,0:T(8,128)(2,1)} %copy-done.1, bf16[16,128,512]{2,1,0:T(8,128)(2,1)} %copy-done.1, f32[16,1024]{1,0:T(8,128)} %slice.17.bias_ref, ...), custom_call_target="tpu_custom_call" | custom-call | flops 5368709120 | bytes 8388608 | tf_op jit(solution)/shard_map/pallas_call | solution.py:215
  72.1 6.9 %all-to-all-start.2 = ((bf16[16,128,512]{2,1,0:T(8,128)(2,1)}), bf16[16,128,512]{2,1,0:T(8,128)(2,1)S(1)}, u32[]{:S(2)}, u32[]{:S(2)}) async-start(bf16[16,128,512]{2,1,0:T(8,128)(2,1)} %get-tuple-element.16), calls=%async_computation.2 | async-start | bytes 4194304 | tf_op jit(solution)/shard_map/all_to_all | solution.py:241
  79.0 11.9 %shard_map.79 = (bf16[8,3,128,512]{3,2,1,0:T(8,128)(2,1)}, f32[1024,512]{1,0:T(8,128)}, f32[1024,512]{1,0:T(8,128)}) custom-call(bf16[1024,512]{1,0:T(8,128)(2,1)} %q_ref.5, bf16[1024,512]{1,0:T(8,128)(2,1)} %do_ref.5, bf16[1024,512]{1,0:T(8,128)(2,1)} %k_ref.5, bf16[1024,512]{1,0:T(8,128)(2,1)} %v_ref.5, f32[16,1024]{1,0:T(8,128)} %slice.15.bias_ref, ...), custom_call_target="tpu_custom_call" | custom-call | flops 5368709120 | bytes 10485760 | tf_op jit(solution)/shard_map/pallas_call | solution.py:244
  90.9 16.6 %all-to-all-done.2.back_ref = bf16[16,128,512]{2,1,0:T(8,128)(2,1)S(1)} async-done(((bf16[16,128,512]{2,1,0:T(8,128)(2,1)}), bf16[16,128,512]{2,1,0:T(8,128)(2,1)S(1)}, u32[]{:S(2)}, u32[]{:S(2)}) %all-to-all-start.2) | async-done | bytes 2097184 | tf_op jit(solution)/shard_map/all_to_all | solution.py:241
  107.5 1.4 copy-done
  108.9 5.0 %shard_map.80 = bf16[8,3,128,512]{3,2,1,0:T(8,128)(2,1)} custom-call(s32[16,128]{1,0:T(8,128)} %bitcast.2, f32[1024,512]{1,0:T(8,128)} %get-tuple-element.14.dk_ref, f32[1024,512]{1,0:T(8,128)} %get-tuple-element.15.dv_ref, bf16[16,128,512]{2,1,0:T(8,128)(2,1)} %copy-done, bf16[8,3,128,512]{3,2,1,0:T(8,128)(2,1)} %get-tuple-element.17._), custom_call_target="tpu_custom_call", output_to_operand_aliasing={{}: (4, {})} | custom-call | flops 2097152 | bytes 8388608 | tf_op jit(solution)/shard_map/pallas_call | solution.py:272
  113.9 41.9 %all_to_all.24.got_ref = bf16[8,3,128,512]{3,2,1,0:T(8,128)(2,1)S(1)} all-to-all(bf16[8,3,128,512]{3,2,1,0:T(8,128)(2,1)} %shard_map.80), channel_id=1, replica_groups=mesh['ctx'=16,'head'=8] {'head'}, dimensions={0} | all-to-all | bytes 6291456 | tf_op jit(solution)/shard_map/all_to_all | solution.py:291
  155.8 1.8 %shard_map.81 = (bf16[128,4096]{1,0:T(8,128)(2,1)}, bf16[128,4096]{1,0:T(8,128)(2,1)}, bf16[128,4096]{1,0:T(8,128)(2,1)}) custom-call(bf16[8,3,128,512]{3,2,1,0:T(8,128)(2,1)S(1)} %all_to_all.24.got_ref), custom_call_target="tpu_custom_call" | custom-call | tf_op jit(solution)/shard_map/pallas_call | solution.py:292
  (8 shorter events, 0.0 us)
Async XLA Ops:
  21.2 4.5 %copy-start.2 = (s32[16,16]{1,0:T(8,128)S(1)}, s32[16,16]{1,0:T(8,128)}, u32[]{:S(2)}) copy-start(s32[16,16]{1,0:T(8,128)} %param.9) | copy-start | bytes 3076
  21.2 32.7 %all-to-all-start.1 = ((bf16[16,128,512]{2,1,0:T(8,128)(2,1)}), bf16[16,128,512]{2,1,0:T(8,128)(2,1)S(1)}, u32[]{:S(2)}, u32[]{:S(2)}) async-start(bf16[16,128,512]{2,1,0:T(8,128)(2,1)} %shard_map.76), calls=%async_computation.1 | async-start | bytes 4194304 | tf_op jit(solution)/shard_map/all_to_all | solution.py:200
  53.9 1.3 copy-start.1
  72.1 35.4 %all-to-all-start.2 = ((bf16[16,128,512]{2,1,0:T(8,128)(2,1)}), bf16[16,128,512]{2,1,0:T(8,128)(2,1)S(1)}, u32[]{:S(2)}, u32[]{:S(2)}) async-start(bf16[16,128,512]{2,1,0:T(8,128)(2,1)} %get-tuple-element.16), calls=%async_computation.2 | async-start | bytes 4194304 | tf_op jit(solution)/shard_map/all_to_all | solution.py:241
  107.5 1.4 copy-start

commit v3 on v2

v3 whole, which is shorter than its diff:
```python
import jax
import jax.numpy as jnp
from jax import lax
from jax.experimental import pallas as pl
from jax.experimental.pallas import tpu as pltpu
from jax.sharding import PartitionSpec as P

HDIM = 128
BLOCK = 64
CHUNK = 256
SCALE = 1.0 / HDIM**0.5
LOG2E = 1.4426950408889634
EXP_SCALE = SCALE * LOG2E
MASKED = -1e30
HALVES = 2
LIMIT = 63
F32 = jnp.float32
BF16 = jnp.bfloat16


def mm(a, b, dims):
    return lax.dot_general(a, b, (dims, ((), ())), preferred_element_type=F32)


NN = ((1,), (0,))
NT = ((1,), (1,))


def add_bias(scores, bias):
    keys, width = scores.shape
    blocks = keys // BLOCK
    return (scores.reshape(blocks, BLOCK, width) + bias[:, None, :]).reshape(keys, width)


def causal(scores):
    key_pos = lax.broadcasted_iota(jnp.int32, scores.shape, 0)
    query_pos = lax.broadcasted_iota(jnp.int32, scores.shape, 1)
    return jnp.where(key_pos <= query_pos, scores, MASKED)


def local_scores(k_ref, q, bias_ref, chunk):
    first = chunk * CHUNK
    last = first + CHUNK
    cols = pl.ds(first, CHUNK)
    diag = mm(k_ref[pl.ds(first, CHUNK), :], q, NT)
    diag = causal(add_bias(diag, bias_ref[pl.ds(first // BLOCK, CHUNK // BLOCK), cols]))
    if chunk == 0:
        return diag
    past = mm(k_ref[pl.ds(0, first), :], q, NT)
    past = add_bias(past, bias_ref[pl.ds(0, first // BLOCK), cols])
    return jnp.concatenate([past, diag], axis=0)


def local_stats_kernel(q_ref, do_ref, k_ref, v_ref, bias_ref, stat_ref):
    for chunk in range(q_ref.shape[0] // CHUNK):
        rows = pl.ds(chunk * CHUNK, CHUNK)
        end = (chunk + 1) * CHUNK
        s = local_scores(k_ref, q_ref[rows, :], bias_ref, chunk)
        dp = mm(v_ref[pl.ds(0, end), :], do_ref[rows, :], NT)
        top = jnp.max(s, axis=0, keepdims=True) * EXP_SCALE
        e = jnp.exp2(s * EXP_SCALE - top)
        stat_ref[0, 0:1, rows] = top
        stat_ref[0, 1:2, rows] = jnp.sum(e, axis=0, keepdims=True)
        stat_ref[0, 2:3, rows] = jnp.sum(e * dp, axis=0, keepdims=True)


def remote_kernel(here_ref, q_ref, do_ref, k_ref, v_ref, bias_ref, stat_ref, *refs):
    *next_ref, dq_ref, grad_ref, full_ref = refs
    slots = k_ref.shape[0] - 1
    keys = slots * BLOCK
    k = k_ref[0:slots].reshape(keys, HDIM)
    v = v_ref[0:slots].reshape(keys, HDIM)
    q = q_ref[...]
    do = do_ref[...]
    s = add_bias(mm(k, q, NT), bias_ref[0:slots, :])
    dp = mm(v, do, NT)
    top_loc = stat_ref[0, 0:1, :]
    top = jnp.maximum(jnp.max(s, axis=0, keepdims=True) * EXP_SCALE, top_loc)
    e = jnp.exp2(s * EXP_SCALE - top)
    keep = jnp.exp2(top_loc - top)
    total = stat_ref[0, 1:2, :] * keep + jnp.sum(e, axis=0, keepdims=True)
    dot = stat_ref[0, 2:3, :] * keep + jnp.sum(e * dp, axis=0, keepdims=True)
    inv = 1.0 / total
    delta = dot * inv
    full_ref[0, 0:1, :] = top
    full_ref[0, 1:2, :] = inv
    full_ref[0, 2:3, :] = delta
    p = e * inv
    ds = (p * (dp - delta)).astype(BF16)
    dq_ref[0] = mm(k.T, ds, NN)
    dk = mm(ds, q, NN) * SCALE
    dv = mm(p.astype(BF16), do, NN)
    grad_ref[0:slots, 0:BLOCK, :] = dk.astype(BF16).reshape(slots, BLOCK, HDIM)
    grad_ref[0:slots, BLOCK:, :] = dv.astype(BF16).reshape(slots, BLOCK, HDIM)
    grad_ref[slots] = jnp.zeros(grad_ref.shape[1:], BF16)
    for ref in next_ref:
        for slot in range(slots + 1):

            @pl.when(slot > here_ref[0])
            def _():
                grad_ref[slot] = ref[slot]


def local_grads_kernel(q_ref, do_ref, k_ref, v_ref, bias_ref, full_ref, dqr_ref, dq_ref, dk_ref, dv_ref, dk_acc, dv_acc):
    k_t = k_ref[...].T
    for chunk in range(q_ref.shape[0] // CHUNK):
        rows = pl.ds(chunk * CHUNK, CHUNK)
        first = chunk * CHUNK
        end = first + CHUNK
        q = q_ref[rows, :]
        do = do_ref[rows, :]
        s = local_scores(k_ref, q, bias_ref, chunk)
        dp = mm(v_ref[pl.ds(0, end), :], do, NT)
        top = full_ref[0, 0:1, rows]
        inv = full_ref[0, 1:2, rows]
        delta = full_ref[0, 2:3, rows]
        p = jnp.exp2(s * EXP_SCALE - top) * inv
        ds = (p * (dp - delta)).astype(BF16)
        p = p.astype(BF16)
        dq = (dqr_ref[0, :, rows] + mm(k_t[:, :end], ds, NN)) * SCALE
        dq_ref[rows, :] = dq.T.astype(BF16)
        dk = mm(ds, q, NN)
        dv = mm(p, do, NN)
        if chunk > 0:
            dk_acc[0:first, :] += dk[:first]
            dv_acc[0:first, :] += dv[:first]
        dk_acc[rows, :] = dk[first:]
        dv_acc[rows, :] = dv[first:]
    dk_ref[...] = dk_acc[...] * SCALE
    dv_ref[...] = dv_acc[...]


def gather_kernel(asks_ref, k_ref, v_ref, *out_refs):
    for slot in range(out_refs[0].shape[0]):
        rows = pl.ds(pl.multiple_of(asks_ref[slot, 0] * BLOCK, BLOCK), BLOCK)
        for half, out_ref in enumerate(out_refs):
            width = out_ref.shape[2]
            cols = pl.ds(half * width, width)
            out_ref[slot, 0:BLOCK, :] = k_ref[rows, cols]
            out_ref[slot, BLOCK:, :] = v_ref[rows, cols]


def add_back(here_ref, asks_ref, dk_ref, dv_ref, back_ref, acc):
    acc[0] = dk_ref[...]
    acc[1] = dv_ref[...]
    for slot in range(1, back_ref.shape[0]):

        @pl.when(slot > here_ref[0])
        def _():
            rows = pl.ds(pl.multiple_of(asks_ref[slot, 0] * BLOCK, BLOCK), BLOCK)
            acc[0, rows, :] += back_ref[slot, 0:BLOCK, :].astype(F32)
            acc[1, rows, :] += back_ref[slot, BLOCK:, :].astype(F32)


def finish_kernel(here_ref, asks_ref, dq_ref, dk_ref, dv_ref, back_ref, out_ref, acc):
    add_back(here_ref, asks_ref, dk_ref, dv_ref, back_ref, acc)
    parts, _, per_part, _ = out_ref.shape
    for which in range(2):
        out_ref[:, which] = acc[which].astype(BF16).reshape(parts, per_part, HDIM)
    out_ref[:, 2] = dq_ref[...].reshape(parts, per_part, HDIM)


def finish_pieces_kernel(here_ref, asks_ref, me_ref, dq_ref, dk_ref, dv_ref, back_ref, *refs):
    *piece_refs, acc = refs
    add_back(here_ref, asks_ref, dk_ref, dv_ref, back_ref, acc)
    for d, piece_ref in enumerate(piece_refs):
        size = piece_ref.shape[1]
        rows = pl.ds(pl.multiple_of((me_ref[0] ^ d) * size, size), size)
        for which in range(2):
            piece_ref[which] = acc[which, rows, :].astype(BF16)
        piece_ref[2] = dq_ref[rows, :]


def unpack_kernel(half, got_ref, *refs):
    *outs, sem = refs
    outs = outs[-3:]
    parts, _, _, width = got_ref.shape
    copies = []
    for part in range(parts):
        for which, out in enumerate(outs):
            cols = pl.ds((part * HALVES + half) * width, width)
            copy = pltpu.make_async_copy(got_ref.at[part, which], out.at[:, cols], sem.at[part, which])
            copy.start()
            copies.append(copy)
    for copy in copies:
        copy.wait()


def unpack_pieces_kernel(half, me_ref, *refs):
    *refs, sem = refs
    pieces, outs = refs[:-3], refs[-3:]
    width = pieces[0].shape[2]
    copies = []
    for d, piece in enumerate(pieces):
        part = me_ref[0] ^ d
        for which, out in enumerate(outs):
            cols = pl.ds(pl.multiple_of((part * HALVES + half) * width, width), width)
            copy = pltpu.make_async_copy(piece.at[which], out.at[:, cols], sem.at[d, which])
            copy.start()
            copies.append(copy)
    for copy in copies:
        copy.wait()


def params(mib=LIMIT):
    return pltpu.CompilerParams(vmem_limit_bytes=mib << 20)


def swap(array, axis):
    return lax.all_to_all(array, axis, split_axis=0, concat_axis=0, tiled=True)


def per_device(queries, key_states, value_states, out_grad, selected):
    ranges = lax.axis_size("ctx")
    members = lax.axis_size("head")
    here = lax.axis_index("ctx")
    per_dev = selected.shape[0]
    tokens, width = queries.shape
    heads = width // HDIM
    half_heads = heads // HALVES
    half_width = width // HALVES
    per_part = tokens // members
    ids = jnp.arange(ranges, dtype=jnp.int32)
    usable = selected >= 0
    owner = jnp.where(usable, selected // per_dev, -1)
    local_blk = jnp.where(usable, selected % per_dev, 0)
    from_range = owner[None] == ids[:, None, None]
    wanted = jnp.max(jnp.where(from_range, local_blk[None], 0), axis=(1, 2))
    asks = swap(jnp.broadcast_to(wanted[:, None], (ranges, HDIM)), "ctx")
    here_arr = here.astype(jnp.int32).reshape(1)
    me_arr = lax.axis_index("head").astype(jnp.int32).reshape(1)

    vmem = pl.BlockSpec(memory_space=pltpu.VMEM)
    smem = pl.BlockSpec(memory_space=pltpu.SMEM)
    in_any = pl.BlockSpec(memory_space=pl.ANY)
    cols_at = lambda first: pl.BlockSpec((tokens, HDIM), lambda h: (0, first + h))
    whole = lambda a: pl.BlockSpec(a.shape, lambda h: (0,) * len(a.shape))
    per_head = lambda shape, first=0: pl.BlockSpec((1,) + shape, lambda h: (first + h, 0, 0))
    slot_cols = pl.BlockSpec((ranges, 2 * BLOCK, HDIM), lambda h: (0, 0, h))
    part_cols = lambda part: pl.BlockSpec((ranges, BLOCK, HDIM), lambda h: (0, part, h))
    pairs = tokens * tokens * half_heads
    cost = lambda dots, arrays: pl.CostEstimate(
        flops=dots * 2 * pairs * HDIM, bytes_accessed=arrays * tokens * half_width * 2, transcendentals=pairs
    )
    slots_half = jax.ShapeDtypeStruct((ranges, 2 * BLOCK, half_width), BF16)

    sent = pl.pallas_call(
        gather_kernel,
        in_specs=[smem, vmem, vmem],
        out_specs=[vmem] * HALVES,
        out_shape=[slots_half] * HALVES,
        compiler_params=params(),
    )(asks, key_states, value_states)
    selected, here, sent = lax.optimization_barrier((selected, here, sent))
    owner = jnp.where(selected >= 0, selected // per_dev, -1)
    from_range = owner[None] == ids[:, None, None]
    blocks = jnp.arange(per_dev, dtype=jnp.int32)
    has_local = jnp.any(selected[None] == (here * per_dev + blocks)[:, None, None], axis=2)
    has_remote = jnp.any(from_range, axis=2) & (ids != here)[:, None]
    bias = jnp.where(jnp.concatenate([has_local, has_remote], axis=0), 0.0, MASKED).astype(F32)
    bias = jnp.repeat(bias, BLOCK, axis=1)
    bias_local, bias_remote = bias[:per_dev], bias[per_dev:]
    got = swap(sent[0], "ctx")
    stats = pl.pallas_call(
        local_stats_kernel,
        grid=(heads,),
        in_specs=[cols_at(0)] * 4 + [whole(bias_local)],
        out_specs=per_head((8, tokens)),
        out_shape=jax.ShapeDtypeStruct((heads, 8, tokens), F32),
        compiler_params=params(),
        cost_estimate=cost(4, 8),
    )(queries, out_grad, key_states, value_states, bias_local)

    def remote(half, got, ahead):
        first = half * half_heads
        return pl.pallas_call(
            remote_kernel,
            grid=(half_heads,),
            in_specs=[
                smem,
                cols_at(first),
                cols_at(first),
                part_cols(0),
                part_cols(1),
                whole(bias_remote),
                per_head((8, tokens), first),
            ]
            + [slot_cols] * len(ahead),
            out_specs=[per_head((HDIM, tokens)), slot_cols, per_head((8, tokens))],
            out_shape=[
                jax.ShapeDtypeStruct((half_heads, HDIM, tokens), F32),
                slots_half,
                jax.ShapeDtypeStruct((half_heads, 8, tokens), F32),
            ],
            compiler_params=params(),
            cost_estimate=cost(5, 8),
        )(here_arr, queries, out_grad, got, got, bias_remote, stats, *ahead)

    def local(half, full, dq_remote):
        first = half * half_heads
        return pl.pallas_call(
            local_grads_kernel,
            grid=(half_heads,),
            in_specs=[cols_at(first)] * 4
            + [whole(bias_local), per_head((8, tokens)), per_head((HDIM, tokens))],
            out_specs=[cols_at(0)] * 3,
            out_shape=[
                jax.ShapeDtypeStruct((tokens, half_width), BF16),
                jax.ShapeDtypeStruct((tokens, half_width), F32),
                jax.ShapeDtypeStruct((tokens, half_width), F32),
            ],
            scratch_shapes=[pltpu.VMEM((tokens, HDIM), F32)] * 2,
            compiler_params=params(),
            cost_estimate=cost(5, 10),
        )(queries, out_grad, key_states, value_states, bias_local, full, dq_remote)

    finish_cost = pl.CostEstimate(
        flops=4 * tokens * half_width, bytes_accessed=16 * tokens * half_width, transcendentals=0
    )
    finish_acc = [pltpu.VMEM((2, tokens, HDIM), F32)]
    outs_shape = [jax.ShapeDtypeStruct((per_part, members * width), BF16)] * 3
    outs_sems = [pltpu.SemaphoreType.DMA((members, 3))]

    def finish(back, grads):
        return pl.pallas_call(
            finish_kernel,
            grid=(half_heads,),
            in_specs=[smem, smem] + [cols_at(0)] * 3 + [slot_cols],
            out_specs=pl.BlockSpec((members, 3, per_part, HDIM), lambda h: (0, 0, 0, h)),
            out_shape=jax.ShapeDtypeStruct((members, 3, per_part, half_width), BF16),
            scratch_shapes=finish_acc,
            compiler_params=params(),
            cost_estimate=finish_cost,
        )(here_arr, asks, *grads, back)

    def finish_pieces(back, grads):
        return pl.pallas_call(
            finish_pieces_kernel,
            grid=(half_heads,),
            in_specs=[smem, smem, smem] + [cols_at(0)] * 3 + [slot_cols],
            out_specs=[pl.BlockSpec((3, per_part, HDIM), lambda h: (0, 0, h))] * members,
            out_shape=[jax.ShapeDtypeStruct((3, per_part, half_width), BF16)] * members,
            scratch_shapes=finish_acc,
            compiler_params=params(),
            cost_estimate=finish_cost,
        )(here_arr, asks, me_arr, *grads, back)

    def unpack_pieces(half, pieces):
        return pl.pallas_call(
            lambda *refs: unpack_pieces_kernel(half, *refs),
            in_specs=[smem] + [vmem] * members,
            out_specs=[in_any] * 3,
            out_shape=outs_shape,
            scratch_shapes=outs_sems,
            compiler_params=params(16),
        )(me_arr, *pieces)

    def unpack(half, theirs, outs):
        return pl.pallas_call(
            lambda *refs: unpack_kernel(half, *refs),
            in_specs=[vmem] + [in_any] * len(outs),
            out_specs=[in_any] * 3,
            out_shape=outs_shape,
            scratch_shapes=outs_sems,
            input_output_aliases={1 + i: i for i in range(len(outs))},
            compiler_params=params(16),
        )(theirs, *outs)

    dq0, both, full0 = remote(0, got, sent[1:])
    both = swap(both, "ctx")
    own0 = local(0, full0, dq0)
    both, own0 = lax.optimization_barrier((both, own0))
    dq1, grads, full1 = remote(1, both, [])
    grads, both = lax.optimization_barrier((grads, both))
    back = swap(grads, "ctx")
    pieces = finish_pieces(both, own0)
    pieces = [pieces[0]] + [
        lax.ppermute(pieces[d], "head", [(i, i ^ d) for i in range(members)]) for d in range(1, members)
    ]
    own1 = local(1, full1, dq1)
    own1, pieces = lax.optimization_barrier((own1, pieces))
    outs = unpack_pieces(0, pieces)
    mine1 = finish(back, own1)
    key_out, value_out, query_out = unpack(1, swap(mine1, "head"), outs)
    return (query_out, key_out, value_out)


def solution(mesh):
    return jax.shard_map(
        per_device,
        mesh=mesh,
        in_specs=(
            P("ctx", "head"),
            P("ctx", "head"),
            P("ctx", "head"),
            P("ctx", "head"),
            P("ctx", None),
        ),
        out_specs=(P(("ctx", "head"), None), P(("ctx", "head"), None), P(("ctx", "head"), None)),
        check_vma=False,
    )
```

time: 160 us -> 154 us (0.963)
  blocking collectives: 58.3 us -> 0 us
  starting transfers between devices: 11.1 us -> 37.7 us
  waiting for transfers between devices: 35.2 us -> 55.1 us
  Pallas kernels: 46 us -> 54.1 us
    all_to_all x2 -> x0, blocking collectives: 58.3 us -> none  [the longest x1 41.9 us: per_device(): lax.all_to_all(mine, 'head', split_axis=0, concat_axis=0, tiled=True)]
    all_to_all x2 -> x5, starting transfers between devices: 11.1 us -> 29.3 us  [swap(): return lax.all_to_all(array, axis, split_axis=0, concat_axis=0, tiled=True)]
    ppermute x0 -> x7, waiting for transfers between devices: none -> 11 us  [per_device(): lax.ppermute(pieces[d], 'head', [(i, i ^ d) for i in range(members)])]
    all_to_all x2 -> x5, waiting for transfers between devices: 35.2 us -> 44.1 us  [swap(): return lax.all_to_all(array, axis, split_axis=0, concat_axis=0, tiled=True)]
    ppermute x0 -> x7, starting transfers between devices: none -> 8.44 us  [per_device(): lax.ppermute(pieces[d], 'head', [(i, i ^ d) for i in range(members)])]
    pallas_call x6 -> x10, Pallas kernels: 46 us -> 54.1 us  [the longest x2 19.4 us: remote(): pl.pallas_call(remote_kernel, grid=(half_heads,), in_specs=[smem, cols_at...]
    unnamed x6, local copies, waits for them, and re-layouts: 2.72 us -> 0.6 us
  transfers between devices with their start and end apart: 2 -> 12, of which waited for: 2 -> 7; matrix products, arithmetic and copies ran while one was open for 2% -> 1% of each run, Pallas kernels for 12% -> 18%
where the time goes in v3:
time: 154 us; the launch traced here: 153 us
  waiting for transfers between devices  55.1 us (36%)
  Pallas kernels  54.1 us (35%)
  starting transfers between devices  37.7 us (24%)
  local copies, waits for them, and re-layouts  2.91 us (2%)
  other arithmetic  2.04 us (1%)
    all_to_all x5, waiting for transfers between devices, swap(): return lax.all_to_all(array, axis, split_axis=0, concat_axis=0, tiled=True)  44.1 us
    all_to_all x5, starting transfers between devices, swap(): return lax.all_to_all(array, axis, split_axis=0, concat_axis=0, tiled=True)  29.3 us
    pallas_call x2, Pallas kernels, remote(): pl.pallas_call(remote_kernel, grid=(half_heads,), in_specs=[smem, cols_at...  19.4 us
    pallas_call x2, Pallas kernels, local(): pl.pallas_call(local_grads_kernel, grid=(half_heads,), in_specs=[cols_at(...  14.1 us
    ppermute x7, waiting for transfers between devices, per_device(): lax.ppermute(pieces[d], 'head', [(i, i ^ d) for i in range(members)])  11 us
    ppermute x7, starting transfers between devices, per_device(): lax.ppermute(pieces[d], 'head', [(i, i ^ d) for i in range(members)])  8.44 us
    pallas_call x1, Pallas kernels, per_device(): pl.pallas_call(local_stats_kernel, grid=(heads,), in_specs=[cols_at(0)] *...  7.33 us
    pallas_call x1, Pallas kernels, finish(): pl.pallas_call(finish_kernel, grid=(half_heads,), in_specs=[smem, smem] +...  3.32 us
  transfers between devices with their start and end apart: 12, of which 7 were waited for; matrix products, arithmetic and copies ran while one was open for 1% of the time, Pallas kernels for 18%

profile of v3, /device:TPU:1, one launch (start us, length us, event | category | flops | bytes accessed | tf_op | source)
XLA Modules:
  0.0 152.8 jit_solution(105952830390065969)
XLA Ops:
  2.5 9.5 %all-to-all-start = ((s32[16,1,128]{2,1,0:T(1,128)}), s32[16,1,128]{2,1,0:T(1,128)S(1)}, u32[]{:S(2)}, u32[]{:S(2)}) async-start(s32[16,1,128]{2,1,0:T(1,128)} %broadcast_in_dim.45), calls=%async_computation | async-start | bytes 16384 | tf_op jit(solution)/shard_map/all_to_all | solution.py:210
  12.0 6.9 %all-to-all-done = s32[16,1,128]{2,1,0:T(1,128)S(1)} async-done(((s32[16,1,128]{2,1,0:T(1,128)}), s32[16,1,128]{2,1,0:T(1,128)S(1)}, u32[]{:S(2)}, u32[]{:S(2)}) %all-to-all-start) | async-done | bytes 8224 | tf_op jit(solution)/shard_map/all_to_all | solution.py:210
  19.5 3.0 %shard_map.76 = (bf16[16,128,256]{2,1,0:T(8,128)(2,1)}, bf16[16,128,256]{2,1,0:T(8,128)(2,1)}) custom-call(s32[16,128]{1,0:T(8,128)} %bitcast.3, bf16[1024,512]{1,0:T(8,128)(2,1)} %k_ref.7, bf16[1024,512]{1,0:T(8,128)(2,1)} %v_ref.7), custom_call_target="tpu_custom_call" | custom-call | tf_op jit(solution)/shard_map/pallas_call | solution.py:247
  22.8 4.7 %all-to-all-start.1 = ((bf16[16,128,256]{2,1,0:T(8,128)(2,1)}), bf16[16,128,256]{2,1,0:T(8,128)(2,1)}, u32[]{:S(2)}, u32[]{:S(2)}) async-start(bf16[16,128,256]{2,1,0:T(8,128)(2,1)} %get-tuple-element.56), calls=%async_computation.1 | async-start | bytes 2097152 | tf_op jit(solution)/shard_map/all_to_all | solution.py:210
  29.8 7.3 %shard_map.77.stat_ref = f32[4,8,1024]{2,1,0:T(8,128)} custom-call(bf16[1024,512]{1,0:T(8,128)(2,1)} %q_ref.9, bf16[1024,512]{1,0:T(8,128)(2,1)} %do_ref.9, bf16[1024,512]{1,0:T(8,128)(2,1)} %k_ref.7, bf16[1024,512]{1,0:T(8,128)(2,1)} %v_ref.7, f32[16,1024]{1,0:T(8,128)} %slice.15.bias_ref), custom_call_target="tpu_custom_call" | custom-call | flops 2147483648 | bytes 4194304 | tf_op jit(solution)/shard_map/pallas_call | solution.py:264
  37.1 7.9 %all-to-all-done.1.k_ref.v_ref = bf16[16,128,256]{2,1,0:T(8,128)(2,1)} async-done(((bf16[16,128,256]{2,1,0:T(8,128)(2,1)}), bf16[16,128,256]{2,1,0:T(8,128)(2,1)}, u32[]{:S(2)}, u32[]{:S(2)}) %all-to-all-start.1) | async-done | bytes 1048608 | tf_op jit(solution)/shard_map/all_to_all | solution.py:210
  45.0 10.1 %shard_map.78 = (f32[2,128,1024]{2,1,0:T(8,128)}, bf16[16,128,256]{2,1,0:T(8,128)(2,1)}, f32[2,8,1024]{2,1,0:T(8,128)}) custom-call(s32[1]{0:T(128)} %bitcast.here_ref, bf16[1024,512]{1,0:T(8,128)(2,1)} %q_ref.9, bf16[1024,512]{1,0:T(8,128)(2,1)} %do_ref.9, bf16[16,128,256]{2,1,0:T(8,128)(2,1)} %all-to-all-done.1.k_ref.v_ref, ...), custom_call_target="tpu_custom_call" | custom-call | flops 2684354560 | bytes 4194304 | tf_op jit(solution)/shard_map/pallas_call | solution.py:276
  55.1 5.0 %all-to-all-start.2 = ((bf16[16,128,256]{2,1,0:T(8,128)(2,1)}), bf16[16,128,256]{2,1,0:T(8,128)(2,1)}, u32[]{:S(2)}, u32[]{:S(2)}) async-start(bf16[16,128,256]{2,1,0:T(8,128)(2,1)} %get-tuple-element.58), calls=%async_computation.2 | async-start | bytes 2097152 | tf_op jit(solution)/shard_map/all_to_all | solution.py:210
  60.1 7.1 %shard_map.79 = (bf16[1024,256]{1,0:T(8,128)(2,1)}, f32[1024,256]{1,0:T(8,128)}, f32[1024,256]{1,0:T(8,128)}) custom-call(bf16[1024,512]{1,0:T(8,128)(2,1)} %q_ref.9, bf16[1024,512]{1,0:T(8,128)(2,1)} %do_ref.9, bf16[1024,512]{1,0:T(8,128)(2,1)} %k_ref.7, bf16[1024,512]{1,0:T(8,128)(2,1)} %v_ref.7, f32[16,1024]{1,0:T(8,128)} %slice.15.bias_ref, ...), custom_call_target="tpu_custom_call" | custom-call | flops 2684354560 | bytes 5242880 | tf_op jit(solution)/shard_map/pallas_call | solution.py:301
  67.2 10.3 %all-to-all-done.2.k_ref.v_ref.back_ref = bf16[16,128,256]{2,1,0:T(8,128)(2,1)} async-done(((bf16[16,128,256]{2,1,0:T(8,128)(2,1)}), bf16[16,128,256]{2,1,0:T(8,128)(2,1)}, u32[]{:S(2)}, u32[]{:S(2)}) %all-to-all-start.2) | async-done | bytes 1048608 | tf_op jit(solution)/shard_map/all_to_all | solution.py:210
  77.5 9.3 %shard_map.80 = (f32[2,128,1024]{2,1,0:T(8,128)}, bf16[16,128,256]{2,1,0:T(8,128)(2,1)}, f32[2,8,1024]{2,1,0:T(8,128)}) custom-call(s32[1]{0:T(128)} %bitcast.here_ref, bf16[1024,512]{1,0:T(8,128)(2,1)} %q_ref.9, bf16[1024,512]{1,0:T(8,128)(2,1)} %do_ref.9, bf16[16,128,256]{2,1,0:T(8,128)(2,1)} %all-to-all-done.2.k_ref.v_ref.back_ref, ...), custom_call_target="tpu_custom_call" | custom-call | flops 2684354560 | bytes 4194304 | tf_op jit(solution)/shard_map/pallas_call | solution.py:276
  86.8 5.2 %all-to-all-start.3 = ((bf16[16,128,256]{2,1,0:T(8,128)(2,1)}), bf16[16,128,256]{2,1,0:T(8,128)(2,1)}, u32[]{:S(2)}, u32[]{:S(2)}) async-start(bf16[16,128,256]{2,1,0:T(8,128)(2,1)} %get-tuple-element.86), calls=%async_computation.3 | async-start | bytes 2097152 | tf_op jit(solution)/shard_map/all_to_all | solution.py:210
  92.0 3.2 %shard_map.82 = (bf16[3,128,256]{2,1,0:T(8,128)(2,1)}, bf16[3,128,256]{2,1,0:T(8,128)(2,1)}, bf16[3,128,256]{2,1,0:T(8,128)(2,1)}, bf16[3,128,256]{2,1,0:T(8,128...) custom-call(s32[1]{0:T(128)} %bitcast.here_ref, ...), custom_call_target="tpu_custom_call" | custom-call | flops 1048576 | bytes 4194304 | tf_op jit(solution)/shard_map/pallas_call | solution.py:337
  96.5 2.4 %collective-permute-start.1 = (bf16[3,128,256]{2,1,0:T(8,128)(2,1)}, bf16[3,128,256]{2,1,0:T(8,128)(2,1)S(1)}, u32[]{:S(2)}, u32[]{:S(2)}) collective-permute-start(bf16[3,128,256]{2,1,0:T(8,128)(2,1)} %get-tuple-element.77), channel_id=1, source_target_pairs={{0,2},{1,3},{2,0},{3,1},{4,6},{5,7},{6,4},{7,5},{8,10},{9,11},{10,... | collective-permute-start | bytes 589832 | tf_op jit(solution)/shard_map/ppermute | solution.py:378
  100.3 1.5 collective-permute-done.refs_2_
  101.8 2.9 %collective-permute-start.5 = (bf16[3,128,256]{2,1,0:T(8,128)(2,1)}, bf16[3,128,256]{2,1,0:T(8,128)(2,1)}, u32[]{:S(2)}, u32[]{:S(2)}) collective-permute-start(bf16[3,128,256]{2,1,0:T(8,128)(2,1)} %get-tuple-element.81), channel_id=1, source_target_pairs={{0,6},{1,7},{2,4},{3,5},{4,2},{5,3},{6,0},{7,1},{8,14},{9,15},{10,... | collective-permute-start | bytes 589832 | tf_op jit(solution)/shard_map/ppermute | solution.py:378
  104.7 3.4 %collective-permute-done.1.refs_3_ = bf16[3,128,256]{2,1,0:T(8,128)(2,1)S(1)} collective-permute-done((bf16[3,128,256]{2,1,0:T(8,128)(2,1)}, bf16[3,128,256]{2,1,0:T(8,128)(2,1)S(1)}, u32[]{:S(2)}, u32[]{:S(2)}) %collective-permute-start.1) | collective-permute-done | bytes 196640 | tf_op jit(solution)/shard_map/ppermute | solution.py:378
  108.5 7.0 %shard_map.81 = (bf16[1024,256]{1,0:T(8,128)(2,1)}, f32[1024,256]{1,0:T(8,128)}, f32[1024,256]{1,0:T(8,128)}) custom-call(bf16[1024,512]{1,0:T(8,128)(2,1)} %q_ref.9, bf16[1024,512]{1,0:T(8,128)(2,1)} %do_ref.9, bf16[1024,512]{1,0:T(8,128)(2,1)} %k_ref.7, bf16[1024,512]{1,0:T(8,128)(2,1)} %v_ref.7, f32[16,1024]{1,0:T(8,128)} %slice.15.bias_ref, ...), custom_call_target="tpu_custom_call" | custom-call | flops 2684354560 | bytes 5242880 | tf_op jit(solution)/shard_map/pallas_call | solution.py:301
  115.6 6.1 %collective-permute-done.3.refs_5_ = bf16[3,128,256]{2,1,0:T(8,128)(2,1)S(1)} collective-permute-done((bf16[3,128,256]{2,1,0:T(8,128)(2,1)}, bf16[3,128,256]{2,1,0:T(8,128)(2,1)S(1)}, u32[]{:S(2)}, u32[]{:S(2)}) %collective-permute-start.3) | collective-permute-done | bytes 196640 | tf_op jit(solution)/shard_map/ppermute | solution.py:378
  121.7 3.3 %shard_map.83 = bf16[8,3,128,256]{3,2,1,0:T(8,128)(2,1)} custom-call(s32[1]{0:T(128)} %bitcast.here_ref, s32[16,128]{1,0:T(8,128)} %bitcast.5, bf16[1024,256]{1,0:T(8,128)(2,1)} %get-tuple-element.83.dq_ref, f32[1024,256]{1,0:T(8,128)} %get-tuple-element.84.dk_ref, f32[1024,256]{1,0:T(8,128)} %get-tuple-element.85.dv_ref, ...), custom_call_target="tpu_custom_call" | custom-call | flops 1048576 | bytes 4194304 | tf_op jit(solution)/shard_map/pallas_call | solution.py:325
  125.0 4.9 %all-to-all-start.4 = ((bf16[8,3,128,256]{3,2,1,0:T(8,128)(2,1)}), bf16[8,3,128,256]{3,2,1,0:T(8,128)(2,1)S(1)}, u32[]{:S(2)}, u32[]{:S(2)}) async-start(bf16[8,3,128,256]{3,2,1,0:T(8,128)(2,1)} %shard_map.83), calls=%async_computation.4 | async-start | bytes 3145728 | tf_op jit(solution)/shard_map/all_to_all | solution.py:210
  129.9 2.4 %shard_map.84 = (bf16[128,4096]{1,0:T(8,128)(2,1)}, bf16[128,4096]{1,0:T(8,128)(2,1)}, bf16[128,4096]{1,0:T(8,128)(2,1)}) custom-call(s32[1]{0:T(128)} %bitcast.2.me_ref.refs_0_, bf16[3,128,256]{2,1,0:T(8,128)(2,1)S(1)} %copy-done, bf16[3,128,256]{2,1,0:T(8,128)(2,1)S(1)} %collective-permute-done.refs_2_, ...), custom_call_target="tpu_custom_call" | custom-call | tf_op jit(solution)/shard_map/pallas_call | solution.py:349
  132.3 19.1 %all-to-all-done.4.refs_0_ = bf16[8,3,128,256]{3,2,1,0:T(8,128)(2,1)S(1)} async-done(((bf16[8,3,128,256]{3,2,1,0:T(8,128)(2,1)}), bf16[8,3,128,256]{3,2,1,0:T(8,128)(2,1)S(1)}, u32[]{:S(2)}, u32[]{:S(2)}) %all-to-all-start.4) | async-done | bytes 1572896 | tf_op jit(solution)/shard_map/all_to_all | solution.py:210
  151.3 1.3 shard_map.85
  (31 shorter events, 8.0 us)
Async XLA Ops:
  0.6 21.8 %copy-start.2 = (s32[16,16]{1,0:T(8,128)S(1)}, s32[16,16]{1,0:T(8,128)}, u32[]{:S(2)}) copy-start(s32[16,16]{1,0:T(8,128)} %param.9) | copy-start | bytes 3076
  2.5 16.4 %all-to-all-start = ((s32[16,1,128]{2,1,0:T(1,128)}), s32[16,1,128]{2,1,0:T(1,128)S(1)}, u32[]{:S(2)}, u32[]{:S(2)}) async-start(s32[16,1,128]{2,1,0:T(1,128)} %broadcast_in_dim.45), calls=%async_computation | async-start | bytes 16384 | tf_op jit(solution)/shard_map/all_to_all | solution.py:210
  18.9 0.6 copy-start.1
  22.8 22.1 %all-to-all-start.1 = ((bf16[16,128,256]{2,1,0:T(8,128)(2,1)}), bf16[16,128,256]{2,1,0:T(8,128)(2,1)}, u32[]{:S(2)}, u32[]{:S(2)}) async-start(bf16[16,128,256]{2,1,0:T(8,128)(2,1)} %get-tuple-element.56), calls=%async_computation.1 | async-start | bytes 2097152 | tf_op jit(solution)/shard_map/all_to_all | solution.py:210
  55.1 22.4 %all-to-all-start.2 = ((bf16[16,128,256]{2,1,0:T(8,128)(2,1)}), bf16[16,128,256]{2,1,0:T(8,128)(2,1)}, u32[]{:S(2)}, u32[]{:S(2)}) async-start(bf16[16,128,256]{2,1,0:T(8,128)(2,1)} %get-tuple-element.58), calls=%async_computation.2 | async-start | bytes 2097152 | tf_op jit(solution)/shard_map/all_to_all | solution.py:210
  86.8 34.9 %all-to-all-start.3 = ((bf16[16,128,256]{2,1,0:T(8,128)(2,1)}), bf16[16,128,256]{2,1,0:T(8,128)(2,1)}, u32[]{:S(2)}, u32[]{:S(2)}) async-start(bf16[16,128,256]{2,1,0:T(8,128)(2,1)} %get-tuple-element.86), calls=%async_computation.3 | async-start | bytes 2097152 | tf_op jit(solution)/shard_map/all_to_all | solution.py:210
  95.2 6.6 %collective-permute-start = (bf16[3,128,256]{2,1,0:T(8,128)(2,1)}, bf16[3,128,256]{2,1,0:T(8,128)(2,1)S(1)}, u32[]{:S(2)}, u32[]{:S(2)}) collective-permute-start(bf16[3,128,256]{2,1,0:T(8,128)(2,1)} %get-tuple-element.76), channel_id=1, source_target_pairs={{0,1},{1,0},{2,3},{3,2},{4,5},{5,4},{6,7},{7,6},{8,9},{9,8},{10,11... | collective-permute-start | bytes 589832 | tf_op jit(solution)/shard_map/ppermute | solution.py:378
  96.5 11.6 %collective-permute-start.1 = (bf16[3,128,256]{2,1,0:T(8,128)(2,1)}, bf16[3,128,256]{2,1,0:T(8,128)(2,1)S(1)}, u32[]{:S(2)}, u32[]{:S(2)}) collective-permute-start(bf16[3,128,256]{2,1,0:T(8,128)(2,1)} %get-tuple-element.77), channel_id=1, source_target_pairs={{0,2},{1,3},{2,0},{3,1},{4,6},{5,7},{6,4},{7,5},{8,10},{9,11},{10,... | collective-permute-start | bytes 589832 | tf_op jit(solution)/shard_map/ppermute | solution.py:378
  99.0 16.6 %collective-permute-start.2 = (bf16[3,128,256]{2,1,0:T(8,128)(2,1)}, bf16[3,128,256]{2,1,0:T(8,128)(2,1)S(1)}, u32[]{:S(2)}, u32[]{:S(2)}) collective-permute-start(bf16[3,128,256]{2,1,0:T(8,128)(2,1)} %get-tuple-element.78), channel_id=1, source_target_pairs={{0,3},{1,2},{2,1},{3,0},{4,7},{5,6},{6,5},{7,4},{8,11},{9,10},{10,... | collective-permute-start | bytes 589832 | tf_op jit(solution)/shard_map/ppermute | solution.py:378
  99.2 22.5 %collective-permute-start.3 = (bf16[3,128,256]{2,1,0:T(8,128)(2,1)}, bf16[3,128,256]{2,1,0:T(8,128)(2,1)S(1)}, u32[]{:S(2)}, u32[]{:S(2)}) collective-permute-start(bf16[3,128,256]{2,1,0:T(8,128)(2,1)} %get-tuple-element.79), channel_id=1, source_target_pairs={{0,4},{1,5},{2,6},{3,7},{4,0},{5,1},{6,2},{7,3},{8,12},{9,13},{10,... | collective-permute-start | bytes 589832 | tf_op jit(solution)/shard_map/ppermute | solution.py:378
  99.6 22.1 %collective-permute-start.4 = (bf16[3,128,256]{2,1,0:T(8,128)(2,1)}, bf16[3,128,256]{2,1,0:T(8,128)(2,1)S(1)}, u32[]{:S(2)}, u32[]{:S(2)}) collective-permute-start(bf16[3,128,256]{2,1,0:T(8,128)(2,1)} %get-tuple-element.80), channel_id=1, source_target_pairs={{0,5},{1,4},{2,7},{3,6},{4,1},{5,0},{6,3},{7,2},{8,13},{9,12},{10,... | collective-permute-start | bytes 589832 | tf_op jit(solution)/shard_map/ppermute | solution.py:378
  101.8 19.9 %collective-permute-start.5 = (bf16[3,128,256]{2,1,0:T(8,128)(2,1)}, bf16[3,128,256]{2,1,0:T(8,128)(2,1)}, u32[]{:S(2)}, u32[]{:S(2)}) collective-permute-start(bf16[3,128,256]{2,1,0:T(8,128)(2,1)} %get-tuple-element.81), channel_id=1, source_target_pairs={{0,6},{1,7},{2,4},{3,5},{4,2},{5,3},{6,0},{7,1},{8,14},{9,15},{10,... | collective-permute-start | bytes 589832 | tf_op jit(solution)/shard_map/ppermute | solution.py:378
  108.1 13.6 %collective-permute-start.6 = (bf16[3,128,256]{2,1,0:T(8,128)(2,1)}, bf16[3,128,256]{2,1,0:T(8,128)(2,1)}, u32[]{:S(2)}, u32[]{:S(2)}) collective-permute-start(bf16[3,128,256]{2,1,0:T(8,128)(2,1)} %get-tuple-element.82), channel_id=1, source_target_pairs={{0,7},{1,6},{2,5},{3,4},{4,3},{5,2},{6,1},{7,0},{8,15},{9,14},{10,... | collective-permute-start | bytes 589832 | tf_op jit(solution)/shard_map/ppermute | solution.py:378
  125.0 4.9 %copy-start = (bf16[3,128,256]{2,1,0:T(8,128)(2,1)S(1)}, bf16[3,128,256]{2,1,0:T(8,128)(2,1)}, u32[]{:S(2)}) copy-start(bf16[3,128,256]{2,1,0:T(8,128)(2,1)} %get-tuple-element.87.refs_1_) | copy-start | bytes 589828
  125.0 26.3 %all-to-all-start.4 = ((bf16[8,3,128,256]{3,2,1,0:T(8,128)(2,1)}), bf16[8,3,128,256]{3,2,1,0:T(8,128)(2,1)S(1)}, u32[]{:S(2)}, u32[]{:S(2)}) async-start(bf16[8,3,128,256]{3,2,1,0:T(8,128)(2,1)} %shard_map.83), calls=%async_computation.4 | async-start | bytes 3145728 | tf_op jit(solution)/shard_map/all_to_all | solution.py:210

commit v4 on v3

--- a/solution.py
+++ b/solution.py
@@ -14,6 +14,8 @@
 MASKED = -1e30
 HALVES = 2
 LIMIT = 63
+KEY_TILE = 320
+SAFE_EXPONENT = 64.0
 F32 = jnp.float32
 BF16 = jnp.bfloat16
 
@@ -62,31 +64,71 @@
         stat_ref[0, 0:1, rows] = top
         stat_ref[0, 1:2, rows] = jnp.sum(e, axis=0, keepdims=True)
         stat_ref[0, 2:3, rows] = jnp.sum(e * dp, axis=0, keepdims=True)
+        q = q_ref[rows, :].astype(F32)
+        square = mm(jnp.ones((8, HDIM), BF16), (q * q).astype(BF16), NT)[0:1]
+        stat_ref[0, 3:4, rows] = jnp.sqrt(square) * (1.02 * EXP_SCALE)
 
 
 def remote_kernel(here_ref, q_ref, do_ref, k_ref, v_ref, bias_ref, stat_ref, *refs):
-    *next_ref, dq_ref, grad_ref, full_ref = refs
+    *next_ref, dq_ref, grad_ref, full_ref, e_buf, dp_buf = refs
     slots = k_ref.shape[0] - 1
     keys = slots * BLOCK
     k = k_ref[0:slots].reshape(keys, HDIM)
-    v = v_ref[0:slots].reshape(keys, HDIM)
     q = q_ref[...]
     do = do_ref[...]
-    s = add_bias(mm(k, q, NT), bias_ref[0:slots, :])
-    dp = mm(v, do, NT)
     top_loc = stat_ref[0, 0:1, :]
-    top = jnp.maximum(jnp.max(s, axis=0, keepdims=True) * EXP_SCALE, top_loc)
-    e = jnp.exp2(s * EXP_SCALE - top)
-    keep = jnp.exp2(top_loc - top)
-    total = stat_ref[0, 1:2, :] * keep + jnp.sum(e, axis=0, keepdims=True)
-    dot = stat_ref[0, 2:3, :] * keep + jnp.sum(e * dp, axis=0, keepdims=True)
-    inv = 1.0 / total
-    delta = dot * inv
-    full_ref[0, 0:1, :] = top
-    full_ref[0, 1:2, :] = inv
-    full_ref[0, 2:3, :] = delta
-    p = e * inv
-    ds = (p * (dp - delta)).astype(BF16)
+    total_loc = stat_ref[0, 1:2, :]
+    dot_loc = stat_ref[0, 2:3, :]
+
+    def tiles():
+        per_tile = KEY_TILE // BLOCK
+        for tile in range(keys // KEY_TILE):
+            at = pl.ds(tile * per_tile, per_tile)
+            k_t = k_ref[at].reshape(KEY_TILE, HDIM)
+            v_t = v_ref[at].reshape(KEY_TILE, HDIM)
+            yield pl.ds(tile * KEY_TILE, KEY_TILE), at, mm(k_t, q, NT), mm(v_t, do, NT)
+
+    def store(top, total, dot):
+        inv = 1.0 / total
+        full_ref[0, 0:1, :] = top
+        full_ref[0, 1:2, :] = inv
+        full_ref[0, 2:3, :] = dot * inv
+
+    k32 = k.astype(F32)
+    length = jnp.sum(k32 * k32, axis=1, keepdims=True)
+    in_use = lax.broadcasted_iota(jnp.int32, length.shape, 0) < here_ref[0] * BLOCK
+    longest = jnp.sqrt(jnp.max(jnp.where(in_use, length, 0.0), axis=0, keepdims=True))
+    excess = jnp.max(stat_ref[0, 3:4, :] * longest - top_loc)
+
+    @pl.when(excess < SAFE_EXPONENT)
+    def _():
+        total = total_loc
+        dot = dot_loc
+        for rows, at, s, dp in tiles():
+            e = jnp.exp2(add_bias(s * EXP_SCALE, bias_ref[at, :] - top_loc))
+            e_buf[rows, :] = e
+            dp_buf[rows, :] = dp
+            total += jnp.sum(e, axis=0, keepdims=True)
+            dot += jnp.sum(e * dp, axis=0, keepdims=True)
+        store(top_loc, total, dot)
+
+    @pl.when(jnp.logical_not(excess < SAFE_EXPONENT))
+    def _():
+        top = top_loc
+        for rows, at, s, dp in tiles():
+            s = add_bias(s, bias_ref[at, :])
+            e_buf[rows, :] = s
+            dp_buf[rows, :] = dp
+            top = jnp.maximum(top, jnp.max(s, axis=0, keepdims=True) * EXP_SCALE)
+        e = jnp.exp2(e_buf[...] * EXP_SCALE - top)
+        e_buf[...] = e
+        keep = jnp.exp2(top_loc - top)
+        total = total_loc * keep + jnp.sum(e, axis=0, keepdims=True)
+        dot = dot_loc * keep + jnp.sum(e * dp_buf[...], axis=0, keepdims=True)
+        store(top, total, dot)
+
+    p = e_buf[...] * full_ref[0, 1:2, :]
+    ds = (p * (dp_buf[...] - full_ref[0, 2:3, :])).astype(BF16)
     dq_ref[0] = mm(k.T, ds, NN)
     dk = mm(ds, q, NN) * SCALE
     dv = mm(p.astype(BF16), do, NN)
@@ -130,14 +172,11 @@
     dv_ref[...] = dv_acc[...]
 
 
-def gather_kernel(asks_ref, k_ref, v_ref, *out_refs):
-    for slot in range(out_refs[0].shape[0]):
+def gather_kernel(asks_ref, k_ref, v_ref, out_ref):
+    for slot in range(out_ref.shape[0]):
         rows = pl.ds(pl.multiple_of(asks_ref[slot, 0] * BLOCK, BLOCK), BLOCK)
-        for half, out_ref in enumerate(out_refs):
-            width = out_ref.shape[2]
-            cols = pl.ds(half * width, width)
-            out_ref[slot, 0:BLOCK, :] = k_ref[rows, cols]
-            out_ref[slot, BLOCK:, :] = v_ref[rows, cols]
+        out_ref[slot, 0:BLOCK, :] = k_ref[rows, :]
+        out_ref[slot, BLOCK:, :] = v_ref[rows, :]
 
 
 def add_back(here_ref, asks_ref, dk_ref, dv_ref, back_ref, acc):
@@ -226,9 +265,11 @@
     local_blk = jnp.where(usable, selected % per_dev, 0)
     from_range = owner[None] == ids[:, None, None]
     wanted = jnp.max(jnp.where(from_range, local_blk[None], 0), axis=(1, 2))
+    me = lax.axis_index("head")
+    wanted, here, me = lax.optimization_barrier((wanted, here, me))
     asks = swap(jnp.broadcast_to(wanted[:, None], (ranges, HDIM)), "ctx")
     here_arr = here.astype(jnp.int32).reshape(1)
-    me_arr = lax.axis_index("head").astype(jnp.int32).reshape(1)
+    me_arr = me.astype(jnp.int32).reshape(1)
 
     vmem = pl.BlockSpec(memory_space=pltpu.VMEM)
     smem = pl.BlockSpec(memory_space=pltpu.SMEM)
@@ -244,14 +285,18 @@
     )
     slots_half = jax.ShapeDtypeStruct((ranges, 2 * BLOCK, half_width), BF16)
 
-    sent = pl.pallas_call(
-        gather_kernel,
-        in_specs=[smem, vmem, vmem],
-        out_specs=[vmem] * HALVES,
-        out_shape=[slots_half] * HALVES,
-        compiler_params=params(),
-    )(asks, key_states, value_states)
-    selected, here, sent = lax.optimization_barrier((selected, here, sent))
+    def gather(half, asks):
+        return pl.pallas_call(
+            gather_kernel,
+            grid=(half_heads,),
+            in_specs=[smem] + [cols_at(half * half_heads)] * 2,
+            out_specs=slot_cols,
+            out_shape=slots_half,
+            compiler_params=params(),
+        )(asks, key_states, value_states)
+
+    sent = gather(0, asks)
+    selected, here, asks, sent = lax.optimization_barrier((selected, here, asks, sent))
     owner = jnp.where(selected >= 0, selected // per_dev, -1)
     from_range = owner[None] == ids[:, None, None]
     blocks = jnp.arange(per_dev, dtype=jnp.int32)
@@ -260,7 +305,8 @@
     bias = jnp.where(jnp.concatenate([has_local, has_remote], axis=0), 0.0, MASKED).astype(F32)
     bias = jnp.repeat(bias, BLOCK, axis=1)
     bias_local, bias_remote = bias[:per_dev], bias[per_dev:]
-    got = swap(sent[0], "ctx")
+    got = swap(sent, "ctx")
+    ahead = gather(1, asks)
     stats = pl.pallas_call(
         local_stats_kernel,
         grid=(heads,),
@@ -292,6 +338,7 @@
                 slots_half,
                 jax.ShapeDtypeStruct((half_heads, 8, tokens), F32),
             ],
+            scratch_shapes=[pltpu.VMEM(((ranges - 1) * BLOCK, tokens), F32)] * 2,
             compiler_params=params(),
             cost_estimate=cost(5, 8),
         )(here_arr, queries, out_grad, got, got, bias_remote, stats, *ahead)
@@ -366,7 +413,7 @@
             compiler_params=params(16),
         )(theirs, *outs)
 
-    dq0, both, full0 = remote(0, got, sent[1:])
+    dq0, both, full0 = remote(0, got, [ahead])
     both = swap(both, "ctx")
     own0 = local(0, full0, dq0)
     both, own0 = lax.optimization_barrier((both, own0))

time: 154 us -> 151 us (0.981)
  blocking collectives: 0 us -> 16.4 us
  waiting for transfers between devices: 55.1 us -> 46.1 us
  starting transfers between devices: 37.7 us -> 28.9 us
    all_to_all x0 -> x1, blocking collectives: none -> 16.4 us  [swap(): return lax.all_to_all(array, axis, split_axis=0, concat_axis=0, tiled=True)]
    all_to_all x5 -> x4, waiting for transfers between devices: 44.1 us -> 35 us  [swap(): return lax.all_to_all(array, axis, split_axis=0, concat_axis=0, tiled=True)]
    all_to_all x5 -> x4, starting transfers between devices: 29.3 us -> 20.4 us  [swap(): return lax.all_to_all(array, axis, split_axis=0, concat_axis=0, tiled=True)]
    pallas_call x1 -> x2, Pallas kernels: 3 us -> 4.12 us  [gather(): pl.pallas_call(gather_kernel, grid=(half_heads,), in_specs=[smem] + [cols...]
  transfers between devices with their start and end apart: 12 -> 11, of which waited for: 7 -> 6; matrix products, arithmetic and copies ran while one was open for 1% -> 1% of each run, Pallas kernels for 18% -> 19%
where the time goes in v4:
time: 151 us; the launch traced here: 150 us
  Pallas kernels  54.6 us (36%)
  waiting for transfers between devices  46.1 us (31%)
  starting transfers between devices  28.9 us (19%)
  blocking collectives  16.4 us (11%)
  other arithmetic  1.97 us (1%)
  local copies, waits for them, and re-layouts  1.71 us (1%)
    all_to_all x4, waiting for transfers between devices, swap(): return lax.all_to_all(array, axis, split_axis=0, concat_axis=0, tiled=True)  35 us
    all_to_all x4, starting transfers between devices, swap(): return lax.all_to_all(array, axis, split_axis=0, concat_axis=0, tiled=True)  20.4 us
    pallas_call x2, Pallas kernels, remote(): pl.pallas_call(remote_kernel, grid=(half_heads,), in_specs=[smem, cols_at...  18.6 us
    all_to_all x1, blocking collectives, swap(): return lax.all_to_all(array, axis, split_axis=0, concat_axis=0, tiled=True)  16.4 us
    pallas_call x2, Pallas kernels, local(): pl.pallas_call(local_grads_kernel, grid=(half_heads,), in_specs=[cols_at(...  14.2 us
    ppermute x7, waiting for transfers between devices, per_device(): lax.ppermute(pieces[d], 'head', [(i, i ^ d) for i in range(members)])  11.1 us
    ppermute x7, starting transfers between devices, per_device(): lax.ppermute(pieces[d], 'head', [(i, i ^ d) for i in range(members)])  8.48 us
    pallas_call x1, Pallas kernels, per_device(): pl.pallas_call(local_stats_kernel, grid=(heads,), in_specs=[cols_at(0)] *...  7.42 us
  transfers between devices with their start and end apart: 11, of which 6 were waited for; matrix products, arithmetic and copies ran while one was open for 1% of the time, Pallas kernels for 19%

profile of v4, /device:TPU:1, one launch (start us, length us, event | category | flops | bytes accessed | tf_op | source)
XLA Modules:
  0.0 150.5 jit_solution(7814383666226516384)
XLA Ops:
  1.8 16.4 %all_to_all.28 = s32[16,1,128]{2,1,0:T(1,128)} all-to-all(s32[16,1,128]{2,1,0:T(1,128)S(1)} %broadcast_in_dim.45), channel_id=1, replica_groups=mesh['ctx'=16,'head'=8] {'ctx'}, dimensions={0} | all-to-all | bytes 16384 | tf_op jit(solution)/shard_map/all_to_all | solution.py:249
  18.2 2.1 %shard_map.76 = bf16[16,128,256]{2,1,0:T(8,128)(2,1)} custom-call(s32[16,128]{1,0:T(8,128)} %bitcast.3, bf16[1024,512]{1,0:T(8,128)(2,1)} %k_ref.9, bf16[1024,512]{1,0:T(8,128)(2,1)} %v_ref.9), custom_call_target="tpu_custom_call" | custom-call | tf_op jit(solution)/shard_map/pallas_call | solution.py:289
  20.6 4.6 %all-to-all-start.1 = ((bf16[16,128,256]{2,1,0:T(8,128)(2,1)}), bf16[16,128,256]{2,1,0:T(8,128)(2,1)}, u32[]{:S(2)}, u32[]{:S(2)}) async-start(bf16[16,128,256]{2,1,0:T(8,128)(2,1)} %shard_map.76), calls=%async_computation.1 | async-start | bytes 2097152 | tf_op jit(solution)/shard_map/all_to_all | solution.py:249
  27.4 2.1 %shard_map.78.refs_0_ = bf16[16,128,256]{2,1,0:T(8,128)(2,1)} custom-call(s32[16,128]{1,0:T(8,128)} %bitcast.4, bf16[1024,512]{1,0:T(8,128)(2,1)} %k_ref.9, bf16[1024,512]{1,0:T(8,128)(2,1)} %v_ref.9), custom_call_target="tpu_custom_call" | custom-call | tf_op jit(solution)/shard_map/pallas_call | solution.py:289
  29.4 7.4 %shard_map.77.stat_ref = f32[4,8,1024]{2,1,0:T(8,128)} custom-call(bf16[1024,512]{1,0:T(8,128)(2,1)} %q_ref.9, bf16[1024,512]{1,0:T(8,128)(2,1)} %do_ref.9, bf16[1024,512]{1,0:T(8,128)(2,1)} %k_ref.9, bf16[1024,512]{1,0:T(8,128)(2,1)} %v_ref.9, f32[16,1024]{1,0:T(8,128)} %slice.15.bias_ref), custom_call_target="tpu_custom_call" | custom-call | flops 2147483648 | bytes 4194304 | tf_op jit(solution)/shard_map/pallas_call | solution.py:310
  36.9 5.7 %all-to-all-done.1.k_ref.v_ref = bf16[16,128,256]{2,1,0:T(8,128)(2,1)} async-done(((bf16[16,128,256]{2,1,0:T(8,128)(2,1)}), bf16[16,128,256]{2,1,0:T(8,128)(2,1)}, u32[]{:S(2)}, u32[]{:S(2)}) %all-to-all-start.1) | async-done | bytes 1048608 | tf_op jit(solution)/shard_map/all_to_all | solution.py:249
  42.6 9.6 %shard_map.79 = (f32[2,128,1024]{2,1,0:T(8,128)}, bf16[16,128,256]{2,1,0:T(8,128)(2,1)}, f32[2,8,1024]{2,1,0:T(8,128)}) custom-call(s32[1]{0:T(128)} %bitcast.here_ref, bf16[1024,512]{1,0:T(8,128)(2,1)} %q_ref.9, bf16[1024,512]{1,0:T(8,128)(2,1)} %do_ref.9, bf16[16,128,256]{2,1,0:T(8,128)(2,1)} %all-to-all-done.1.k_ref.v_ref, ...), custom_call_target="tpu_custom_call" | custom-call | flops 2684354560 | bytes 4194304 | tf_op jit(solution)/shard_map/pallas_call | solution.py:322
  52.2 5.5 %all-to-all-start.2 = ((bf16[16,128,256]{2,1,0:T(8,128)(2,1)}), bf16[16,128,256]{2,1,0:T(8,128)(2,1)}, u32[]{:S(2)}, u32[]{:S(2)}) async-start(bf16[16,128,256]{2,1,0:T(8,128)(2,1)} %get-tuple-element.59), calls=%async_computation.2 | async-start | bytes 2097152 | tf_op jit(solution)/shard_map/all_to_all | solution.py:249
  57.7 7.2 %shard_map.80 = (bf16[1024,256]{1,0:T(8,128)(2,1)}, f32[1024,256]{1,0:T(8,128)}, f32[1024,256]{1,0:T(8,128)}) custom-call(bf16[1024,512]{1,0:T(8,128)(2,1)} %q_ref.9, bf16[1024,512]{1,0:T(8,128)(2,1)} %do_ref.9, bf16[1024,512]{1,0:T(8,128)(2,1)} %k_ref.9, bf16[1024,512]{1,0:T(8,128)(2,1)} %v_ref.9, f32[16,1024]{1,0:T(8,128)} %slice.15.bias_ref, ...), custom_call_target="tpu_custom_call" | custom-call | flops 2684354560 | bytes 5242880 | tf_op jit(solution)/shard_map/pallas_call | solution.py:348
  64.8 10.1 %all-to-all-done.2.k_ref.v_ref.back_ref = bf16[16,128,256]{2,1,0:T(8,128)(2,1)} async-done(((bf16[16,128,256]{2,1,0:T(8,128)(2,1)}), bf16[16,128,256]{2,1,0:T(8,128)(2,1)}, u32[]{:S(2)}, u32[]{:S(2)}) %all-to-all-start.2) | async-done | bytes 1048608 | tf_op jit(solution)/shard_map/all_to_all | solution.py:249
  75.0 9.0 %shard_map.81 = (f32[2,128,1024]{2,1,0:T(8,128)}, bf16[16,128,256]{2,1,0:T(8,128)(2,1)}, f32[2,8,1024]{2,1,0:T(8,128)}) custom-call(s32[1]{0:T(128)} %bitcast.here_ref, bf16[1024,512]{1,0:T(8,128)(2,1)} %q_ref.9, bf16[1024,512]{1,0:T(8,128)(2,1)} %do_ref.9, bf16[16,128,256]{2,1,0:T(8,128)(2,1)} %all-to-all-done.2.k_ref.v_ref.back_ref, ...), custom_call_target="tpu_custom_call" | custom-call | flops 2684354560 | bytes 4194304 | tf_op jit(solution)/shard_map/pallas_call | solution.py:322
  84.0 5.5 %all-to-all-start.3 = ((bf16[16,128,256]{2,1,0:T(8,128)(2,1)}), bf16[16,128,256]{2,1,0:T(8,128)(2,1)}, u32[]{:S(2)}, u32[]{:S(2)}) async-start(bf16[16,128,256]{2,1,0:T(8,128)(2,1)} %get-tuple-element.88), calls=%async_computation.3 | async-start | bytes 2097152 | tf_op jit(solution)/shard_map/all_to_all | solution.py:249
  89.5 3.2 %shard_map.83 = (bf16[3,128,256]{2,1,0:T(8,128)(2,1)}, bf16[3,128,256]{2,1,0:T(8,128)(2,1)}, bf16[3,128,256]{2,1,0:T(8,128)(2,1)}, bf16[3,128,256]{2,1,0:T(8,128...) custom-call(s32[1]{0:T(128)} %bitcast.here_ref, ...), custom_call_target="tpu_custom_call" | custom-call | flops 1048576 | bytes 4194304 | tf_op jit(solution)/shard_map/pallas_call | solution.py:384
  94.0 2.4 %collective-permute-start.1 = (bf16[3,128,256]{2,1,0:T(8,128)(2,1)}, bf16[3,128,256]{2,1,0:T(8,128)(2,1)S(1)}, u32[]{:S(2)}, u32[]{:S(2)}) collective-permute-start(bf16[3,128,256]{2,1,0:T(8,128)(2,1)} %get-tuple-element.79), channel_id=1, source_target_pairs={{0,2},{1,3},{2,0},{3,1},{4,6},{5,7},{6,4},{7,5},{8,10},{9,11},{10,... | collective-permute-start | bytes 589832 | tf_op jit(solution)/shard_map/ppermute | solution.py:425
  97.8 1.6 %collective-permute-done.refs_2_ = bf16[3,128,256]{2,1,0:T(8,128)(2,1)S(1)} collective-permute-done((bf16[3,128,256]{2,1,0:T(8,128)(2,1)}, bf16[3,128,256]{2,1,0:T(8,128)(2,1)S(1)}, u32[]{:S(2)}, u32[]{:S(2)}) %collective-permute-start) | collective-permute-done | bytes 196640 | tf_op jit(solution)/shard_map/ppermute | solution.py:425
  99.4 3.0 %collective-permute-start.5 = (bf16[3,128,256]{2,1,0:T(8,128)(2,1)}, bf16[3,128,256]{2,1,0:T(8,128)(2,1)}, u32[]{:S(2)}, u32[]{:S(2)}) collective-permute-start(bf16[3,128,256]{2,1,0:T(8,128)(2,1)} %get-tuple-element.83), channel_id=1, source_target_pairs={{0,6},{1,7},{2,4},{3,5},{4,2},{5,3},{6,0},{7,1},{8,14},{9,15},{10,... | collective-permute-start | bytes 589832 | tf_op jit(solution)/shard_map/ppermute | solution.py:425
  102.4 3.4 %collective-permute-done.1.refs_3_ = bf16[3,128,256]{2,1,0:T(8,128)(2,1)S(1)} collective-permute-done((bf16[3,128,256]{2,1,0:T(8,128)(2,1)}, bf16[3,128,256]{2,1,0:T(8,128)(2,1)S(1)}, u32[]{:S(2)}, u32[]{:S(2)}) %collective-permute-start.1) | collective-permute-done | bytes 196640 | tf_op jit(solution)/shard_map/ppermute | solution.py:425
  106.2 7.0 %shard_map.82 = (bf16[1024,256]{1,0:T(8,128)(2,1)}, f32[1024,256]{1,0:T(8,128)}, f32[1024,256]{1,0:T(8,128)}) custom-call(bf16[1024,512]{1,0:T(8,128)(2,1)} %q_ref.9, bf16[1024,512]{1,0:T(8,128)(2,1)} %do_ref.9, bf16[1024,512]{1,0:T(8,128)(2,1)} %k_ref.9, bf16[1024,512]{1,0:T(8,128)(2,1)} %v_ref.9, f32[16,1024]{1,0:T(8,128)} %slice.15.bias_ref, ...), custom_call_target="tpu_custom_call" | custom-call | flops 2684354560 | bytes 5242880 | tf_op jit(solution)/shard_map/pallas_call | solution.py:348
  113.2 6.1 %collective-permute-done.3.refs_5_ = bf16[3,128,256]{2,1,0:T(8,128)(2,1)S(1)} collective-permute-done((bf16[3,128,256]{2,1,0:T(8,128)(2,1)}, bf16[3,128,256]{2,1,0:T(8,128)(2,1)S(1)}, u32[]{:S(2)}, u32[]{:S(2)}) %collective-permute-start.3) | collective-permute-done | bytes 196640 | tf_op jit(solution)/shard_map/ppermute | solution.py:425
  119.4 3.3 %shard_map.84 = bf16[8,3,128,256]{3,2,1,0:T(8,128)(2,1)} custom-call(s32[1]{0:T(128)} %bitcast.here_ref, s32[16,128]{1,0:T(8,128)} %bitcast.6, bf16[1024,256]{1,0:T(8,128)(2,1)} %get-tuple-element.85.dq_ref, f32[1024,256]{1,0:T(8,128)} %get-tuple-element.86.dk_ref, f32[1024,256]{1,0:T(8,128)} %get-tuple-element.87.dv_ref, ...), custom_call_target="tpu_custom_call" | custom-call | flops 1048576 | bytes 4194304 | tf_op jit(solution)/shard_map/pallas_call | solution.py:372
  122.7 4.9 %all-to-all-start.4 = ((bf16[8,3,128,256]{3,2,1,0:T(8,128)(2,1)}), bf16[8,3,128,256]{3,2,1,0:T(8,128)(2,1)S(1)}, u32[]{:S(2)}, u32[]{:S(2)}) async-start(bf16[8,3,128,256]{3,2,1,0:T(8,128)(2,1)} %shard_map.84), calls=%async_computation.4 | async-start | bytes 3145728 | tf_op jit(solution)/shard_map/all_to_all | solution.py:249
  127.5 2.4 %shard_map.85 = (bf16[128,4096]{1,0:T(8,128)(2,1)}, bf16[128,4096]{1,0:T(8,128)(2,1)}, bf16[128,4096]{1,0:T(8,128)(2,1)}) custom-call(s32[1]{0:T(128)} %bitcast.2.me_ref.refs_0_, bf16[3,128,256]{2,1,0:T(8,128)(2,1)S(1)} %copy-done, bf16[3,128,256]{2,1,0:T(8,128)(2,1)S(1)} %collective-permute-done.refs_2_, ...), custom_call_target="tpu_custom_call" | custom-call | tf_op jit(solution)/shard_map/pallas_call | solution.py:396
  129.9 19.1 %all-to-all-done.4.refs_0_ = bf16[8,3,128,256]{3,2,1,0:T(8,128)(2,1)S(1)} async-done(((bf16[8,3,128,256]{3,2,1,0:T(8,128)(2,1)}), bf16[8,3,128,256]{3,2,1,0:T(8,128)(2,1)S(1)}, u32[]{:S(2)}, u32[]{:S(2)}) %all-to-all-start.4) | async-done | bytes 1572896 | tf_op jit(solution)/shard_map/all_to_all | solution.py:249
  149.0 1.3 shard_map.86
  (29 shorter events, 6.8 us)
Async XLA Ops:
  18.2 2.1 %copy-start.1 = (s32[16,16]{1,0:T(8,128)S(1)}, s32[16,16]{1,0:T(8,128)}, u32[]{:S(2)}) copy-start(s32[16,16]{1,0:T(8,128)} %param.9) | copy-start | bytes 3076
  20.6 22.0 %all-to-all-start.1 = ((bf16[16,128,256]{2,1,0:T(8,128)(2,1)}), bf16[16,128,256]{2,1,0:T(8,128)(2,1)}, u32[]{:S(2)}, u32[]{:S(2)}) async-start(bf16[16,128,256]{2,1,0:T(8,128)(2,1)} %shard_map.76), calls=%async_computation.1 | async-start | bytes 2097152 | tf_op jit(solution)/shard_map/all_to_all | solution.py:249
  52.2 22.8 %all-to-all-start.2 = ((bf16[16,128,256]{2,1,0:T(8,128)(2,1)}), bf16[16,128,256]{2,1,0:T(8,128)(2,1)}, u32[]{:S(2)}, u32[]{:S(2)}) async-start(bf16[16,128,256]{2,1,0:T(8,128)(2,1)} %get-tuple-element.59), calls=%async_computation.2 | async-start | bytes 2097152 | tf_op jit(solution)/shard_map/all_to_all | solution.py:249
  84.0 35.3 %all-to-all-start.3 = ((bf16[16,128,256]{2,1,0:T(8,128)(2,1)}), bf16[16,128,256]{2,1,0:T(8,128)(2,1)}, u32[]{:S(2)}, u32[]{:S(2)}) async-start(bf16[16,128,256]{2,1,0:T(8,128)(2,1)} %get-tuple-element.88), calls=%async_computation.3 | async-start | bytes 2097152 | tf_op jit(solution)/shard_map/all_to_all | solution.py:249
  92.7 6.7 %collective-permute-start = (bf16[3,128,256]{2,1,0:T(8,128)(2,1)}, bf16[3,128,256]{2,1,0:T(8,128)(2,1)S(1)}, u32[]{:S(2)}, u32[]{:S(2)}) collective-permute-start(bf16[3,128,256]{2,1,0:T(8,128)(2,1)} %get-tuple-element.78), channel_id=1, source_target_pairs={{0,1},{1,0},{2,3},{3,2},{4,5},{5,4},{6,7},{7,6},{8,9},{9,8},{10,11... | collective-permute-start | bytes 589832 | tf_op jit(solution)/shard_map/ppermute | solution.py:425
  94.0 11.8 %collective-permute-start.1 = (bf16[3,128,256]{2,1,0:T(8,128)(2,1)}, bf16[3,128,256]{2,1,0:T(8,128)(2,1)S(1)}, u32[]{:S(2)}, u32[]{:S(2)}) collective-permute-start(bf16[3,128,256]{2,1,0:T(8,128)(2,1)} %get-tuple-element.79), channel_id=1, source_target_pairs={{0,2},{1,3},{2,0},{3,1},{4,6},{5,7},{6,4},{7,5},{8,10},{9,11},{10,... | collective-permute-start | bytes 589832 | tf_op jit(solution)/shard_map/ppermute | solution.py:425
  96.5 16.8 %collective-permute-start.2 = (bf16[3,128,256]{2,1,0:T(8,128)(2,1)}, bf16[3,128,256]{2,1,0:T(8,128)(2,1)S(1)}, u32[]{:S(2)}, u32[]{:S(2)}) collective-permute-start(bf16[3,128,256]{2,1,0:T(8,128)(2,1)} %get-tuple-element.80), channel_id=1, source_target_pairs={{0,3},{1,2},{2,1},{3,0},{4,7},{5,6},{6,5},{7,4},{8,11},{9,10},{10,... | collective-permute-start | bytes 589832 | tf_op jit(solution)/shard_map/ppermute | solution.py:425
  96.6 22.7 %collective-permute-start.3 = (bf16[3,128,256]{2,1,0:T(8,128)(2,1)}, bf16[3,128,256]{2,1,0:T(8,128)(2,1)S(1)}, u32[]{:S(2)}, u32[]{:S(2)}) collective-permute-start(bf16[3,128,256]{2,1,0:T(8,128)(2,1)} %get-tuple-element.81), channel_id=1, source_target_pairs={{0,4},{1,5},{2,6},{3,7},{4,0},{5,1},{6,2},{7,3},{8,12},{9,13},{10,... | collective-permute-start | bytes 589832 | tf_op jit(solution)/shard_map/ppermute | solution.py:425
  97.1 22.2 %collective-permute-start.4 = (bf16[3,128,256]{2,1,0:T(8,128)(2,1)}, bf16[3,128,256]{2,1,0:T(8,128)(2,1)S(1)}, u32[]{:S(2)}, u32[]{:S(2)}) collective-permute-start(bf16[3,128,256]{2,1,0:T(8,128)(2,1)} %get-tuple-element.82), channel_id=1, source_target_pairs={{0,5},{1,4},{2,7},{3,6},{4,1},{5,0},{6,3},{7,2},{8,13},{9,12},{10,... | collective-permute-start | bytes 589832 | tf_op jit(solution)/shard_map/ppermute | solution.py:425
  99.4 19.9 %collective-permute-start.5 = (bf16[3,128,256]{2,1,0:T(8,128)(2,1)}, bf16[3,128,256]{2,1,0:T(8,128)(2,1)}, u32[]{:S(2)}, u32[]{:S(2)}) collective-permute-start(bf16[3,128,256]{2,1,0:T(8,128)(2,1)} %get-tuple-element.83), channel_id=1, source_target_pairs={{0,6},{1,7},{2,4},{3,5},{4,2},{5,3},{6,0},{7,1},{8,14},{9,15},{10,... | collective-permute-start | bytes 589832 | tf_op jit(solution)/shard_map/ppermute | solution.py:425
  105.8 13.5 %collective-permute-start.6 = (bf16[3,128,256]{2,1,0:T(8,128)(2,1)}, bf16[3,128,256]{2,1,0:T(8,128)(2,1)}, u32[]{:S(2)}, u32[]{:S(2)}) collective-permute-start(bf16[3,128,256]{2,1,0:T(8,128)(2,1)} %get-tuple-element.84), channel_id=1, source_target_pairs={{0,7},{1,6},{2,5},{3,4},{4,3},{5,2},{6,1},{7,0},{8,15},{9,14},{10,... | collective-permute-start | bytes 589832 | tf_op jit(solution)/shard_map/ppermute | solution.py:425
  122.7 4.9 %copy-start = (bf16[3,128,256]{2,1,0:T(8,128)(2,1)S(1)}, bf16[3,128,256]{2,1,0:T(8,128)(2,1)}, u32[]{:S(2)}) copy-start(bf16[3,128,256]{2,1,0:T(8,128)(2,1)} %get-tuple-element.89.refs_1_) | copy-start | bytes 589828
  122.7 26.3 %all-to-all-start.4 = ((bf16[8,3,128,256]{3,2,1,0:T(8,128)(2,1)}), bf16[8,3,128,256]{3,2,1,0:T(8,128)(2,1)S(1)}, u32[]{:S(2)}, u32[]{:S(2)}) async-start(bf16[8,3,128,256]{3,2,1,0:T(8,128)(2,1)} %shard_map.84), calls=%async_computation.4 | async-start | bytes 3145728 | tf_op jit(solution)/shard_map/all_to_all | solution.py:249

commit v5 on v4

--- a/solution.py
+++ b/solution.py
@@ -14,7 +14,7 @@
 MASKED = -1e30
 HALVES = 2
 LIMIT = 63
-KEY_TILE = 320
+KEY_TILE = 960
 SAFE_EXPONENT = 64.0
 F32 = jnp.float32
 BF16 = jnp.bfloat16
@@ -168,8 +168,8 @@
             dv_acc[0:first, :] += dv[:first]
         dk_acc[rows, :] = dk[first:]
         dv_acc[rows, :] = dv[first:]
-    dk_ref[...] = dk_acc[...] * SCALE
-    dv_ref[...] = dv_acc[...]
+    dk_ref[...] = (dk_acc[...] * SCALE).astype(BF16)
+    dv_ref[...] = dv_acc[...].astype(BF16)
 
 
 def gather_kernel(asks_ref, k_ref, v_ref, out_ref):
@@ -180,8 +180,8 @@
 
 
 def add_back(here_ref, asks_ref, dk_ref, dv_ref, back_ref, acc):
-    acc[0] = dk_ref[...]
-    acc[1] = dv_ref[...]
+    acc[0] = dk_ref[...].astype(F32)
+    acc[1] = dv_ref[...].astype(F32)
     for slot in range(1, back_ref.shape[0]):
 
         @pl.when(slot > here_ref[0])
@@ -353,8 +353,8 @@
             out_specs=[cols_at(0)] * 3,
             out_shape=[
                 jax.ShapeDtypeStruct((tokens, half_width), BF16),
-                jax.ShapeDtypeStruct((tokens, half_width), F32),
-                jax.ShapeDtypeStruct((tokens, half_width), F32),
+                jax.ShapeDtypeStruct((tokens, half_width), BF16),
+                jax.ShapeDtypeStruct((tokens, half_width), BF16),
             ],
             scratch_shapes=[pltpu.VMEM((tokens, HDIM), F32)] * 2,
             compiler_params=params(),

time: 151 us -> 150 us (level)
  no operation moved by 1% of the time
where the time goes in v5:
time: 150 us; the launch traced here: 149 us
  Pallas kernels  53.7 us (36%)
  waiting for transfers between devices  46.6 us (31%)
  starting transfers between devices  27.9 us (19%)
  blocking collectives  16.4 us (11%)
  other arithmetic  1.97 us (1%)
  local copies, waits for them, and re-layouts  1.72 us (1%)
    all_to_all x4, waiting for transfers between devices, swap(): return lax.all_to_all(array, axis, split_axis=0, concat_axis=0, tiled=True)  35.2 us
    all_to_all x4, starting transfers between devices, swap(): return lax.all_to_all(array, axis, split_axis=0, concat_axis=0, tiled=True)  19.4 us
    pallas_call x2, Pallas kernels, remote(): pl.pallas_call(remote_kernel, grid=(half_heads,), in_specs=[smem, cols_at...  18.6 us
    all_to_all x1, blocking collectives, swap(): return lax.all_to_all(array, axis, split_axis=0, concat_axis=0, tiled=True)  16.4 us
    pallas_call x2, Pallas kernels, local(): pl.pallas_call(local_grads_kernel, grid=(half_heads,), in_specs=[cols_at(...  14 us
    ppermute x7, waiting for transfers between devices, per_device(): lax.ppermute(pieces[d], 'head', [(i, i ^ d) for i in range(members)])  11.4 us
    ppermute x7, starting transfers between devices, per_device(): lax.ppermute(pieces[d], 'head', [(i, i ^ d) for i in range(members)])  8.46 us
    pallas_call x1, Pallas kernels, per_device(): pl.pallas_call(local_stats_kernel, grid=(heads,), in_specs=[cols_at(0)] *...  7.42 us
  transfers between devices with their start and end apart: 11, of which 6 were waited for; matrix products, arithmetic and copies ran while one was open for 1% of the time, Pallas kernels for 19%

profile of v5, /device:TPU:1, one launch (start us, length us, event | category | flops | bytes accessed | tf_op | source)
XLA Modules:
  0.0 149.1 jit_solution(3504310797732818261)
XLA Ops:
  1.8 16.4 %all_to_all.28 = s32[16,1,128]{2,1,0:T(1,128)} all-to-all(s32[16,1,128]{2,1,0:T(1,128)S(1)} %broadcast_in_dim.45), channel_id=1, replica_groups=mesh['ctx'=16,'head'=8] {'ctx'}, dimensions={0} | all-to-all | bytes 16384 | tf_op jit(solution)/shard_map/all_to_all | solution.py:249
  18.2 2.1 %shard_map.76 = bf16[16,128,256]{2,1,0:T(8,128)(2,1)} custom-call(s32[16,128]{1,0:T(8,128)} %bitcast.3, bf16[1024,512]{1,0:T(8,128)(2,1)} %k_ref.9, bf16[1024,512]{1,0:T(8,128)(2,1)} %v_ref.9), custom_call_target="tpu_custom_call" | custom-call | tf_op jit(solution)/shard_map/pallas_call | solution.py:289
  20.6 4.6 %all-to-all-start.1 = ((bf16[16,128,256]{2,1,0:T(8,128)(2,1)}), bf16[16,128,256]{2,1,0:T(8,128)(2,1)}, u32[]{:S(2)}, u32[]{:S(2)}) async-start(bf16[16,128,256]{2,1,0:T(8,128)(2,1)} %shard_map.76), calls=%async_computation.1 | async-start | bytes 2097152 | tf_op jit(solution)/shard_map/all_to_all | solution.py:249
  27.4 2.1 %shard_map.78.refs_0_ = bf16[16,128,256]{2,1,0:T(8,128)(2,1)} custom-call(s32[16,128]{1,0:T(8,128)} %bitcast.4, bf16[1024,512]{1,0:T(8,128)(2,1)} %k_ref.9, bf16[1024,512]{1,0:T(8,128)(2,1)} %v_ref.9), custom_call_target="tpu_custom_call" | custom-call | tf_op jit(solution)/shard_map/pallas_call | solution.py:289
  29.5 7.4 %shard_map.77.stat_ref = f32[4,8,1024]{2,1,0:T(8,128)} custom-call(bf16[1024,512]{1,0:T(8,128)(2,1)} %q_ref.9, bf16[1024,512]{1,0:T(8,128)(2,1)} %do_ref.9, bf16[1024,512]{1,0:T(8,128)(2,1)} %k_ref.9, bf16[1024,512]{1,0:T(8,128)(2,1)} %v_ref.9, f32[16,1024]{1,0:T(8,128)} %slice.15.bias_ref), custom_call_target="tpu_custom_call" | custom-call | flops 2147483648 | bytes 4194304 | tf_op jit(solution)/shard_map/pallas_call | solution.py:310
  36.9 5.7 %all-to-all-done.1.k_ref.v_ref = bf16[16,128,256]{2,1,0:T(8,128)(2,1)} async-done(((bf16[16,128,256]{2,1,0:T(8,128)(2,1)}), bf16[16,128,256]{2,1,0:T(8,128)(2,1)}, u32[]{:S(2)}, u32[]{:S(2)}) %all-to-all-start.1) | async-done | bytes 1048608 | tf_op jit(solution)/shard_map/all_to_all | solution.py:249
  42.6 9.6 %shard_map.79 = (f32[2,128,1024]{2,1,0:T(8,128)}, bf16[16,128,256]{2,1,0:T(8,128)(2,1)}, f32[2,8,1024]{2,1,0:T(8,128)}) custom-call(s32[1]{0:T(128)} %bitcast.here_ref, bf16[1024,512]{1,0:T(8,128)(2,1)} %q_ref.9, bf16[1024,512]{1,0:T(8,128)(2,1)} %do_ref.9, bf16[16,128,256]{2,1,0:T(8,128)(2,1)} %all-to-all-done.1.k_ref.v_ref, ...), custom_call_target="tpu_custom_call" | custom-call | flops 2684354560 | bytes 4194304 | tf_op jit(solution)/shard_map/pallas_call | solution.py:322
  52.2 5.0 %all-to-all-start.2 = ((bf16[16,128,256]{2,1,0:T(8,128)(2,1)}), bf16[16,128,256]{2,1,0:T(8,128)(2,1)}, u32[]{:S(2)}, u32[]{:S(2)}) async-start(bf16[16,128,256]{2,1,0:T(8,128)(2,1)} %get-tuple-element.59), calls=%async_computation.2 | async-start | bytes 2097152 | tf_op jit(solution)/shard_map/all_to_all | solution.py:249
  57.2 7.0 %shard_map.80 = (bf16[1024,256]{1,0:T(8,128)(2,1)}, bf16[1024,256]{1,0:T(8,128)(2,1)}, bf16[1024,256]{1,0:T(8,128)(2,1)}) custom-call(bf16[1024,512]{1,0:T(8,128)(2,1)} %q_ref.9, bf16[1024,512]{1,0:T(8,128)(2,1)} %do_ref.9, bf16[1024,512]{1,0:T(8,128)(2,1)} %k_ref.9, bf16[1024,512]{1,0:T(8,128)(2,1)} %v_ref.9, f32[16,1024]{1,0:T(8,128)} %slice.15.bias_ref, ...), custom_call_target="tpu_custom_call" | custom-call | flops 2684354560 | bytes 5242880 | tf_op jit(solution)/shard_map/pallas_call | solution.py:348
  64.2 10.4 %all-to-all-done.2.k_ref.v_ref.back_ref = bf16[16,128,256]{2,1,0:T(8,128)(2,1)} async-done(((bf16[16,128,256]{2,1,0:T(8,128)(2,1)}), bf16[16,128,256]{2,1,0:T(8,128)(2,1)}, u32[]{:S(2)}, u32[]{:S(2)}) %all-to-all-start.2) | async-done | bytes 1048608 | tf_op jit(solution)/shard_map/all_to_all | solution.py:249
  74.6 9.0 %shard_map.81 = (f32[2,128,1024]{2,1,0:T(8,128)}, bf16[16,128,256]{2,1,0:T(8,128)(2,1)}, f32[2,8,1024]{2,1,0:T(8,128)}) custom-call(s32[1]{0:T(128)} %bitcast.here_ref, bf16[1024,512]{1,0:T(8,128)(2,1)} %q_ref.9, bf16[1024,512]{1,0:T(8,128)(2,1)} %do_ref.9, bf16[16,128,256]{2,1,0:T(8,128)(2,1)} %all-to-all-done.2.k_ref.v_ref.back_ref, ...), custom_call_target="tpu_custom_call" | custom-call | flops 2684354560 | bytes 4194304 | tf_op jit(solution)/shard_map/pallas_call | solution.py:322
  83.6 5.0 %all-to-all-start.3 = ((bf16[16,128,256]{2,1,0:T(8,128)(2,1)}), bf16[16,128,256]{2,1,0:T(8,128)(2,1)}, u32[]{:S(2)}, u32[]{:S(2)}) async-start(bf16[16,128,256]{2,1,0:T(8,128)(2,1)} %get-tuple-element.88), calls=%async_computation.3 | async-start | bytes 2097152 | tf_op jit(solution)/shard_map/all_to_all | solution.py:249
  88.6 2.9 %shard_map.83 = (bf16[3,128,256]{2,1,0:T(8,128)(2,1)}, bf16[3,128,256]{2,1,0:T(8,128)(2,1)}, bf16[3,128,256]{2,1,0:T(8,128)(2,1)}, bf16[3,128,256]{2,1,0:T(8,128...) custom-call(s32[1]{0:T(128)} %bitcast.here_ref, ...), custom_call_target="tpu_custom_call" | custom-call | flops 1048576 | bytes 4194304 | tf_op jit(solution)/shard_map/pallas_call | solution.py:384
  92.8 2.4 %collective-permute-start.1 = (bf16[3,128,256]{2,1,0:T(8,128)(2,1)}, bf16[3,128,256]{2,1,0:T(8,128)(2,1)S(1)}, u32[]{:S(2)}, u32[]{:S(2)}) collective-permute-start(bf16[3,128,256]{2,1,0:T(8,128)(2,1)} %get-tuple-element.79), channel_id=1, source_target_pairs={{0,2},{1,3},{2,0},{3,1},{4,6},{5,7},{6,4},{7,5},{8,10},{9,11},{10,... | collective-permute-start | bytes 589832 | tf_op jit(solution)/shard_map/ppermute | solution.py:425
  96.6 1.4 collective-permute-done.refs_2_
  98.1 2.9 %collective-permute-start.5 = (bf16[3,128,256]{2,1,0:T(8,128)(2,1)}, bf16[3,128,256]{2,1,0:T(8,128)(2,1)}, u32[]{:S(2)}, u32[]{:S(2)}) collective-permute-start(bf16[3,128,256]{2,1,0:T(8,128)(2,1)} %get-tuple-element.83), channel_id=1, source_target_pairs={{0,6},{1,7},{2,4},{3,5},{4,2},{5,3},{6,0},{7,1},{8,14},{9,15},{10,... | collective-permute-start | bytes 589832 | tf_op jit(solution)/shard_map/ppermute | solution.py:425
  101.0 3.4 %collective-permute-done.1.refs_3_ = bf16[3,128,256]{2,1,0:T(8,128)(2,1)S(1)} collective-permute-done((bf16[3,128,256]{2,1,0:T(8,128)(2,1)}, bf16[3,128,256]{2,1,0:T(8,128)(2,1)S(1)}, u32[]{:S(2)}, u32[]{:S(2)}) %collective-permute-start.1) | collective-permute-done | bytes 196640 | tf_op jit(solution)/shard_map/ppermute | solution.py:425
  104.8 6.9 %shard_map.82 = (bf16[1024,256]{1,0:T(8,128)(2,1)}, bf16[1024,256]{1,0:T(8,128)(2,1)}, bf16[1024,256]{1,0:T(8,128)(2,1)}) custom-call(bf16[1024,512]{1,0:T(8,128)(2,1)} %q_ref.9, bf16[1024,512]{1,0:T(8,128)(2,1)} %do_ref.9, bf16[1024,512]{1,0:T(8,128)(2,1)} %k_ref.9, bf16[1024,512]{1,0:T(8,128)(2,1)} %v_ref.9, f32[16,1024]{1,0:T(8,128)} %slice.15.bias_ref, ...), custom_call_target="tpu_custom_call" | custom-call | flops 2684354560 | bytes 5242880 | tf_op jit(solution)/shard_map/pallas_call | solution.py:348
  111.8 6.5 %collective-permute-done.3.refs_5_ = bf16[3,128,256]{2,1,0:T(8,128)(2,1)S(1)} collective-permute-done((bf16[3,128,256]{2,1,0:T(8,128)(2,1)}, bf16[3,128,256]{2,1,0:T(8,128)(2,1)S(1)}, u32[]{:S(2)}, u32[]{:S(2)}) %collective-permute-start.3) | collective-permute-done | bytes 196640 | tf_op jit(solution)/shard_map/ppermute | solution.py:425
  118.3 3.0 %shard_map.84 = bf16[8,3,128,256]{3,2,1,0:T(8,128)(2,1)} custom-call(s32[1]{0:T(128)} %bitcast.here_ref, s32[16,128]{1,0:T(8,128)} %bitcast.6, bf16[1024,256]{1,0:T(8,128)(2,1)} %get-tuple-element.85.dq_ref, bf16[1024,256]{1,0:T(8,128)(2,1)} %get-tuple-element.86.dk_ref, bf16[1024,256]{1,0:T(8,128)(2,1)} %get-tuple-element.87.dv_ref, ...), custom_call_target="tpu_custom_call" | custom-call | flops 1048576 | bytes 4194304 | tf_op jit(solution)/shard_map/pallas_call | solution.py:372
  121.3 4.9 %all-to-all-start.4 = ((bf16[8,3,128,256]{3,2,1,0:T(8,128)(2,1)}), bf16[8,3,128,256]{3,2,1,0:T(8,128)(2,1)S(1)}, u32[]{:S(2)}, u32[]{:S(2)}) async-start(bf16[8,3,128,256]{3,2,1,0:T(8,128)(2,1)} %shard_map.84), calls=%async_computation.4 | async-start | bytes 3145728 | tf_op jit(solution)/shard_map/all_to_all | solution.py:249
  126.2 2.4 %shard_map.85 = (bf16[128,4096]{1,0:T(8,128)(2,1)}, bf16[128,4096]{1,0:T(8,128)(2,1)}, bf16[128,4096]{1,0:T(8,128)(2,1)}) custom-call(s32[1]{0:T(128)} %bitcast.2.me_ref.refs_0_, bf16[3,128,256]{2,1,0:T(8,128)(2,1)S(1)} %copy-done, bf16[3,128,256]{2,1,0:T(8,128)(2,1)S(1)} %collective-permute-done.refs_2_, ...), custom_call_target="tpu_custom_call" | custom-call | tf_op jit(solution)/shard_map/pallas_call | solution.py:396
  128.5 19.1 %all-to-all-done.4.refs_0_ = bf16[8,3,128,256]{3,2,1,0:T(8,128)(2,1)S(1)} async-done(((bf16[8,3,128,256]{3,2,1,0:T(8,128)(2,1)}), bf16[8,3,128,256]{3,2,1,0:T(8,128)(2,1)S(1)}, u32[]{:S(2)}, u32[]{:S(2)}) %all-to-all-start.4) | async-done | bytes 1572896 | tf_op jit(solution)/shard_map/all_to_all | solution.py:249
  147.6 1.3 shard_map.86
  (29 shorter events, 6.8 us)
Async XLA Ops:
  18.2 2.1 %copy-start.1 = (s32[16,16]{1,0:T(8,128)S(1)}, s32[16,16]{1,0:T(8,128)}, u32[]{:S(2)}) copy-start(s32[16,16]{1,0:T(8,128)} %param.9) | copy-start | bytes 3076
  20.6 22.0 %all-to-all-start.1 = ((bf16[16,128,256]{2,1,0:T(8,128)(2,1)}), bf16[16,128,256]{2,1,0:T(8,128)(2,1)}, u32[]{:S(2)}, u32[]{:S(2)}) async-start(bf16[16,128,256]{2,1,0:T(8,128)(2,1)} %shard_map.76), calls=%async_computation.1 | async-start | bytes 2097152 | tf_op jit(solution)/shard_map/all_to_all | solution.py:249
  52.2 22.4 %all-to-all-start.2 = ((bf16[16,128,256]{2,1,0:T(8,128)(2,1)}), bf16[16,128,256]{2,1,0:T(8,128)(2,1)}, u32[]{:S(2)}, u32[]{:S(2)}) async-start(bf16[16,128,256]{2,1,0:T(8,128)(2,1)} %get-tuple-element.59), calls=%async_computation.2 | async-start | bytes 2097152 | tf_op jit(solution)/shard_map/all_to_all | solution.py:249
  83.6 34.7 %all-to-all-start.3 = ((bf16[16,128,256]{2,1,0:T(8,128)(2,1)}), bf16[16,128,256]{2,1,0:T(8,128)(2,1)}, u32[]{:S(2)}, u32[]{:S(2)}) async-start(bf16[16,128,256]{2,1,0:T(8,128)(2,1)} %get-tuple-element.88), calls=%async_computation.3 | async-start | bytes 2097152 | tf_op jit(solution)/shard_map/all_to_all | solution.py:249
  91.5 6.6 %collective-permute-start = (bf16[3,128,256]{2,1,0:T(8,128)(2,1)}, bf16[3,128,256]{2,1,0:T(8,128)(2,1)S(1)}, u32[]{:S(2)}, u32[]{:S(2)}) collective-permute-start(bf16[3,128,256]{2,1,0:T(8,128)(2,1)} %get-tuple-element.78), channel_id=1, source_target_pairs={{0,1},{1,0},{2,3},{3,2},{4,5},{5,4},{6,7},{7,6},{8,9},{9,8},{10,11... | collective-permute-start | bytes 589832 | tf_op jit(solution)/shard_map/ppermute | solution.py:425
  92.8 11.6 %collective-permute-start.1 = (bf16[3,128,256]{2,1,0:T(8,128)(2,1)}, bf16[3,128,256]{2,1,0:T(8,128)(2,1)S(1)}, u32[]{:S(2)}, u32[]{:S(2)}) collective-permute-start(bf16[3,128,256]{2,1,0:T(8,128)(2,1)} %get-tuple-element.79), channel_id=1, source_target_pairs={{0,2},{1,3},{2,0},{3,1},{4,6},{5,7},{6,4},{7,5},{8,10},{9,11},{10,... | collective-permute-start | bytes 589832 | tf_op jit(solution)/shard_map/ppermute | solution.py:425
  95.2 16.5 %collective-permute-start.2 = (bf16[3,128,256]{2,1,0:T(8,128)(2,1)}, bf16[3,128,256]{2,1,0:T(8,128)(2,1)S(1)}, u32[]{:S(2)}, u32[]{:S(2)}) collective-permute-start(bf16[3,128,256]{2,1,0:T(8,128)(2,1)} %get-tuple-element.80), channel_id=1, source_target_pairs={{0,3},{1,2},{2,1},{3,0},{4,7},{5,6},{6,5},{7,4},{8,11},{9,10},{10,... | collective-permute-start | bytes 589832 | tf_op jit(solution)/shard_map/ppermute | solution.py:425
  95.4 22.8 %collective-permute-start.3 = (bf16[3,128,256]{2,1,0:T(8,128)(2,1)}, bf16[3,128,256]{2,1,0:T(8,128)(2,1)S(1)}, u32[]{:S(2)}, u32[]{:S(2)}) collective-permute-start(bf16[3,128,256]{2,1,0:T(8,128)(2,1)} %get-tuple-element.81), channel_id=1, source_target_pairs={{0,4},{1,5},{2,6},{3,7},{4,0},{5,1},{6,2},{7,3},{8,12},{9,13},{10,... | collective-permute-start | bytes 589832 | tf_op jit(solution)/shard_map/ppermute | solution.py:425
  95.9 22.4 %collective-permute-start.4 = (bf16[3,128,256]{2,1,0:T(8,128)(2,1)}, bf16[3,128,256]{2,1,0:T(8,128)(2,1)S(1)}, u32[]{:S(2)}, u32[]{:S(2)}) collective-permute-start(bf16[3,128,256]{2,1,0:T(8,128)(2,1)} %get-tuple-element.82), channel_id=1, source_target_pairs={{0,5},{1,4},{2,7},{3,6},{4,1},{5,0},{6,3},{7,2},{8,13},{9,12},{10,... | collective-permute-start | bytes 589832 | tf_op jit(solution)/shard_map/ppermute | solution.py:425
  98.1 20.2 %collective-permute-start.5 = (bf16[3,128,256]{2,1,0:T(8,128)(2,1)}, bf16[3,128,256]{2,1,0:T(8,128)(2,1)}, u32[]{:S(2)}, u32[]{:S(2)}) collective-permute-start(bf16[3,128,256]{2,1,0:T(8,128)(2,1)} %get-tuple-element.83), channel_id=1, source_target_pairs={{0,6},{1,7},{2,4},{3,5},{4,2},{5,3},{6,0},{7,1},{8,14},{9,15},{10,... | collective-permute-start | bytes 589832 | tf_op jit(solution)/shard_map/ppermute | solution.py:425
  104.4 13.9 %collective-permute-start.6 = (bf16[3,128,256]{2,1,0:T(8,128)(2,1)}, bf16[3,128,256]{2,1,0:T(8,128)(2,1)}, u32[]{:S(2)}, u32[]{:S(2)}) collective-permute-start(bf16[3,128,256]{2,1,0:T(8,128)(2,1)} %get-tuple-element.84), channel_id=1, source_target_pairs={{0,7},{1,6},{2,5},{3,4},{4,3},{5,2},{6,1},{7,0},{8,15},{9,14},{10,... | collective-permute-start | bytes 589832 | tf_op jit(solution)/shard_map/ppermute | solution.py:425
  121.3 4.9 %copy-start = (bf16[3,128,256]{2,1,0:T(8,128)(2,1)S(1)}, bf16[3,128,256]{2,1,0:T(8,128)(2,1)}, u32[]{:S(2)}) copy-start(bf16[3,128,256]{2,1,0:T(8,128)(2,1)} %get-tuple-element.89.refs_1_) | copy-start | bytes 589828
  121.3 26.3 %all-to-all-start.4 = ((bf16[8,3,128,256]{3,2,1,0:T(8,128)(2,1)}), bf16[8,3,128,256]{3,2,1,0:T(8,128)(2,1)S(1)}, u32[]{:S(2)}, u32[]{:S(2)}) async-start(bf16[8,3,128,256]{3,2,1,0:T(8,128)(2,1)} %shard_map.84), calls=%async_computation.4 | async-start | bytes 3145728 | tf_op jit(solution)/shard_map/all_to_all | solution.py:249

commit v6 on v5

--- a/solution.py
+++ b/solution.py
@@ -296,7 +296,9 @@
         )(asks, key_states, value_states)
 
     sent = gather(0, asks)
-    selected, here, asks, sent = lax.optimization_barrier((selected, here, asks, sent))
+    asks, sent = lax.optimization_barrier((asks, sent))
+    ahead = gather(1, asks)
+    selected, here, ahead = lax.optimization_barrier((selected, here, ahead))
     owner = jnp.where(selected >= 0, selected // per_dev, -1)
     from_range = owner[None] == ids[:, None, None]
     blocks = jnp.arange(per_dev, dtype=jnp.int32)
@@ -306,7 +308,6 @@
     bias = jnp.repeat(bias, BLOCK, axis=1)
     bias_local, bias_remote = bias[:per_dev], bias[per_dev:]
     got = swap(sent, "ctx")
-    ahead = gather(1, asks)
     stats = pl.pallas_call(
         local_stats_kernel,
         grid=(heads,),

time: 150 us -> 149 us (level)
  transfers between devices with their start and end apart: 11 -> 11, of which waited for: 6 -> 6; matrix products, arithmetic and copies ran while one was open for 1% -> 2% of each run, Pallas kernels for 19% -> 19%
where the time goes in v6:
time: 149 us
  Pallas kernels  53.7 us (36%)
  waiting for transfers between devices  46.1 us (31%)
  starting transfers between devices  27.9 us (19%)
  blocking collectives  16.4 us (11%)
  other arithmetic  1.98 us (1%)
  local copies, waits for them, and re-layouts  1.72 us (1%)
    all_to_all x4, waiting for transfers between devices, swap(): return lax.all_to_all(array, axis, split_axis=0, concat_axis=0, tiled=True)  34.7 us
    all_to_all x4, starting transfers between devices, swap(): return lax.all_to_all(array, axis, split_axis=0, concat_axis=0, tiled=True)  19.4 us
    pallas_call x2, Pallas kernels, remote(): pl.pallas_call(remote_kernel, grid=(half_heads,), in_specs=[smem, cols_at...  18.6 us
    all_to_all x1, blocking collectives, swap(): return lax.all_to_all(array, axis, split_axis=0, concat_axis=0, tiled=True)  16.4 us
    pallas_call x2, Pallas kernels, local(): pl.pallas_call(local_grads_kernel, grid=(half_heads,), in_specs=[cols_at(...  14 us
    ppermute x7, waiting for transfers between devices, per_device(): lax.ppermute(pieces[d], 'head', [(i, i ^ d) for i in range(members)])  11.4 us
    ppermute x7, starting transfers between devices, per_device(): lax.ppermute(pieces[d], 'head', [(i, i ^ d) for i in range(members)])  8.45 us
    pallas_call x1, Pallas kernels, per_device(): pl.pallas_call(local_stats_kernel, grid=(heads,), in_specs=[cols_at(0)] *...  7.42 us
  transfers between devices with their start and end apart: 11, of which 6 were waited for; matrix products, arithmetic and copies ran while one was open for 2% of the time, Pallas kernels for 19%

profile of v6, /device:TPU:1, one launch (start us, length us, event | category | flops | bytes accessed | tf_op | source)
XLA Modules:
  0.0 148.7 jit_solution(16039050124190279519)
XLA Ops:
  1.8 16.4 %all_to_all.28 = s32[16,1,128]{2,1,0:T(1,128)} all-to-all(s32[16,1,128]{2,1,0:T(1,128)S(1)} %broadcast_in_dim.45), channel_id=1, replica_groups=mesh['ctx'=16,'head'=8] {'ctx'}, dimensions={0} | all-to-all | bytes 16384 | tf_op jit(solution)/shard_map/all_to_all | solution.py:249
  18.2 2.1 %shard_map.76 = bf16[16,128,256]{2,1,0:T(8,128)(2,1)} custom-call(s32[16,128]{1,0:T(8,128)} %bitcast.3, bf16[1024,512]{1,0:T(8,128)(2,1)} %k_ref.9, bf16[1024,512]{1,0:T(8,128)(2,1)} %v_ref.9), custom_call_target="tpu_custom_call" | custom-call | tf_op jit(solution)/shard_map/pallas_call | solution.py:289
  20.2 4.6 %all-to-all-start.1 = ((bf16[16,128,256]{2,1,0:T(8,128)(2,1)}), bf16[16,128,256]{2,1,0:T(8,128)(2,1)}, u32[]{:S(2)}, u32[]{:S(2)}) async-start(bf16[16,128,256]{2,1,0:T(8,128)(2,1)} %shard_map.76), calls=%async_computation.1 | async-start | bytes 2097152 | tf_op jit(solution)/shard_map/all_to_all | solution.py:249
  24.8 2.1 %shard_map.77.refs_0_ = bf16[16,128,256]{2,1,0:T(8,128)(2,1)} custom-call(s32[16,128]{1,0:T(8,128)} %bitcast.4, bf16[1024,512]{1,0:T(8,128)(2,1)} %k_ref.9, bf16[1024,512]{1,0:T(8,128)(2,1)} %v_ref.9), custom_call_target="tpu_custom_call" | custom-call | tf_op jit(solution)/shard_map/pallas_call | solution.py:289
  29.5 7.4 %shard_map.78.stat_ref = f32[4,8,1024]{2,1,0:T(8,128)} custom-call(bf16[1024,512]{1,0:T(8,128)(2,1)} %q_ref.9, bf16[1024,512]{1,0:T(8,128)(2,1)} %do_ref.9, bf16[1024,512]{1,0:T(8,128)(2,1)} %k_ref.9, bf16[1024,512]{1,0:T(8,128)(2,1)} %v_ref.9, f32[16,1024]{1,0:T(8,128)} %slice.15.bias_ref), custom_call_target="tpu_custom_call" | custom-call | flops 2147483648 | bytes 4194304 | tf_op jit(solution)/shard_map/pallas_call | solution.py:311
  36.9 5.3 %all-to-all-done.1.k_ref.v_ref = bf16[16,128,256]{2,1,0:T(8,128)(2,1)} async-done(((bf16[16,128,256]{2,1,0:T(8,128)(2,1)}), bf16[16,128,256]{2,1,0:T(8,128)(2,1)}, u32[]{:S(2)}, u32[]{:S(2)}) %all-to-all-start.1) | async-done | bytes 1048608 | tf_op jit(solution)/shard_map/all_to_all | solution.py:249
  42.2 9.6 %shard_map.79 = (f32[2,128,1024]{2,1,0:T(8,128)}, bf16[16,128,256]{2,1,0:T(8,128)(2,1)}, f32[2,8,1024]{2,1,0:T(8,128)}) custom-call(s32[1]{0:T(128)} %bitcast.here_ref, bf16[1024,512]{1,0:T(8,128)(2,1)} %q_ref.9, bf16[1024,512]{1,0:T(8,128)(2,1)} %do_ref.9, bf16[16,128,256]{2,1,0:T(8,128)(2,1)} %all-to-all-done.1.k_ref.v_ref, ...), custom_call_target="tpu_custom_call" | custom-call | flops 2684354560 | bytes 4194304 | tf_op jit(solution)/shard_map/pallas_call | solution.py:323
  51.8 5.0 %all-to-all-start.2 = ((bf16[16,128,256]{2,1,0:T(8,128)(2,1)}), bf16[16,128,256]{2,1,0:T(8,128)(2,1)}, u32[]{:S(2)}, u32[]{:S(2)}) async-start(bf16[16,128,256]{2,1,0:T(8,128)(2,1)} %get-tuple-element.61), calls=%async_computation.2 | async-start | bytes 2097152 | tf_op jit(solution)/shard_map/all_to_all | solution.py:249
  56.8 7.0 %shard_map.80 = (bf16[1024,256]{1,0:T(8,128)(2,1)}, bf16[1024,256]{1,0:T(8,128)(2,1)}, bf16[1024,256]{1,0:T(8,128)(2,1)}) custom-call(bf16[1024,512]{1,0:T(8,128)(2,1)} %q_ref.9, bf16[1024,512]{1,0:T(8,128)(2,1)} %do_ref.9, bf16[1024,512]{1,0:T(8,128)(2,1)} %k_ref.9, bf16[1024,512]{1,0:T(8,128)(2,1)} %v_ref.9, f32[16,1024]{1,0:T(8,128)} %slice.15.bias_ref, ...), custom_call_target="tpu_custom_call" | custom-call | flops 2684354560 | bytes 5242880 | tf_op jit(solution)/shard_map/pallas_call | solution.py:349
  63.8 10.4 %all-to-all-done.2.k_ref.v_ref.back_ref = bf16[16,128,256]{2,1,0:T(8,128)(2,1)} async-done(((bf16[16,128,256]{2,1,0:T(8,128)(2,1)}), bf16[16,128,256]{2,1,0:T(8,128)(2,1)}, u32[]{:S(2)}, u32[]{:S(2)}) %all-to-all-start.2) | async-done | bytes 1048608 | tf_op jit(solution)/shard_map/all_to_all | solution.py:249
  74.2 9.0 %shard_map.81 = (f32[2,128,1024]{2,1,0:T(8,128)}, bf16[16,128,256]{2,1,0:T(8,128)(2,1)}, f32[2,8,1024]{2,1,0:T(8,128)}) custom-call(s32[1]{0:T(128)} %bitcast.here_ref, bf16[1024,512]{1,0:T(8,128)(2,1)} %q_ref.9, bf16[1024,512]{1,0:T(8,128)(2,1)} %do_ref.9, bf16[16,128,256]{2,1,0:T(8,128)(2,1)} %all-to-all-done.2.k_ref.v_ref.back_ref, ...), custom_call_target="tpu_custom_call" | custom-call | flops 2684354560 | bytes 4194304 | tf_op jit(solution)/shard_map/pallas_call | solution.py:323
  83.2 5.0 %all-to-all-start.3 = ((bf16[16,128,256]{2,1,0:T(8,128)(2,1)}), bf16[16,128,256]{2,1,0:T(8,128)(2,1)}, u32[]{:S(2)}, u32[]{:S(2)}) async-start(bf16[16,128,256]{2,1,0:T(8,128)(2,1)} %get-tuple-element.90), calls=%async_computation.3 | async-start | bytes 2097152 | tf_op jit(solution)/shard_map/all_to_all | solution.py:249
  88.2 2.9 %shard_map.83 = (bf16[3,128,256]{2,1,0:T(8,128)(2,1)}, bf16[3,128,256]{2,1,0:T(8,128)(2,1)}, bf16[3,128,256]{2,1,0:T(8,128)(2,1)}, bf16[3,128,256]{2,1,0:T(8,128...) custom-call(s32[1]{0:T(128)} %bitcast.here_ref, ...), custom_call_target="tpu_custom_call" | custom-call | flops 1048576 | bytes 4194304 | tf_op jit(solution)/shard_map/pallas_call | solution.py:385
  92.4 2.4 %collective-permute-start.1 = (bf16[3,128,256]{2,1,0:T(8,128)(2,1)}, bf16[3,128,256]{2,1,0:T(8,128)(2,1)S(1)}, u32[]{:S(2)}, u32[]{:S(2)}) collective-permute-start(bf16[3,128,256]{2,1,0:T(8,128)(2,1)} %get-tuple-element.81), channel_id=1, source_target_pairs={{0,2},{1,3},{2,0},{3,1},{4,6},{5,7},{6,4},{7,5},{8,10},{9,11},{10,... | collective-permute-start | bytes 589832 | tf_op jit(solution)/shard_map/ppermute | solution.py:426
  96.2 1.5 collective-permute-done.refs_2_
  97.7 2.9 %collective-permute-start.5 = (bf16[3,128,256]{2,1,0:T(8,128)(2,1)}, bf16[3,128,256]{2,1,0:T(8,128)(2,1)}, u32[]{:S(2)}, u32[]{:S(2)}) collective-permute-start(bf16[3,128,256]{2,1,0:T(8,128)(2,1)} %get-tuple-element.85), channel_id=1, source_target_pairs={{0,6},{1,7},{2,4},{3,5},{4,2},{5,3},{6,0},{7,1},{8,14},{9,15},{10,... | collective-permute-start | bytes 589832 | tf_op jit(solution)/shard_map/ppermute | solution.py:426
  100.6 3.4 %collective-permute-done.1.refs_3_ = bf16[3,128,256]{2,1,0:T(8,128)(2,1)S(1)} collective-permute-done((bf16[3,128,256]{2,1,0:T(8,128)(2,1)}, bf16[3,128,256]{2,1,0:T(8,128)(2,1)S(1)}, u32[]{:S(2)}, u32[]{:S(2)}) %collective-permute-start.1) | collective-permute-done | bytes 196640 | tf_op jit(solution)/shard_map/ppermute | solution.py:426
  104.4 6.9 %shard_map.82 = (bf16[1024,256]{1,0:T(8,128)(2,1)}, bf16[1024,256]{1,0:T(8,128)(2,1)}, bf16[1024,256]{1,0:T(8,128)(2,1)}) custom-call(bf16[1024,512]{1,0:T(8,128)(2,1)} %q_ref.9, bf16[1024,512]{1,0:T(8,128)(2,1)} %do_ref.9, bf16[1024,512]{1,0:T(8,128)(2,1)} %k_ref.9, bf16[1024,512]{1,0:T(8,128)(2,1)} %v_ref.9, f32[16,1024]{1,0:T(8,128)} %slice.15.bias_ref, ...), custom_call_target="tpu_custom_call" | custom-call | flops 2684354560 | bytes 5242880 | tf_op jit(solution)/shard_map/pallas_call | solution.py:349
  111.4 6.5 %collective-permute-done.3.refs_5_ = bf16[3,128,256]{2,1,0:T(8,128)(2,1)S(1)} collective-permute-done((bf16[3,128,256]{2,1,0:T(8,128)(2,1)}, bf16[3,128,256]{2,1,0:T(8,128)(2,1)S(1)}, u32[]{:S(2)}, u32[]{:S(2)}) %collective-permute-start.3) | collective-permute-done | bytes 196640 | tf_op jit(solution)/shard_map/ppermute | solution.py:426
  117.9 3.0 %shard_map.84 = bf16[8,3,128,256]{3,2,1,0:T(8,128)(2,1)} custom-call(s32[1]{0:T(128)} %bitcast.here_ref, s32[16,128]{1,0:T(8,128)} %bitcast.6, bf16[1024,256]{1,0:T(8,128)(2,1)} %get-tuple-element.87.dq_ref, bf16[1024,256]{1,0:T(8,128)(2,1)} %get-tuple-element.88.dk_ref, bf16[1024,256]{1,0:T(8,128)(2,1)} %get-tuple-element.89.dv_ref, ...), custom_call_target="tpu_custom_call" | custom-call | flops 1048576 | bytes 4194304 | tf_op jit(solution)/shard_map/pallas_call | solution.py:373
  120.9 4.9 %all-to-all-start.4 = ((bf16[8,3,128,256]{3,2,1,0:T(8,128)(2,1)}), bf16[8,3,128,256]{3,2,1,0:T(8,128)(2,1)S(1)}, u32[]{:S(2)}, u32[]{:S(2)}) async-start(bf16[8,3,128,256]{3,2,1,0:T(8,128)(2,1)} %shard_map.84), calls=%async_computation.4 | async-start | bytes 3145728 | tf_op jit(solution)/shard_map/all_to_all | solution.py:249
  125.8 2.4 %shard_map.85 = (bf16[128,4096]{1,0:T(8,128)(2,1)}, bf16[128,4096]{1,0:T(8,128)(2,1)}, bf16[128,4096]{1,0:T(8,128)(2,1)}) custom-call(s32[1]{0:T(128)} %bitcast.2.me_ref.refs_0_, bf16[3,128,256]{2,1,0:T(8,128)(2,1)S(1)} %copy-done, bf16[3,128,256]{2,1,0:T(8,128)(2,1)S(1)} %collective-permute-done.refs_2_, ...), custom_call_target="tpu_custom_call" | custom-call | tf_op jit(solution)/shard_map/pallas_call | solution.py:397
  128.1 19.1 %all-to-all-done.4.refs_0_ = bf16[8,3,128,256]{3,2,1,0:T(8,128)(2,1)S(1)} async-done(((bf16[8,3,128,256]{3,2,1,0:T(8,128)(2,1)}), bf16[8,3,128,256]{3,2,1,0:T(8,128)(2,1)S(1)}, u32[]{:S(2)}, u32[]{:S(2)}) %all-to-all-start.4) | async-done | bytes 1572896 | tf_op jit(solution)/shard_map/all_to_all | solution.py:249
  147.2 1.3 shard_map.86
  (29 shorter events, 6.8 us)
Async XLA Ops:
  20.2 22.0 %all-to-all-start.1 = ((bf16[16,128,256]{2,1,0:T(8,128)(2,1)}), bf16[16,128,256]{2,1,0:T(8,128)(2,1)}, u32[]{:S(2)}, u32[]{:S(2)}) async-start(bf16[16,128,256]{2,1,0:T(8,128)(2,1)} %shard_map.76), calls=%async_computation.1 | async-start | bytes 2097152 | tf_op jit(solution)/shard_map/all_to_all | solution.py:249
  24.8 2.1 %copy-start.1 = (s32[16,16]{1,0:T(8,128)S(1)}, s32[16,16]{1,0:T(8,128)}, u32[]{:S(2)}) copy-start(s32[16,16]{1,0:T(8,128)} %param.9) | copy-start | bytes 3076
  51.8 22.4 %all-to-all-start.2 = ((bf16[16,128,256]{2,1,0:T(8,128)(2,1)}), bf16[16,128,256]{2,1,0:T(8,128)(2,1)}, u32[]{:S(2)}, u32[]{:S(2)}) async-start(bf16[16,128,256]{2,1,0:T(8,128)(2,1)} %get-tuple-element.61), calls=%async_computation.2 | async-start | bytes 2097152 | tf_op jit(solution)/shard_map/all_to_all | solution.py:249
  83.2 34.7 %all-to-all-start.3 = ((bf16[16,128,256]{2,1,0:T(8,128)(2,1)}), bf16[16,128,256]{2,1,0:T(8,128)(2,1)}, u32[]{:S(2)}, u32[]{:S(2)}) async-start(bf16[16,128,256]{2,1,0:T(8,128)(2,1)} %get-tuple-element.90), calls=%async_computation.3 | async-start | bytes 2097152 | tf_op jit(solution)/shard_map/all_to_all | solution.py:249
  91.1 6.6 %collective-permute-start = (bf16[3,128,256]{2,1,0:T(8,128)(2,1)}, bf16[3,128,256]{2,1,0:T(8,128)(2,1)S(1)}, u32[]{:S(2)}, u32[]{:S(2)}) collective-permute-start(bf16[3,128,256]{2,1,0:T(8,128)(2,1)} %get-tuple-element.80), channel_id=1, source_target_pairs={{0,1},{1,0},{2,3},{3,2},{4,5},{5,4},{6,7},{7,6},{8,9},{9,8},{10,11... | collective-permute-start | bytes 589832 | tf_op jit(solution)/shard_map/ppermute | solution.py:426
  92.4 11.6 %collective-permute-start.1 = (bf16[3,128,256]{2,1,0:T(8,128)(2,1)}, bf16[3,128,256]{2,1,0:T(8,128)(2,1)S(1)}, u32[]{:S(2)}, u32[]{:S(2)}) collective-permute-start(bf16[3,128,256]{2,1,0:T(8,128)(2,1)} %get-tuple-element.81), channel_id=1, source_target_pairs={{0,2},{1,3},{2,0},{3,1},{4,6},{5,7},{6,4},{7,5},{8,10},{9,11},{10,... | collective-permute-start | bytes 589832 | tf_op jit(solution)/shard_map/ppermute | solution.py:426
  94.8 16.5 %collective-permute-start.2 = (bf16[3,128,256]{2,1,0:T(8,128)(2,1)}, bf16[3,128,256]{2,1,0:T(8,128)(2,1)S(1)}, u32[]{:S(2)}, u32[]{:S(2)}) collective-permute-start(bf16[3,128,256]{2,1,0:T(8,128)(2,1)} %get-tuple-element.82), channel_id=1, source_target_pairs={{0,3},{1,2},{2,1},{3,0},{4,7},{5,6},{6,5},{7,4},{8,11},{9,10},{10,... | collective-permute-start | bytes 589832 | tf_op jit(solution)/shard_map/ppermute | solution.py:426
  95.1 22.8 %collective-permute-start.3 = (bf16[3,128,256]{2,1,0:T(8,128)(2,1)}, bf16[3,128,256]{2,1,0:T(8,128)(2,1)S(1)}, u32[]{:S(2)}, u32[]{:S(2)}) collective-permute-start(bf16[3,128,256]{2,1,0:T(8,128)(2,1)} %get-tuple-element.83), channel_id=1, source_target_pairs={{0,4},{1,5},{2,6},{3,7},{4,0},{5,1},{6,2},{7,3},{8,12},{9,13},{10,... | collective-permute-start | bytes 589832 | tf_op jit(solution)/shard_map/ppermute | solution.py:426
  95.5 22.4 %collective-permute-start.4 = (bf16[3,128,256]{2,1,0:T(8,128)(2,1)}, bf16[3,128,256]{2,1,0:T(8,128)(2,1)S(1)}, u32[]{:S(2)}, u32[]{:S(2)}) collective-permute-start(bf16[3,128,256]{2,1,0:T(8,128)(2,1)} %get-tuple-element.84), channel_id=1, source_target_pairs={{0,5},{1,4},{2,7},{3,6},{4,1},{5,0},{6,3},{7,2},{8,13},{9,12},{10,... | collective-permute-start | bytes 589832 | tf_op jit(solution)/shard_map/ppermute | solution.py:426
  97.7 20.2 %collective-permute-start.5 = (bf16[3,128,256]{2,1,0:T(8,128)(2,1)}, bf16[3,128,256]{2,1,0:T(8,128)(2,1)}, u32[]{:S(2)}, u32[]{:S(2)}) collective-permute-start(bf16[3,128,256]{2,1,0:T(8,128)(2,1)} %get-tuple-element.85), channel_id=1, source_target_pairs={{0,6},{1,7},{2,4},{3,5},{4,2},{5,3},{6,0},{7,1},{8,14},{9,15},{10,... | collective-permute-start | bytes 589832 | tf_op jit(solution)/shard_map/ppermute | solution.py:426
  104.0 13.9 %collective-permute-start.6 = (bf16[3,128,256]{2,1,0:T(8,128)(2,1)}, bf16[3,128,256]{2,1,0:T(8,128)(2,1)}, u32[]{:S(2)}, u32[]{:S(2)}) collective-permute-start(bf16[3,128,256]{2,1,0:T(8,128)(2,1)} %get-tuple-element.86), channel_id=1, source_target_pairs={{0,7},{1,6},{2,5},{3,4},{4,3},{5,2},{6,1},{7,0},{8,15},{9,14},{10,... | collective-permute-start | bytes 589832 | tf_op jit(solution)/shard_map/ppermute | solution.py:426
  120.9 4.9 %copy-start = (bf16[3,128,256]{2,1,0:T(8,128)(2,1)S(1)}, bf16[3,128,256]{2,1,0:T(8,128)(2,1)}, u32[]{:S(2)}) copy-start(bf16[3,128,256]{2,1,0:T(8,128)(2,1)} %get-tuple-element.91.refs_1_) | copy-start | bytes 589828
  120.9 26.3 %all-to-all-start.4 = ((bf16[8,3,128,256]{3,2,1,0:T(8,128)(2,1)}), bf16[8,3,128,256]{3,2,1,0:T(8,128)(2,1)S(1)}, u32[]{:S(2)}, u32[]{:S(2)}) async-start(bf16[8,3,128,256]{3,2,1,0:T(8,128)(2,1)} %shard_map.84), calls=%async_computation.4 | async-start | bytes 3145728 | tf_op jit(solution)/shard_map/all_to_all | solution.py:249

commit v7 on v6

--- a/solution.py
+++ b/solution.py
@@ -199,10 +199,14 @@
     out_ref[:, 2] = dq_ref[...].reshape(parts, per_part, HDIM)
 
 
+def partners(members):
+    return sorted(range(members), key=lambda d: (d >= members // 2, d % 4 == 2, d))
+
+
 def finish_pieces_kernel(here_ref, asks_ref, me_ref, dq_ref, dk_ref, dv_ref, back_ref, *refs):
     *piece_refs, acc = refs
     add_back(here_ref, asks_ref, dk_ref, dv_ref, back_ref, acc)
-    for d, piece_ref in enumerate(piece_refs):
+    for d, piece_ref in zip(partners(len(piece_refs)), piece_refs):
         size = piece_ref.shape[1]
         rows = pl.ds(pl.multiple_of((me_ref[0] ^ d) * size, size), size)
         for which in range(2):
@@ -230,7 +234,7 @@
     pieces, outs = refs[:-3], refs[-3:]
     width = pieces[0].shape[2]
     copies = []
-    for d, piece in enumerate(pieces):
+    for d, piece in zip(partners(len(pieces)), pieces):
         part = me_ref[0] ^ d
         for which, out in enumerate(outs):
             cols = pl.ds(pl.multiple_of((part * HALVES + half) * width, width), width)
@@ -422,8 +426,9 @@
     grads, both = lax.optimization_barrier((grads, both))
     back = swap(grads, "ctx")
     pieces = finish_pieces(both, own0)
-    pieces = [pieces[0]] + [
-        lax.ppermute(pieces[d], "head", [(i, i ^ d) for i in range(members)]) for d in range(1, members)
+    pieces = [
+        lax.ppermute(piece, "head", [(i, i ^ d) for i in range(members)]) if d else piece
+        for d, piece in zip(partners(members), pieces)
     ]
     own1 = local(1, full1, dq1)
     own1, pieces = lax.optimization_barrier((own1, pieces))

time: 149 us -> 149 us (level)
  no operation moved by 1% of the time
where the time goes in v7:
time: 149 us
  Pallas kernels  53.7 us (36%)
  waiting for transfers between devices  46.2 us (31%)
  starting transfers between devices  27.8 us (19%)
  blocking collectives  16.4 us (11%)
  other arithmetic  1.98 us (1%)
  local copies, waits for them, and re-layouts  1.72 us (1%)
    all_to_all x4, waiting for transfers between devices, swap(): return lax.all_to_all(array, axis, split_axis=0, concat_axis=0, tiled=True)  34.7 us
    all_to_all x4, starting transfers between devices, swap(): return lax.all_to_all(array, axis, split_axis=0, concat_axis=0, tiled=True)  19.4 us
    pallas_call x2, Pallas kernels, remote(): pl.pallas_call(remote_kernel, grid=(half_heads,), in_specs=[smem, cols_at...  18.6 us
    all_to_all x1, blocking collectives, swap(): return lax.all_to_all(array, axis, split_axis=0, concat_axis=0, tiled=True)  16.4 us
    pallas_call x2, Pallas kernels, local(): pl.pallas_call(local_grads_kernel, grid=(half_heads,), in_specs=[cols_at(...  14 us
    ppermute x7, waiting for transfers between devices, per_device(): lax.ppermute(piece, 'head', [(i, i ^ d) for i in range(members)])  11.4 us
    ppermute x7, starting transfers between devices, per_device(): lax.ppermute(piece, 'head', [(i, i ^ d) for i in range(members)])  8.39 us
    pallas_call x1, Pallas kernels, per_device(): pl.pallas_call(local_stats_kernel, grid=(heads,), in_specs=[cols_at(0)] *...  7.42 us
  transfers between devices with their start and end apart: 11, of which 6 were waited for; matrix products, arithmetic and copies ran while one was open for 2% of the time, Pallas kernels for 19%

profile of v7, /device:TPU:1, one launch (start us, length us, event | category | flops | bytes accessed | tf_op | source)
XLA Modules:
  0.0 148.7 jit_solution(3002876608699271203)
XLA Ops:
  1.8 16.4 %all_to_all.28 = s32[16,1,128]{2,1,0:T(1,128)} all-to-all(s32[16,1,128]{2,1,0:T(1,128)S(1)} %broadcast_in_dim.45), channel_id=1, replica_groups=mesh['ctx'=16,'head'=8] {'ctx'}, dimensions={0} | all-to-all | bytes 16384 | tf_op jit(solution)/shard_map/all_to_all | solution.py:253
  18.2 2.1 %shard_map.76 = bf16[16,128,256]{2,1,0:T(8,128)(2,1)} custom-call(s32[16,128]{1,0:T(8,128)} %bitcast.3, bf16[1024,512]{1,0:T(8,128)(2,1)} %k_ref.9, bf16[1024,512]{1,0:T(8,128)(2,1)} %v_ref.9), custom_call_target="tpu_custom_call" | custom-call | tf_op jit(solution)/shard_map/pallas_call | solution.py:293
  20.2 4.6 %all-to-all-start.1 = ((bf16[16,128,256]{2,1,0:T(8,128)(2,1)}), bf16[16,128,256]{2,1,0:T(8,128)(2,1)}, u32[]{:S(2)}, u32[]{:S(2)}) async-start(bf16[16,128,256]{2,1,0:T(8,128)(2,1)} %shard_map.76), calls=%async_computation.1 | async-start | bytes 2097152 | tf_op jit(solution)/shard_map/all_to_all | solution.py:253
  24.8 2.1 %shard_map.77.refs_0_ = bf16[16,128,256]{2,1,0:T(8,128)(2,1)} custom-call(s32[16,128]{1,0:T(8,128)} %bitcast.4, bf16[1024,512]{1,0:T(8,128)(2,1)} %k_ref.9, bf16[1024,512]{1,0:T(8,128)(2,1)} %v_ref.9), custom_call_target="tpu_custom_call" | custom-call | tf_op jit(solution)/shard_map/pallas_call | solution.py:293
  29.5 7.4 %shard_map.78.stat_ref = f32[4,8,1024]{2,1,0:T(8,128)} custom-call(bf16[1024,512]{1,0:T(8,128)(2,1)} %q_ref.9, bf16[1024,512]{1,0:T(8,128)(2,1)} %do_ref.9, bf16[1024,512]{1,0:T(8,128)(2,1)} %k_ref.9, bf16[1024,512]{1,0:T(8,128)(2,1)} %v_ref.9, f32[16,1024]{1,0:T(8,128)} %slice.15.bias_ref), custom_call_target="tpu_custom_call" | custom-call | flops 2147483648 | bytes 4194304 | tf_op jit(solution)/shard_map/pallas_call | solution.py:315
  36.9 5.3 %all-to-all-done.1.k_ref.v_ref = bf16[16,128,256]{2,1,0:T(8,128)(2,1)} async-done(((bf16[16,128,256]{2,1,0:T(8,128)(2,1)}), bf16[16,128,256]{2,1,0:T(8,128)(2,1)}, u32[]{:S(2)}, u32[]{:S(2)}) %all-to-all-start.1) | async-done | bytes 1048608 | tf_op jit(solution)/shard_map/all_to_all | solution.py:253
  42.2 9.6 %shard_map.79 = (f32[2,128,1024]{2,1,0:T(8,128)}, bf16[16,128,256]{2,1,0:T(8,128)(2,1)}, f32[2,8,1024]{2,1,0:T(8,128)}) custom-call(s32[1]{0:T(128)} %bitcast.here_ref, bf16[1024,512]{1,0:T(8,128)(2,1)} %q_ref.9, bf16[1024,512]{1,0:T(8,128)(2,1)} %do_ref.9, bf16[16,128,256]{2,1,0:T(8,128)(2,1)} %all-to-all-done.1.k_ref.v_ref, ...), custom_call_target="tpu_custom_call" | custom-call | flops 2684354560 | bytes 4194304 | tf_op jit(solution)/shard_map/pallas_call | solution.py:327
  51.8 5.0 %all-to-all-start.2 = ((bf16[16,128,256]{2,1,0:T(8,128)(2,1)}), bf16[16,128,256]{2,1,0:T(8,128)(2,1)}, u32[]{:S(2)}, u32[]{:S(2)}) async-start(bf16[16,128,256]{2,1,0:T(8,128)(2,1)} %get-tuple-element.61), calls=%async_computation.2 | async-start | bytes 2097152 | tf_op jit(solution)/shard_map/all_to_all | solution.py:253
  56.8 7.0 %shard_map.80 = (bf16[1024,256]{1,0:T(8,128)(2,1)}, bf16[1024,256]{1,0:T(8,128)(2,1)}, bf16[1024,256]{1,0:T(8,128)(2,1)}) custom-call(bf16[1024,512]{1,0:T(8,128)(2,1)} %q_ref.9, bf16[1024,512]{1,0:T(8,128)(2,1)} %do_ref.9, bf16[1024,512]{1,0:T(8,128)(2,1)} %k_ref.9, bf16[1024,512]{1,0:T(8,128)(2,1)} %v_ref.9, f32[16,1024]{1,0:T(8,128)} %slice.15.bias_ref, ...), custom_call_target="tpu_custom_call" | custom-call | flops 2684354560 | bytes 5242880 | tf_op jit(solution)/shard_map/pallas_call | solution.py:353
  63.8 10.4 %all-to-all-done.2.k_ref.v_ref.back_ref = bf16[16,128,256]{2,1,0:T(8,128)(2,1)} async-done(((bf16[16,128,256]{2,1,0:T(8,128)(2,1)}), bf16[16,128,256]{2,1,0:T(8,128)(2,1)}, u32[]{:S(2)}, u32[]{:S(2)}) %all-to-all-start.2) | async-done | bytes 1048608 | tf_op jit(solution)/shard_map/all_to_all | solution.py:253
  74.2 9.0 %shard_map.81 = (f32[2,128,1024]{2,1,0:T(8,128)}, bf16[16,128,256]{2,1,0:T(8,128)(2,1)}, f32[2,8,1024]{2,1,0:T(8,128)}) custom-call(s32[1]{0:T(128)} %bitcast.here_ref, bf16[1024,512]{1,0:T(8,128)(2,1)} %q_ref.9, bf16[1024,512]{1,0:T(8,128)(2,1)} %do_ref.9, bf16[16,128,256]{2,1,0:T(8,128)(2,1)} %all-to-all-done.2.k_ref.v_ref.back_ref, ...), custom_call_target="tpu_custom_call" | custom-call | flops 2684354560 | bytes 4194304 | tf_op jit(solution)/shard_map/pallas_call | solution.py:327
  83.2 5.0 %all-to-all-start.3 = ((bf16[16,128,256]{2,1,0:T(8,128)(2,1)}), bf16[16,128,256]{2,1,0:T(8,128)(2,1)}, u32[]{:S(2)}, u32[]{:S(2)}) async-start(bf16[16,128,256]{2,1,0:T(8,128)(2,1)} %get-tuple-element.90), calls=%async_computation.3 | async-start | bytes 2097152 | tf_op jit(solution)/shard_map/all_to_all | solution.py:253
  88.2 2.9 %shard_map.83 = (bf16[3,128,256]{2,1,0:T(8,128)(2,1)}, bf16[3,128,256]{2,1,0:T(8,128)(2,1)}, bf16[3,128,256]{2,1,0:T(8,128)(2,1)}, bf16[3,128,256]{2,1,0:T(8,128...) custom-call(s32[1]{0:T(128)} %bitcast.here_ref, ...), custom_call_target="tpu_custom_call" | custom-call | flops 1048576 | bytes 4194304 | tf_op jit(solution)/shard_map/pallas_call | solution.py:389
  92.4 1.8 %collective-permute-start.1 = (bf16[3,128,256]{2,1,0:T(8,128)(2,1)}, bf16[3,128,256]{2,1,0:T(8,128)(2,1)S(1)}, u32[]{:S(2)}, u32[]{:S(2)}) collective-permute-start(bf16[3,128,256]{2,1,0:T(8,128)(2,1)} %get-tuple-element.81), channel_id=1, source_target_pairs={{0,3},{1,2},{2,1},{3,0},{4,7},{5,6},{6,5},{7,4},{8,11},{9,10},{10,... | collective-permute-start | bytes 589832 | tf_op jit(solution)/shard_map/ppermute | solution.py:430
  95.3 1.5 %collective-permute-start.4 = (bf16[3,128,256]{2,1,0:T(8,128)(2,1)}, bf16[3,128,256]{2,1,0:T(8,128)(2,1)S(1)}, u32[]{:S(2)}, u32[]{:S(2)}) collective-permute-start(bf16[3,128,256]{2,1,0:T(8,128)(2,1)} %get-tuple-element.84), channel_id=1, source_target_pairs={{0,5},{1,4},{2,7},{3,6},{4,1},{5,0},{6,3},{7,2},{8,13},{9,12},{10,... | collective-permute-start | bytes 589832 | tf_op jit(solution)/shard_map/ppermute | solution.py:430
  97.7 2.7 %collective-permute-start.5 = (bf16[3,128,256]{2,1,0:T(8,128)(2,1)}, bf16[3,128,256]{2,1,0:T(8,128)(2,1)}, u32[]{:S(2)}, u32[]{:S(2)}) collective-permute-start(bf16[3,128,256]{2,1,0:T(8,128)(2,1)} %get-tuple-element.85), channel_id=1, source_target_pairs={{0,7},{1,6},{2,5},{3,4},{4,3},{5,2},{6,1},{7,0},{8,15},{9,14},{10,... | collective-permute-start | bytes 589832 | tf_op jit(solution)/shard_map/ppermute | solution.py:430
  100.4 1.6 %collective-permute-done.1.refs_3_ = bf16[3,128,256]{2,1,0:T(8,128)(2,1)S(1)} collective-permute-done((bf16[3,128,256]{2,1,0:T(8,128)(2,1)}, bf16[3,128,256]{2,1,0:T(8,128)(2,1)S(1)}, u32[]{:S(2)}, u32[]{:S(2)}) %collective-permute-start.1) | collective-permute-done | bytes 196640 | tf_op jit(solution)/shard_map/ppermute | solution.py:430
  101.9 6.9 %shard_map.82 = (bf16[1024,256]{1,0:T(8,128)(2,1)}, bf16[1024,256]{1,0:T(8,128)(2,1)}, bf16[1024,256]{1,0:T(8,128)(2,1)}) custom-call(bf16[1024,512]{1,0:T(8,128)(2,1)} %q_ref.9, bf16[1024,512]{1,0:T(8,128)(2,1)} %do_ref.9, bf16[1024,512]{1,0:T(8,128)(2,1)} %k_ref.9, bf16[1024,512]{1,0:T(8,128)(2,1)} %v_ref.9, f32[16,1024]{1,0:T(8,128)} %slice.15.bias_ref, ...), custom_call_target="tpu_custom_call" | custom-call | flops 2684354560 | bytes 5242880 | tf_op jit(solution)/shard_map/pallas_call | solution.py:353
  108.9 9.0 %collective-permute-done.3.refs_5_ = bf16[3,128,256]{2,1,0:T(8,128)(2,1)S(1)} collective-permute-done((bf16[3,128,256]{2,1,0:T(8,128)(2,1)}, bf16[3,128,256]{2,1,0:T(8,128)(2,1)S(1)}, u32[]{:S(2)}, u32[]{:S(2)}) %collective-permute-start.3) | collective-permute-done | bytes 196640 | tf_op jit(solution)/shard_map/ppermute | solution.py:430
  117.9 3.0 %shard_map.84 = bf16[8,3,128,256]{3,2,1,0:T(8,128)(2,1)} custom-call(s32[1]{0:T(128)} %bitcast.here_ref, s32[16,128]{1,0:T(8,128)} %bitcast.6, bf16[1024,256]{1,0:T(8,128)(2,1)} %get-tuple-element.87.dq_ref, bf16[1024,256]{1,0:T(8,128)(2,1)} %get-tuple-element.88.dk_ref, bf16[1024,256]{1,0:T(8,128)(2,1)} %get-tuple-element.89.dv_ref, ...), custom_call_target="tpu_custom_call" | custom-call | flops 1048576 | bytes 4194304 | tf_op jit(solution)/shard_map/pallas_call | solution.py:377
  120.9 4.9 %all-to-all-start.4 = ((bf16[8,3,128,256]{3,2,1,0:T(8,128)(2,1)}), bf16[8,3,128,256]{3,2,1,0:T(8,128)(2,1)S(1)}, u32[]{:S(2)}, u32[]{:S(2)}) async-start(bf16[8,3,128,256]{3,2,1,0:T(8,128)(2,1)} %shard_map.84), calls=%async_computation.4 | async-start | bytes 3145728 | tf_op jit(solution)/shard_map/all_to_all | solution.py:253
  125.8 2.4 %shard_map.85 = (bf16[128,4096]{1,0:T(8,128)(2,1)}, bf16[128,4096]{1,0:T(8,128)(2,1)}, bf16[128,4096]{1,0:T(8,128)(2,1)}) custom-call(s32[1]{0:T(128)} %bitcast.2.me_ref.refs_0_, bf16[3,128,256]{2,1,0:T(8,128)(2,1)S(1)} %copy-done, bf16[3,128,256]{2,1,0:T(8,128)(2,1)S(1)} %collective-permute-done.refs_2_, ...), custom_call_target="tpu_custom_call" | custom-call | tf_op jit(solution)/shard_map/pallas_call | solution.py:401
  128.1 19.1 %all-to-all-done.4.refs_0_ = bf16[8,3,128,256]{3,2,1,0:T(8,128)(2,1)S(1)} async-done(((bf16[8,3,128,256]{3,2,1,0:T(8,128)(2,1)}), bf16[8,3,128,256]{3,2,1,0:T(8,128)(2,1)S(1)}, u32[]{:S(2)}, u32[]{:S(2)}) %all-to-all-start.4) | async-done | bytes 1572896 | tf_op jit(solution)/shard_map/all_to_all | solution.py:253
  147.2 1.3 shard_map.86
  (29 shorter events, 7.0 us)
Async XLA Ops:
  20.2 22.0 %all-to-all-start.1 = ((bf16[16,128,256]{2,1,0:T(8,128)(2,1)}), bf16[16,128,256]{2,1,0:T(8,128)(2,1)}, u32[]{:S(2)}, u32[]{:S(2)}) async-start(bf16[16,128,256]{2,1,0:T(8,128)(2,1)} %shard_map.76), calls=%async_computation.1 | async-start | bytes 2097152 | tf_op jit(solution)/shard_map/all_to_all | solution.py:253
  24.8 2.1 %copy-start.1 = (s32[16,16]{1,0:T(8,128)S(1)}, s32[16,16]{1,0:T(8,128)}, u32[]{:S(2)}) copy-start(s32[16,16]{1,0:T(8,128)} %param.9) | copy-start | bytes 3076
  51.8 22.4 %all-to-all-start.2 = ((bf16[16,128,256]{2,1,0:T(8,128)(2,1)}), bf16[16,128,256]{2,1,0:T(8,128)(2,1)}, u32[]{:S(2)}, u32[]{:S(2)}) async-start(bf16[16,128,256]{2,1,0:T(8,128)(2,1)} %get-tuple-element.61), calls=%async_computation.2 | async-start | bytes 2097152 | tf_op jit(solution)/shard_map/all_to_all | solution.py:253
  83.2 34.7 %all-to-all-start.3 = ((bf16[16,128,256]{2,1,0:T(8,128)(2,1)}), bf16[16,128,256]{2,1,0:T(8,128)(2,1)}, u32[]{:S(2)}, u32[]{:S(2)}) async-start(bf16[16,128,256]{2,1,0:T(8,128)(2,1)} %get-tuple-element.90), calls=%async_computation.3 | async-start | bytes 2097152 | tf_op jit(solution)/shard_map/all_to_all | solution.py:253
  91.1 6.6 %collective-permute-start = (bf16[3,128,256]{2,1,0:T(8,128)(2,1)}, bf16[3,128,256]{2,1,0:T(8,128)(2,1)S(1)}, u32[]{:S(2)}, u32[]{:S(2)}) collective-permute-start(bf16[3,128,256]{2,1,0:T(8,128)(2,1)} %get-tuple-element.80), channel_id=1, source_target_pairs={{0,1},{1,0},{2,3},{3,2},{4,5},{5,4},{6,7},{7,6},{8,9},{9,8},{10,11... | collective-permute-start | bytes 589832 | tf_op jit(solution)/shard_map/ppermute | solution.py:430
  92.4 9.5 %collective-permute-start.1 = (bf16[3,128,256]{2,1,0:T(8,128)(2,1)}, bf16[3,128,256]{2,1,0:T(8,128)(2,1)S(1)}, u32[]{:S(2)}, u32[]{:S(2)}) collective-permute-start(bf16[3,128,256]{2,1,0:T(8,128)(2,1)} %get-tuple-element.81), channel_id=1, source_target_pairs={{0,3},{1,2},{2,1},{3,0},{4,7},{5,6},{6,5},{7,4},{8,11},{9,10},{10,... | collective-permute-start | bytes 589832 | tf_op jit(solution)/shard_map/ppermute | solution.py:430
  94.2 14.6 %collective-permute-start.2 = (bf16[3,128,256]{2,1,0:T(8,128)(2,1)}, bf16[3,128,256]{2,1,0:T(8,128)(2,1)S(1)}, u32[]{:S(2)}, u32[]{:S(2)}) collective-permute-start(bf16[3,128,256]{2,1,0:T(8,128)(2,1)} %get-tuple-element.82), channel_id=1, source_target_pairs={{0,2},{1,3},{2,0},{3,1},{4,6},{5,7},{6,4},{7,5},{8,10},{9,11},{10,... | collective-permute-start | bytes 589832 | tf_op jit(solution)/shard_map/ppermute | solution.py:430
  94.8 23.0 %collective-permute-start.3 = (bf16[3,128,256]{2,1,0:T(8,128)(2,1)}, bf16[3,128,256]{2,1,0:T(8,128)(2,1)S(1)}, u32[]{:S(2)}, u32[]{:S(2)}) collective-permute-start(bf16[3,128,256]{2,1,0:T(8,128)(2,1)} %get-tuple-element.83), channel_id=1, source_target_pairs={{0,4},{1,5},{2,6},{3,7},{4,0},{5,1},{6,2},{7,3},{8,12},{9,13},{10,... | collective-permute-start | bytes 589832 | tf_op jit(solution)/shard_map/ppermute | solution.py:430
  95.3 22.6 %collective-permute-start.4 = (bf16[3,128,256]{2,1,0:T(8,128)(2,1)}, bf16[3,128,256]{2,1,0:T(8,128)(2,1)S(1)}, u32[]{:S(2)}, u32[]{:S(2)}) collective-permute-start(bf16[3,128,256]{2,1,0:T(8,128)(2,1)} %get-tuple-element.84), channel_id=1, source_target_pairs={{0,5},{1,4},{2,7},{3,6},{4,1},{5,0},{6,3},{7,2},{8,13},{9,12},{10,... | collective-permute-start | bytes 589832 | tf_op jit(solution)/shard_map/ppermute | solution.py:430
  97.7 20.2 %collective-permute-start.5 = (bf16[3,128,256]{2,1,0:T(8,128)(2,1)}, bf16[3,128,256]{2,1,0:T(8,128)(2,1)}, u32[]{:S(2)}, u32[]{:S(2)}) collective-permute-start(bf16[3,128,256]{2,1,0:T(8,128)(2,1)} %get-tuple-element.85), channel_id=1, source_target_pairs={{0,7},{1,6},{2,5},{3,4},{4,3},{5,2},{6,1},{7,0},{8,15},{9,14},{10,... | collective-permute-start | bytes 589832 | tf_op jit(solution)/shard_map/ppermute | solution.py:430
  101.9 16.0 %collective-permute-start.6 = (bf16[3,128,256]{2,1,0:T(8,128)(2,1)}, bf16[3,128,256]{2,1,0:T(8,128)(2,1)}, u32[]{:S(2)}, u32[]{:S(2)}) collective-permute-start(bf16[3,128,256]{2,1,0:T(8,128)(2,1)} %get-tuple-element.86), channel_id=1, source_target_pairs={{0,6},{1,7},{2,4},{3,5},{4,2},{5,3},{6,0},{7,1},{8,14},{9,15},{10,... | collective-permute-start | bytes 589832 | tf_op jit(solution)/shard_map/ppermute | solution.py:430
  120.9 4.9 %copy-start = (bf16[3,128,256]{2,1,0:T(8,128)(2,1)S(1)}, bf16[3,128,256]{2,1,0:T(8,128)(2,1)}, u32[]{:S(2)}) copy-start(bf16[3,128,256]{2,1,0:T(8,128)(2,1)} %get-tuple-element.91.refs_1_) | copy-start | bytes 589828
  120.9 26.3 %all-to-all-start.4 = ((bf16[8,3,128,256]{3,2,1,0:T(8,128)(2,1)}), bf16[8,3,128,256]{3,2,1,0:T(8,128)(2,1)S(1)}, u32[]{:S(2)}, u32[]{:S(2)}) async-start(bf16[8,3,128,256]{3,2,1,0:T(8,128)(2,1)} %shard_map.84), calls=%async_computation.4 | async-start | bytes 3145728 | tf_op jit(solution)/shard_map/all_to_all | solution.py:253
